TPU v7x, 32 devices: a whole 2x2x4 slice. The times are simulated.
32 devices in a mesh: cols: 8 (over z, x), rows: 4 (over y, core).
Axes of the slice: x: 2, y: 2, z: 4, core: 2. Of those that a mesh axis runs over, the one named last changes fastest.
Arguments:
- slide_pixels: bfloat16 [3, 1024, 4096], P(None, 'rows', 'cols'), may hold values from -6 to 6
- stem_first: bfloat16 [6, 6, 3, 64], replicated, may hold values from -0.625 to 0.625
- stem_second: bfloat16 [6, 6, 64, 256], replicated, may hold values from -0.125 to 0.125
- stem_third: bfloat16 [3, 3, 256, 1024], replicated, may hold values from -0.125 to 0.125
- key_weight: bfloat16 [1024, 1024], replicated, may hold values from -0.1875 to 0.1875
- value_weight: bfloat16 [1024, 1024], replicated, may hold values from -0.1875 to 0.1875
- queries: bfloat16 [512, 1024], replicated, may hold values from -240 to 240
Outputs:
- attended: bfloat16 [512, 1024], P(('cols', 'rows'))
All inputs are finite; a program needn't handle non-finite values.
Results may differ from a plain program's by a relative error of at most 0.033.
Values may be sent and summed in bfloat16 or wider, within the bound.
No kernel may reach another device: no remote copies, remote signals or barrier semaphores. Data moves between devices by JAX's collectives and lax.ppermute only.
A program may use at most 128 MiB of HBM per device.

v0:
```python
import math

import jax
import jax.numpy as jnp
from jax import lax
from jax.sharding import PartitionSpec as P

HEADS = 8


def with_halo(shard, sides, width):
    for axis, dim in sides:
        size, length = (lax.axis_size(axis), shard.shape[dim])
        up = [(i, (i + 1) % size) for i in range(size - 1)]
        down = [(j, i) for i, j in up]
        last = lax.slice_in_dim(shard, length - width, length, axis=dim)
        leading = lax.slice_in_dim(shard, 0, width, axis=dim)
        before = lax.ppermute(last, axis, up)
        after = lax.ppermute(leading, axis, down)
        shard = jnp.concatenate([before, shard, after], axis=dim)
    return shard


def shifted(value, axis, steps):
    count = lax.axis_size(axis)
    leading, last = (max(0, -steps), min(count, count - steps))
    return lax.ppermute(value, axis, [(source, source + steps) for source in range(leading, last)])


def extend(features):
    return with_halo(features, (("cols", 2), ("rows", 1)), 1)


def convolve(features, kernel, stride, layout):
    return lax.conv_general_dilated(
        features[None],
        kernel,
        (stride, stride),
        "VALID",
        dimension_numbers=layout,
        preferred_element_type=jnp.float32,
    )[0]


def norm_rows(features):
    tok_mean = jnp.mean(features, axis=-1, keepdims=True)
    centred = features - tok_mean
    tok_var = jnp.mean(centred * centred, axis=-1, keepdims=True)
    return (centred * lax.rsqrt(tok_var + 1e-05)).astype(jnp.bfloat16)


def on_device(slide_pixels, stem_first, stem_second, stem_third, key_weight, value_weight, queries):
    first_map = jax.nn.gelu(
        convolve(extend(slide_pixels), stem_first, 4, ("NCHW", "HWIO", "NCHW"))
    ).astype(jnp.bfloat16)
    second_map = jax.nn.gelu(
        convolve(extend(first_map), stem_second, 4, ("NCHW", "HWIO", "NHWC"))
    ).astype(jnp.bfloat16)
    upper_rim = shifted(second_map[-1:], "rows", 1)
    second_map = jnp.concatenate([upper_rim, second_map], axis=0)
    left_rim = shifted(second_map[:, -1:], "cols", 1)
    second_map = jnp.concatenate([left_rim, second_map], axis=1)
    third_map = convolve(second_map, stem_third, 2, ("NHWC", "HWIO", "NHWC"))
    model_width = third_map.shape[-1]
    normed = norm_rows(third_map.reshape(-1, model_width))
    tok_count = normed.shape[0]
    key_rows = jnp.dot(normed, key_weight, preferred_element_type=jnp.float32).astype(jnp.bfloat16)
    value_rows = jnp.dot(normed, value_weight, preferred_element_type=jnp.float32).astype(
        jnp.bfloat16
    )
    head_size = model_width // HEADS
    latent_count = queries.shape[0]
    query_heads = queries.reshape(latent_count, HEADS, head_size)
    scores = jnp.einsum(
        "lhd,thd->hlt",
        query_heads,
        key_rows.reshape(tok_count, HEADS, head_size),
        preferred_element_type=jnp.float32,
    ) * (1.0 / math.sqrt(head_size))
    peak_score = lax.pmax(jnp.max(scores, axis=2), ("cols", "rows"))
    weights = jnp.exp(scores - peak_score[:, :, None])
    row_total = jnp.sum(weights, axis=2).T
    rounded = weights.astype(jnp.bfloat16)
    weighted = jnp.einsum(
        "hlt,thd->lhd",
        rounded,
        value_rows.reshape(tok_count, HEADS, head_size),
        preferred_element_type=jnp.float32,
    ).reshape(latent_count, model_width)
    share_rows = latent_count // lax.axis_size(("cols", "rows"))
    weighted, row_total = lax.psum((weighted, row_total), ("cols", "rows"))
    share_start = lax.axis_index(("cols", "rows")) * share_rows
    weighted = lax.dynamic_slice_in_dim(weighted, share_start, share_rows, 0)
    row_total = lax.dynamic_slice_in_dim(row_total, share_start, share_rows, 0)
    attended = weighted.reshape(share_rows, HEADS, head_size) / row_total[:, :, None]
    return attended.reshape(share_rows, model_width).astype(jnp.bfloat16)


def solution(mesh):
    placed = (P(None, "rows", "cols"), P(), P(), P(), P(), P(), P())
    return jax.shard_map(
        on_device, mesh=mesh, in_specs=placed, out_specs=P(("cols", "rows"), None), check_vma=False
    )
```

profile of v0, /device:TPU:0, one launch (start us, length us, event | category | flops | bytes accessed | tf_op | source)
XLA Modules:
  0.0 329.5 jit_solution(13825358691176323215)
XLA Ops:
  7.8 4.9 %collective-permute-start = (bf16[3,256,1]{2,1,0:T(8,128)(2,1)S(1)}, bf16[3,256,1]{2,1,0:T(8,128)(2,1)S(1)}, u32[]{:S(2)}, u32[]{:S(2)}) collective-permute-start(bf16[3,256,1]{2,1,0:T(8,128)(2,1)S(1)} %get-tuple-element.13), channel_id=1, source_target_pairs={{0,4},{4,8},{8,12},{12,16},{16,20},{20,24},{24,28},{1,5},{5,9},{9,... | collective-permute-start | bytes 4616 | tf_op jit(solution)/shard_map/ppermute | solution.py:18
  14.0 2.9 collective-permute-done
  16.9 4.0 %collective-permute-done.1 = bf16[3,256,1]{2,1,0:T(8,128)(2,1)S(1)} collective-permute-done((bf16[3,256,1]{2,1,0:T(8,128)(2,1)S(1)}, bf16[3,256,1]{2,1,0:T(8,128)(2,1)S(1)}, u32[]{:S(2)}, u32[]{:S(2)}) %collective-permute-start.1) | collective-permute-done | bytes 1568 | tf_op jit(solution)/shard_map/ppermute | solution.py:19
  24.4 3.5 %collective-permute-done.3 = bf16[3,1,514]{2,1,0:T(2,128)(2,1)S(1)} collective-permute-done((bf16[3,1,514]{2,1,0:T(2,128)(2,1)S(1)}, bf16[3,1,514]{2,1,0:T(2,128)(2,1)S(1)}, u32[]{:S(2)}, u32[]{:S(2)}) %collective-permute-start.3) | collective-permute-done | bytes 3116 | tf_op jit(solution)/shard_map/ppermute | solution.py:19
  28.9 2.8 reshape.95
  31.7 19.5 %copy.95 = bf16[3,258,1,8,68]{3,0,4,1,2:T(4,128)(2,1)} copy(bf16[3,258,1,8,68]{4,3,1,0,2:T(8,128)(2,1)} %reshape.95) | data formatting | bytes 1684224 | tf_op jit(solution)/shard_map/conv_general_dilated | solution.py:35
  51.1 2.1 slice.46
  53.3 23.5 %broadcast_select_fusion = f32[64,8,17,64]{3,1,2,0:T(8,128)S(1)} fusion(pred[8,17]{0,1:T(8,128)(4,1)S(1)} %copy-done.5, bf16[6,6,3,64]{3,2,1,0:T(4,128)(2,1)S(1)} %copy-done.4, bf16[3,258,1,7,5]{3,0,4,1,2:T(4,128)(2,1)S(1)} %slice.46, bf16[3,258,1,8,68]{3,0,4,1,2:T(4,128)(2,1)} %copy.95), kind=kOutput, calls=%fused_computation.25 | convolution fusion | flops 123593248 | bytes 3138476 | tf_op jit(solution)/shard_map/conv_general_dilated | solution.py:35
  77.6 1.4 fusion.14
  79.0 4.5 %collective-permute-start.4 = (bf16[64,64,1]{0,1,2:T(8,128)(2,1)S(1)}, bf16[64,64,1]{0,1,2:T(8,128)(2,1)S(1)}, u32[]{:S(2)}, u32[]{:S(2)}) collective-permute-start(bf16[64,64,1]{0,1,2:T(8,128)(2,1)S(1)} %get-tuple-element.7), channel_id=1, source_target_pairs={{0,4},{4,8},{8,12},{12,16},{16,20},{20,24},{24,28},{1,5},{5,9},{9,... | collective-permute-start | bytes 24584 | tf_op jit(solution)/shard_map/ppermute | solution.py:18
  84.9 4.6 %collective-permute-done.5 = bf16[64,64,1]{0,1,2:T(8,128)(2,1)S(1)} collective-permute-done((bf16[64,64,1]{0,1,2:T(8,128)(2,1)S(1)}, bf16[64,64,1]{0,1,2:T(8,128)(2,1)S(1)}, u32[]{:S(2)}, u32[]{:S(2)}) %collective-permute-start.5) | collective-permute-done | bytes 8224 | tf_op jit(solution)/shard_map/ppermute | solution.py:19
  89.7 3.2 collective-permute-start.6
  92.9 1.5 collective-permute-start.7
  94.4 2.3 collective-permute-done.7
  96.7 4.0 %maximum_bitcast_fusion = bf16[64,66,1,130]{0,1,3,2:T(8,128)(2,1)} fusion(bf16[64,1,130]{0,1,2:T(2,128)(2,1)S(1)} %collective-permute-done.7, bf16[64,64,1]{0,1,2:T(8,128)(2,1)S(1)} %collective-permute-done.5, bf16[64,64,128]{0,1,2:T(8,128)(2,1)S(1)} %fusion.14, bf16[64,64,1]{0,1,2:T(8,128)(2,1)S(1)} %collective-permute-done.4, ...), kind=kLoop, calls=%fused_computation.24 | loop fusion | flops 5491200 | bytes 2196480 | tf_op jit(solution)/shard_map/broadcast_in_dim | solution.py:36
  100.7 4.4 %copy.122 = bf16[64,66,1,130]{1,0,3,2:T(8,128)(2,1)} copy(bf16[64,66,1,130]{0,1,3,2:T(8,128)(2,1)} %maximum_bitcast_fusion) | data formatting | bytes 2196480
  105.0 3.9 %pad.2.clone = bf16[64,66,1,160]{1,0,3,2:T(8,128)(2,1)} pad(bf16[64,66,1,130]{1,0,3,2:T(8,128)(2,1)} %copy.122, bf16[]{:T(256)} %constant.41), padding=0_0x0_0x0_0x0_30 | pad | bytes 2449922 | tf_op jit(solution)/shard_map/broadcast_in_dim | solution.py:36
  108.9 4.9 %copy.99 = bf16[64,66,1,8,20]{0,3,4,1,2:T(8,128)(2,1)} copy(bf16[64,66,1,8,20]{1,0,4,3,2:T(8,128)(2,1)} %bitcast.93) | data formatting | bytes 2703360 | tf_op jit(solution)/shard_map/conv_general_dilated | solution.py:35
  113.8 1.4 slice.50
  115.3 3.0 fusion.28
  118.7 4.8 %collective-permute-start.8 = (bf16[1,32,256]{2,0,1:T(2,128)(2,1)S(1)}, bf16[1,32,256]{2,0,1:T(2,128)(2,1)S(1)}, u32[]{:S(2)}, u32[]{:S(2)}) collective-permute-start(bf16[1,32,256]{2,0,1:T(2,128)(2,1)S(1)} %slice.52), channel_id=1, source_target_pairs={{0,1},{1,2},{2,3},{4,5},{5,6},{6,7},{8,9},{9,10},{10,11},{12,13},{... | collective-permute-start | bytes 49160 | tf_op jit(solution)/shard_map/ppermute | solution.py:27
  124.4 4.8 %collective-permute-start.9 = (bf16[17,1,256]{2,0,1:T(8,128)(2,1)S(1)}, bf16[17,1,256]{2,0,1:T(8,128)(2,1)S(1)}, u32[]{:S(2)}, u32[]{:S(2)}) collective-permute-start(bf16[17,1,256]{2,0,1:T(8,128)(2,1)S(1)} %pad_maximum_fusion.3), channel_id=1, source_target_pairs={{0,4},{4,8},{8,12},{12,16},{16,20},{20,24},{24,28},{1,5},{5,9},{9,... | collective-permute-start | bytes 26120 | tf_op jit(solution)/shard_map/ppermute | solution.py:27
  129.2 1.4 collective-permute-done.9
  134.6 1.8 bitcast_reduce_fusion
  136.4 42.2 %pmax.7 = f32[8,512]{1,0:T(8,128)S(1)} all-reduce(f32[8,512]{1,0:T(8,128)S(1)} %get-tuple-element.15), channel_id=1, replica_groups=mesh['cols'=8,'rows'=4] {'cols','rows'}, use_global_device_ids=true, to_apply=%region_3.0 | all-reduce | flops 4096 | bytes 32768 | tf_op jit(solution)/shard_map/pmax | solution.py:80
  178.6 2.0 convolution_convert_fusion.1
  180.8 3.4 %fusion.33 = f32[8,128,512]{2,1,0:T(8,128)} fusion(bf16[128,8,128]{0,2,1:T(8,128)(2,1)S(1)} %bitcast.99, f32[8,128,512]{2,1,0:T(8,128)} %get-tuple-element.16, f32[8,512]{1,0:T(8,128)S(1)} %pmax.7), kind=kOutput, calls=%fused_computation.39 | convolution fusion | flops 135790592 | bytes 4472832 | tf_op jit(solution)/shard_map/hlt,thd->lhd/dot_general | solution.py:84
  184.2 2.9 copy.113
  187.2 2.0 fusion.25
  189.1 40.1 %psum.15 = f32[512,8]{0,1:T(8,128)S(1)} all-reduce(f32[512,8]{0,1:T(8,128)S(1)} %bitcast.101), channel_id=1, replica_groups=mesh['cols'=8,'rows'=4] {'cols','rows'}, use_global_device_ids=true, to_apply=%region_6.0 | all-reduce | flops 4096 | bytes 32768 | tf_op jit(solution)/shard_map/psum | solution.py:91
  229.4 91.8 %all-reduce.2.cloned.1.call-done = f32[512,1024]{1,0:T(8,128)} async-done(((f32[512,1024]{1,0:T(8,128)}), f32[512,1024]{1,0:T(8,128)}) %all-reduce.2.cloned.1.call-update) | async-done | bytes 2097168 | tf_op jit(solution)/shard_map/psum | solution.py:91
  321.2 1.5 fusion.61
  (64 shorter events, 15.0 us)
Async XLA Ops:
  6.5 127.3 %copy-start = (bf16[1024,1024]{1,0:T(8,128)(2,1)S(1)}, bf16[1024,1024]{1,0:T(8,128)(2,1)}, u32[]{:S(2)}) copy-start(bf16[1024,1024]{1,0:T(8,128)(2,1)} %param.11) | copy-start | bytes 6291460
  6.5 21.4 %copy-start.1 = (bf16[3,256,512]{2,1,0:T(8,128)(2,1)S(1)}, bf16[3,256,512]{2,1,0:T(8,128)(2,1)}, u32[]{:S(2)}) copy-start(bf16[3,256,512]{2,1,0:T(8,128)(2,1)} %param.7) | copy-start | bytes 2359300
  6.5 314.6 %all-reduce.2.cloned.1.call-start = ((), (), s32[]{:S(2)}) async-start(), calls=%async_computation | async-start | bytes 4194304 | tf_op jit(solution)/shard_map/psum | solution.py:91
  7.8 9.1 %collective-permute-start = (bf16[3,256,1]{2,1,0:T(8,128)(2,1)S(1)}, bf16[3,256,1]{2,1,0:T(8,128)(2,1)S(1)}, u32[]{:S(2)}, u32[]{:S(2)}) collective-permute-start(bf16[3,256,1]{2,1,0:T(8,128)(2,1)S(1)} %get-tuple-element.13), channel_id=1, source_target_pairs={{0,4},{4,8},{8,12},{12,16},{16,20},{20,24},{24,28},{1,5},{5,9},{9,... | collective-permute-start | bytes 4616 | tf_op jit(solution)/shard_map/ppermute | solution.py:18
  12.7 8.3 %collective-permute-start.1 = (bf16[3,256,1]{2,1,0:T(8,128)(2,1)S(1)}, bf16[3,256,1]{2,1,0:T(8,128)(2,1)S(1)}, u32[]{:S(2)}, u32[]{:S(2)}) collective-permute-start(bf16[3,256,1]{2,1,0:T(8,128)(2,1)S(1)} %get-tuple-element.14), channel_id=1, source_target_pairs={{4,0},{8,4},{12,8},{16,12},{20,16},{24,20},{28,24},{5,1},{9,5},{13... | collective-permute-start | bytes 4616 | tf_op jit(solution)/shard_map/ppermute | solution.py:19
  21.8 2.6 collective-permute-start.2
  23.1 4.8 %collective-permute-start.3 = (bf16[3,1,514]{2,1,0:T(2,128)(2,1)S(1)}, bf16[3,1,514]{2,1,0:T(2,128)(2,1)S(1)}, u32[]{:S(2)}, u32[]{:S(2)}) collective-permute-start(bf16[3,1,514]{2,1,0:T(2,128)(2,1)S(1)} %get-tuple-element.10), channel_id=1, source_target_pairs={{1,0},{2,1},{3,2},{5,4},{6,5},{7,6},{9,8},{10,9},{11,10},{13,12},{... | collective-permute-start | bytes 9260 | tf_op jit(solution)/shard_map/ppermute | solution.py:19
  51.1 2.1 copy-start.4
  51.1 2.1 copy-start.5
  79.0 5.9 %collective-permute-start.4 = (bf16[64,64,1]{0,1,2:T(8,128)(2,1)S(1)}, bf16[64,64,1]{0,1,2:T(8,128)(2,1)S(1)}, u32[]{:S(2)}, u32[]{:S(2)}) collective-permute-start(bf16[64,64,1]{0,1,2:T(8,128)(2,1)S(1)} %get-tuple-element.7), channel_id=1, source_target_pairs={{0,4},{4,8},{8,12},{12,16},{16,20},{20,24},{24,28},{1,5},{5,9},{9,... | collective-permute-start | bytes 24584 | tf_op jit(solution)/shard_map/ppermute | solution.py:18
  83.5 6.1 %collective-permute-start.5 = (bf16[64,64,1]{0,1,2:T(8,128)(2,1)S(1)}, bf16[64,64,1]{0,1,2:T(8,128)(2,1)S(1)}, u32[]{:S(2)}, u32[]{:S(2)}) collective-permute-start(bf16[64,64,1]{0,1,2:T(8,128)(2,1)S(1)} %get-tuple-element.8), channel_id=1, source_target_pairs={{4,0},{8,4},{12,8},{16,12},{20,16},{24,20},{28,24},{5,1},{9,5},{13... | collective-permute-start | bytes 24584 | tf_op jit(solution)/shard_map/ppermute | solution.py:19
  89.7 4.6 %collective-permute-start.6 = (bf16[64,1,130]{0,1,2:T(2,128)(2,1)S(1)}, bf16[64,1,130]{0,1,2:T(2,128)(2,1)S(1)}, u32[]{:S(2)}, u32[]{:S(2)}) collective-permute-start(bf16[64,1,130]{0,1,2:T(2,128)(2,1)S(1)} %get-tuple-element.5), channel_id=1, source_target_pairs={{0,1},{1,2},{2,3},{4,5},{5,6},{6,7},{8,9},{9,10},{10,11},{12,13},{... | collective-permute-start | bytes 49928 | tf_op jit(solution)/shard_map/ppermute | solution.py:18
  92.9 3.8 %collective-permute-start.7 = (bf16[64,1,130]{0,1,2:T(2,128)(2,1)S(1)}, bf16[64,1,130]{0,1,2:T(2,128)(2,1)S(1)}, u32[]{:S(2)}, u32[]{:S(2)}) collective-permute-start(bf16[64,1,130]{0,1,2:T(2,128)(2,1)S(1)} %get-tuple-element.6), channel_id=1, source_target_pairs={{1,0},{2,1},{3,2},{5,4},{6,5},{7,6},{9,8},{10,9},{11,10},{13,12},{... | collective-permute-start | bytes 49928 | tf_op jit(solution)/shard_map/ppermute | solution.py:19
  108.9 6.3 %copy-start.3 = (bf16[6,6,64,256]{3,2,1,0:T(8,128)(2,1)S(1)}, bf16[6,6,64,256]{3,2,1,0:T(8,128)(2,1)}, u32[]{:S(2)}) copy-start(bf16[6,6,64,256]{3,2,1,0:T(8,128)(2,1)} %param.9) | copy-start | bytes 3538948
  108.9 6.3 %copy-start.6 = (pred[8,5]{0,1:T(8,128)(4,1)S(1)}, pred[8,5]{0,1:T(8,128)(4,1)}, u32[]{:S(2)}) copy-start(pred[8,5]{0,1:T(8,128)(4,1)} %constant.54) | copy-start | bytes 124
  113.8 17.2 %slice-start = ((s8[4718592]{0:T(1024)(128)(4,1)}), s8[4194304]{0:T(1024)(128)(4,1)S(1)}, s32[]{:S(2)}) async-start(s8[4718592]{0:T(1024)(128)(4,1)} %bitcast.102), calls=%async_computation.1 | async-start | bytes 8388608
  115.3 15.8 %slice-start.1 = ((s8[4718592]{0:T(1024)(128)(4,1)}), s8[524288]{0:T(1024)(128)(4,1)S(1)}, s32[]{:S(2)}) async-start(s8[4718592]{0:T(1024)(128)(4,1)} %bitcast.102), calls=%async_computation.2 | async-start | bytes 1048576
  118.5 12.6 %copy-start.7 = (pred[8,3]{0,1:T(4,128)(4,1)S(1)}, pred[8,3]{0,1:T(4,128)(4,1)}, u32[]{:S(2)}) copy-start(pred[8,3]{0,1:T(4,128)(4,1)} %constant.53) | copy-start | bytes 76
  118.7 5.7 %collective-permute-start.8 = (bf16[1,32,256]{2,0,1:T(2,128)(2,1)S(1)}, bf16[1,32,256]{2,0,1:T(2,128)(2,1)S(1)}, u32[]{:S(2)}, u32[]{:S(2)}) collective-permute-start(bf16[1,32,256]{2,0,1:T(2,128)(2,1)S(1)} %slice.52), channel_id=1, source_target_pairs={{0,1},{1,2},{2,3},{4,5},{5,6},{6,7},{8,9},{9,10},{10,11},{12,13},{... | collective-permute-start | bytes 49160 | tf_op jit(solution)/shard_map/ppermute | solution.py:27
  124.4 6.2 %collective-permute-start.9 = (bf16[17,1,256]{2,0,1:T(8,128)(2,1)S(1)}, bf16[17,1,256]{2,0,1:T(8,128)(2,1)S(1)}, u32[]{:S(2)}, u32[]{:S(2)}) collective-permute-start(bf16[17,1,256]{2,0,1:T(8,128)(2,1)S(1)} %pad_maximum_fusion.3), channel_id=1, source_target_pairs={{0,4},{4,8},{8,12},{12,16},{16,20},{20,24},{24,28},{1,5},{5,9},{9,... | collective-permute-start | bytes 26120 | tf_op jit(solution)/shard_map/ppermute | solution.py:27
  133.4 1.2 copy-start.2
Sparse Core Ops, SparseCore 0:
  187.3 133.8 all-reduce.1
where the time goes:
time: 332 us; the launch traced here: 330 us
  waiting for transfers between devices  112 us (34%)
  blocking collectives  82.2 us (25%)
  local copies, waits for them, and re-layouts  46.4 us (14%)
  matrix products  35.3 us (11%)
  starting transfers between devices  28.8 us (9%)
  between operations  13.8 us (4%)
  other arithmetic  11.4 us (3%)
    psum x1, waiting for transfers between devices, on_device(): weighted, row_total = lax.psum((weighted, row_total), ('cols', 'rows'))  91.8 us
    pmax x1, blocking collectives, on_device(): peak_score = lax.pmax(jnp.max(scores, axis=2), ('cols', 'rows'))  42.2 us
    psum x1, blocking collectives, on_device(): weighted, row_total = lax.psum((weighted, row_total), ('cols', 'rows'))  40.1 us
    conv_general_dilated x11, local copies, waits for them, and re-layouts, convolve(): lax.conv_general_dilated(features[None], kernel, (stride, stride), 'VALID...  32.7 us
    conv_general_dilated x3, matrix products, convolve(): lax.conv_general_dilated(features[None], kernel, (stride, stride), 'VALID...  27.6 us
    ppermute x4, waiting for transfers between devices, with_halo(): after = lax.ppermute(leading, axis, down)  14.5 us
    ppermute x4, starting transfers between devices, with_halo(): before = lax.ppermute(last, axis, up)  13.8 us
    ppermute x2, starting transfers between devices, shifted(): lax.ppermute(value, axis, [(source, source + steps) for source in range(l...  9.66 us
  transfers between devices with their start and end apart: 11, of which 9 were waited for; matrix products, arithmetic and copies ran while one was open for 1% of the time, Pallas kernels for 0%

commit v1 on v0

v1 whole, which is shorter than its diff:
```python
import functools
import math

import jax
import jax.numpy as jnp
from jax import lax
from jax.experimental import pallas as pl
from jax.experimental.pallas import tpu as pltpu
from jax.sharding import PartitionSpec as P

HEADS = 8
BEFORE, AFTER = 21, 5
TAPS1 = 18
BLOCK_COLS = 28
BLOCKS = 5
BLOCK_LANES = BLOCK_COLS * 64
ROWS1 = 80
ROWS2 = 24
COLS2 = 34
STAT = 128
VMEM = pltpu.MemorySpace.VMEM


def gelu(x):
    inner = x * (0.7978845608028654 + 0.035677408136300125 * (x * x))
    half = 0.5 * x
    return half + half * jnp.tanh(inner)


def lanes_of(shape):
    return lax.broadcasted_iota(jnp.int32, shape, len(shape) - 1)


def col_edges_kernel(lo_ref, hi_ref, a_ref, b_ref):
    even = lax.axis_index("cols") % 2 == 0
    lane = lanes_of((128, 128))
    first = jnp.zeros((128, 128), jnp.float32)
    last = jnp.zeros((128, 128), jnp.float32)
    for c in range(3):
        for half in range(2):
            g = BEFORE * (2 * c + half)
            rows = slice(half * 128, half * 128 + 128)
            lo = lo_ref[c, rows, :].astype(jnp.float32)
            hi = hi_ref[c, rows, :].astype(jnp.float32)
            lo = pltpu.roll(lo, g, 1) if g else lo
            hi = pltpu.roll(hi, (g + BEFORE) % 128, 1)
            first = jnp.where((lane >= g) & (lane < g + AFTER), lo, first)
            last = jnp.where((lane >= g) & (lane < g + BEFORE), hi, last)
    a_ref[...] = jnp.where(even, last, first).astype(jnp.bfloat16)
    b_ref[...] = jnp.where(even, first, last).astype(jnp.bfloat16)


def row_edges_kernel(top_ref, bottom_ref, ca_ref, cb_ref, a_ref, b_ref):
    even_col = lax.axis_index("cols") % 2 == 0
    even = lax.axis_index("rows") % 2 == 0
    ca = ca_ref[...].astype(jnp.float32)
    cb = cb_ref[...].astype(jnp.float32)
    left = jnp.where(even_col, cb, ca)
    right = jnp.where(even_col, ca, cb)
    lane = lanes_of((24, 128))
    for c in range(3):
        pieces = []
        for half, rows, main in ((0, slice(0, 24), top_ref[c, 0:24, :]), (1, slice(104, 128), bottom_ref[c, 8:32, :])):
            g = BEFORE * (2 * c + half)
            lt = pltpu.roll(left[rows], (128 - g) % 128, 1) if g else left[rows]
            rt = pltpu.roll(right[rows], (128 - g + BEFORE) % 128, 1)
            side = jnp.where(lane < BEFORE, lt, jnp.where(lane < BEFORE + AFTER, rt, 0.0))
            pieces.append((main.astype(jnp.float32), side))
        (top_main, top_side), (bottom_main, bottom_side) = pieces
        a_ref[c, :, 0:512] = jnp.where(even, bottom_main, top_main).astype(jnp.bfloat16)
        b_ref[c, :, 0:512] = jnp.where(even, top_main, bottom_main).astype(jnp.bfloat16)
        a_ref[c, :, 512:640] = jnp.where(even, bottom_side, top_side).astype(jnp.bfloat16)
        b_ref[c, :, 512:640] = jnp.where(even, top_side, bottom_side).astype(jnp.bfloat16)


def windows(xb_ref, c, row0, main, left, right):
    n = main.shape[0]
    lane = lanes_of((n, 128))
    moved = pltpu.roll(main, BEFORE, 1)
    tiles = [moved[:, 128 * k : 128 * k + 128] for k in range(4)]
    tail = jnp.where(lane < BEFORE, tiles[0], jnp.where(lane < BEFORE + AFTER, right, 0.0))
    tiles = [jnp.where(lane < BEFORE, left, tiles[0])] + tiles[1:] + [tail]
    xb_ref[0, c, pl.ds(row0, n), :] = tiles[0]
    for b in range(1, BLOCKS):
        t, s = divmod(4 * BLOCK_COLS * b, 128)
        early = pltpu.roll(tiles[t], 128 - s, 1)
        late = pltpu.roll(tiles[t + 1], 128 - s, 1)
        xb_ref[b, c, pl.ds(row0, n), :] = jnp.where(lane < 128 - s, early, late)


def main_kernel(
    ca_ref, cb_ref, ra_ref, rb_ref, taps_ref, slide_hbm, w2_hbm, w3_hbm, wk_hbm, wv_hbm, q_hbm,
    keep_ref, send_ref,
    slide, w2, w3, wk, wv, q, sems, toep, xb, lhs1, fmap, lhs2, smap, lhs3, third, kbd, vbd, out,
    *, col_last, row_last,
):
    col = lax.axis_index("cols")
    row = lax.axis_index("rows")
    copies = [
        pltpu.make_async_copy(src, dst, sems.at[i])
        for i, (src, dst) in enumerate(
            ((slide_hbm, slide), (w2_hbm, w2), (w3_hbm, w3), (wk_hbm, wk), (wv_hbm, wv), (q_hbm, q))
        )
    ]
    for copy in copies:
        copy.start()

    def band(k, carry):
        base = pl.multiple_of(k * 128, 128)
        toep[pl.ds(base, 128), :] = jnp.zeros((128, BLOCK_LANES), jnp.bfloat16)
        p0 = taps_ref[k, 0:16, :]
        p1 = taps_ref[k, 16:32, :]
        p2 = taps_ref[k, 32:48, :]
        for m in range(BLOCK_LANES // 256):
            toep[pl.ds(base + 16 * m, 16), 256 * m : 256 * m + 128] = p0
            toep[pl.ds(base + 16 * m, 16), 256 * m + 128 : 256 * m + 256] = p1
            toep[pl.ds(base + 16 * m + 16, 16), 256 * m + 128 : 256 * m + 256] = p2
        return carry

    lax.fori_loop(0, TAPS1, band, 0)

    even_col = col % 2 == 0
    even_row = row % 2 == 0
    copies[0].wait()
    for c in range(3):
        above = jnp.where(even_row, rb_ref[c].astype(jnp.float32), ra_ref[c].astype(jnp.float32))
        below = jnp.where(even_row, ra_ref[c].astype(jnp.float32), rb_ref[c].astype(jnp.float32))[0:8]
        windows(xb, c, 0, above[:, 0:512], above[:, 512:640], above[:, 512:640])
        windows(xb, c, 280, below[:, 0:512], below[:, 512:640], below[:, 512:640])
        for b in range(BLOCKS):
            xb[b, c, 288:328, :] = jnp.zeros((40, 128), jnp.float32)
        for half in range(2):
            g = BEFORE * (2 * c + half)

            def part(k, carry, c=c, half=half, g=g):
                r = pl.multiple_of(k * 32, 32)
                ca = ca_ref[pl.ds(r, 32), :].astype(jnp.float32)
                cb = cb_ref[pl.ds(r, 32), :].astype(jnp.float32)
                left = jnp.where(even_col, cb, ca)
                right = jnp.where(even_col, ca, cb)
                left = pltpu.roll(left, 128 - g, 1) if g else left
                right = pltpu.roll(right, (128 - g + BEFORE) % 128, 1)
                main = slide[c, pl.ds(half * 128 + r, 32), :].astype(jnp.float32)
                windows(xb, c, half * 128 + 24 + r, main, left, right)
                return carry

            lax.fori_loop(0, 4, part, 0)

    for b in range(BLOCKS):
        for c in range(3):
            for kh in range(6):
                k = 6 * c + kh
                lhs1[ROWS1 * b : ROWS1 * b + ROWS1, 128 * k : 128 * k + 128] = xb[
                    b, c, pl.ds(24 - BEFORE + kh, ROWS1, stride=4), :
                ].astype(jnp.bfloat16)

    def first(n, carry):
        lanes = pl.ds(pl.multiple_of(n * 256, 256), 256)
        acc = gelu(jnp.dot(lhs1[...], toep[:, lanes], preferred_element_type=jnp.float32))
        for b in range(BLOCKS):
            for u in range(2):
                fmap[b, 2 * n + u, 0:ROWS1, :] = acc[ROWS1 * b : ROWS1 * b + ROWS1, 128 * u : 128 * u + 128]
        return carry

    lax.fori_loop(0, BLOCK_LANES // 256, first, 0)

    @pl.when(row == 0)
    def _():
        for b in range(BLOCKS):
            fmap[b, :, 0:5, :] = jnp.zeros((BLOCK_LANES // 128, 5, 128), jnp.float32)

    @pl.when(row == row_last)
    def _():
        for b in range(BLOCKS):
            fmap[b, :, 69:70, :] = jnp.zeros((BLOCK_LANES // 128, 1, 128), jnp.float32)

    @pl.when(col == 0)
    def _():
        fmap[0, 0:2, 0:ROWS1, :] = jnp.zeros((2, ROWS1, 128), jnp.float32)
        fmap[0, 2, 0:ROWS1, 0:64] = jnp.zeros((ROWS1, 64), jnp.float32)

    @pl.when(col == col_last)
    def _():
        tile, side = divmod(133 - 4 * BLOCK_COLS, 2)
        fmap[4, tile, 0:ROWS1, 64 * side : 64 * side + 64] = jnp.zeros((ROWS1, 64), jnp.float32)

    for kh in range(6):
        for pair in range(COLS2 // 2):
            both = []
            for j in (2 * pair, 2 * pair + 1):
                b, t = divmod(j, 7)
                rows = pl.ds(kh, ROWS2, stride=4)
                tiles = [divmod(14 * b + 2 * t + u, 14) for u in range(3)]
                both.append([fmap[block, tile, rows, :] for block, tile in tiles])
            for u in range(3):
                lhs2[48 * pair : 48 * pair + 48, 384 * kh + 128 * u : 384 * kh + 128 * u + 128] = jnp.concatenate(
                    [both[0][u], both[1][u]], axis=0
                ).astype(jnp.bfloat16)
    copies[1].wait()
    for start, size in ((0, 288), (288, 288), (576, 240)):
        acc = gelu(jnp.dot(lhs2[start : start + size, :], w2[...], preferred_element_type=jnp.float32))
        for u in range(2):
            smap[u, start // ROWS2 : (start + size) // ROWS2] = acc[:, 128 * u : 128 * u + 128].reshape(
                size // ROWS2, ROWS2, 128
            )

    @pl.when(row == 0)
    def _():
        smap[:, :, 0:1, :] = jnp.zeros((2, COLS2, 1, 128), jnp.float32)

    @pl.when(col == 0)
    def _():
        smap[:, 0] = jnp.zeros((2, ROWS2, 128), jnp.float32)

    for kh in range(3):
        for kw in range(3):
            k = 3 * kh + kw
            for pair in range(8):
                for u in range(2):
                    lhs3[16 * pair : 16 * pair + 16, 256 * k + 128 * u : 256 * k + 128 * u + 128] = jnp.concatenate(
                        [
                            smap[u, 4 * pair + 2 * v + kw, pl.ds(kh, 8, stride=2), :]
                            for v in range(2)
                        ],
                        axis=0,
                    ).astype(jnp.bfloat16)
    copies[2].wait()

    def conv3(n, carry):
        lanes = pl.ds(pl.multiple_of(n * 256, 256), 256)
        third[:, lanes] = jnp.dot(lhs3[...], w3[:, lanes], preferred_element_type=jnp.float32)
        return carry

    lax.fori_loop(0, 4, conv3, 0)
    tokens = third[...]
    centred = tokens - jnp.mean(tokens, axis=-1, keepdims=True)
    var = jnp.mean(centred * centred, axis=-1, keepdims=True)
    normed = (centred * lax.rsqrt(var + 1e-05)).astype(jnp.bfloat16)
    lhs3[:, 0:1024] = normed
    copies[3].wait()
    copies[4].wait()
    low = lanes_of((128, 256)) < 128

    def project(n, carry):
        lanes = pl.ds(pl.multiple_of(n * 256, 256), 256)
        for w, dst in ((wk, kbd), (wv, vbd)):
            rows = jnp.dot(lhs3[:, 0:1024], w[:, lanes], preferred_element_type=jnp.float32)
            dst[n, 0:128, :] = jnp.where(low, rows, 0.0).astype(jnp.bfloat16)
            dst[n, 128:256, :] = jnp.where(low, 0.0, rows).astype(jnp.bfloat16)
        return carry

    lax.fori_loop(0, 4, project, 0)
    copies[5].wait()
    scale = 1.0 / math.sqrt(128)
    latents = out.shape[0]
    step = 128

    def attend(i, carry):
        rows = pl.ds(pl.multiple_of(i * step, step), step)
        lane = lanes_of((step, 128))
        stat = jnp.zeros((step, 128), jnp.float32)
        for n in range(4):
            scores = lax.dot_general(
                q[rows, 256 * n : 256 * n + 256], kbd[n], (((1,), (1,)), ((), ())), preferred_element_type=jnp.float32
            ) * scale
            probs, recips = [], []
            for u in range(2):
                s = scores[:, 128 * u : 128 * u + 128]
                peak = jnp.max(s, axis=1, keepdims=True)
                w = jnp.exp(s - peak)
                total = jnp.sum(w, axis=1, keepdims=True)
                probs.append(w.astype(jnp.bfloat16))
                recips.append(1.0 / total)
                stat = jnp.where(lane == 2 * n + u, peak + jnp.log(total), stat)
            o = jnp.dot(jnp.concatenate(probs, axis=1), vbd[n], preferred_element_type=jnp.float32)
            out[rows, 256 * n : 256 * n + 128] = o[:, 0:128] * recips[0]
            out[rows, 256 * n + 128 : 256 * n + 256] = o[:, 128:256] * recips[1]
        out[rows, 1024:1152] = stat
        return carry

    lax.fori_loop(0, latents // step, attend, 0)
    half = latents // 2
    bit = row % 2
    keep_ref[...] = out[pl.ds(pl.multiple_of(bit * half, half), half), :]
    other = pl.ds(pl.multiple_of((1 - bit) * half, half), half)
    send_ref[:, 0:1024] = out[other, 0:1024].astype(jnp.bfloat16)
    send_ref[:, 1024:1152] = pack_stat(out[other, 1024:1152])


def pack_stat(stat):
    lane = lanes_of(stat.shape)
    stat = jnp.where(lane < HEADS, stat, 0.0)
    high = stat.astype(jnp.bfloat16).astype(jnp.float32)
    rest = stat - high
    mid = rest.astype(jnp.bfloat16).astype(jnp.float32)
    low = rest - mid
    return (high + pltpu.roll(mid, HEADS, 1) + pltpu.roll(low, 2 * HEADS, 1)).astype(jnp.bfloat16)


def unpack_stat(stat):
    stat = stat.astype(jnp.float32)
    return stat + pltpu.roll(stat, 128 - HEADS, 1) + pltpu.roll(stat, 128 - 2 * HEADS, 1)


def merge_kernel(keep_ref, recv_ref, *outs, bit_of):
    n = keep_ref.shape[0]
    mine = keep_ref[:, 1024:1152]
    theirs = unpack_stat(recv_ref[:, 1024:1152])
    peak = jnp.maximum(mine, theirs)
    em = jnp.exp(mine - peak)
    total = em + jnp.exp(theirs - peak)
    share = em / total
    stat = peak + jnp.log(total)
    merged = []
    for h in range(HEADS):
        lanes = slice(128 * h, 128 * h + 128)
        a = keep_ref[:, lanes]
        b = recv_ref[:, lanes].astype(jnp.float32)
        merged.append(b + jnp.broadcast_to(share[:, h : h + 1], (n, 128)) * (a - b))
    if bit_of is None:
        for h in range(HEADS):
            outs[0][:, 128 * h : 128 * h + 128] = merged[h].astype(jnp.bfloat16)
        return
    upper = bit_of() == 1
    half = n // 2
    for h in range(HEADS):
        lanes = slice(128 * h, 128 * h + 128)
        outs[0][:, lanes] = jnp.where(upper, merged[h][half:], merged[h][:half])
        outs[1][:, lanes] = jnp.where(upper, merged[h][:half], merged[h][half:]).astype(jnp.bfloat16)
    outs[0][:, 1024:1152] = jnp.where(upper, stat[half:], stat[:half])
    outs[1][:, 1024:1152] = pack_stat(jnp.where(upper, stat[:half], stat[half:]))


def merge(keep, recv, bit_of):
    n, width = keep.shape
    if bit_of is None:
        shapes = jax.ShapeDtypeStruct((n, 1024), jnp.bfloat16)
    else:
        shapes = (
            jax.ShapeDtypeStruct((n // 2, width), jnp.float32),
            jax.ShapeDtypeStruct((n // 2, width), jnp.bfloat16),
        )
    return pl.pallas_call(functools.partial(merge_kernel, bit_of=bit_of), out_shape=shapes, name="merge")(keep, recv)


def swap_pairs(size, odd):
    pairs = []
    for i in range(1 if odd else 0, size - 1, 2):
        pairs += [(i, i + 1), (i + 1, i)]
    return pairs


def bits_of(size):
    return size.bit_length() - 1


def plan(mesh):
    n_rows, n_cols = mesh.shape["rows"], mesh.shape["cols"]
    row_bits = [("rows", k) for k in range(1, bits_of(n_rows))]
    col_bits = [("cols", k) for k in range(bits_of(n_cols))]
    return row_bits + col_bits, col_bits[:1] + row_bits + col_bits[1:]


def solution(mesh):
    n_rows, n_cols = mesh.shape["rows"], mesh.shape["cols"]
    orders = plan(mesh)

    def partner(index, stage):
        col, row = divmod(index, n_rows)
        if stage < 0:
            return col * n_rows + (row ^ 1)
        axis, k = orders[row & 1][stage]
        return col * n_rows + (row ^ (1 << k)) if axis == "rows" else (col ^ (1 << k)) * n_rows + row

    def exchange(value, stage):
        pairs = [(i, partner(i, stage)) for i in range(n_rows * n_cols)]
        return lax.ppermute(value, ("cols", "rows"), pairs)

    def bit_of(stage):
        def read():
            row = lax.axis_index("rows")
            (axis0, k0), (axis1, k1) = orders[0][stage], orders[1][stage]
            return jnp.where(
                row % 2 == 0, (lax.axis_index(axis0) >> k0) & 1, (lax.axis_index(axis1) >> k1) & 1
            )

        return read

    def order_queries(queries):
        latents, width = queries.shape
        share = latents // (n_rows * n_cols)
        names = [("cols", k) for k in reversed(range(bits_of(n_cols)))]
        names += [("rows", k) for k in reversed(range(bits_of(n_rows)))]
        split = queries.reshape([2] * len(names) + [share, width])
        at = names.index(("rows", 0))
        rest = names[:at] + names[at + 1 :]
        halves = []
        for core in range(2):
            part = lax.index_in_dim(split, core, at, keepdims=False)
            axes = [rest.index(name) for name in orders[core]]
            halves.append(part.transpose(axes + [len(rest), len(rest) + 1]).reshape(latents // 2, width))
        return jnp.concatenate(halves, axis=0)

    def on_device(slide_pixels, stem_first, stem_second, stem_third, key_weight, value_weight, queries):
        bf16 = jnp.bfloat16
        edge = jax.ShapeDtypeStruct((128, 128), bf16)
        col_a, col_b = pl.pallas_call(
            col_edges_kernel,
            grid=(1,),
            in_specs=[
                pl.BlockSpec((3, 256, 128), lambda i: (0, 0, 0)),
                pl.BlockSpec((3, 256, 128), lambda i: (0, 0, 3)),
            ],
            out_specs=[pl.BlockSpec((128, 128), lambda i: (0, 0))] * 2,
            out_shape=(edge, edge),
            name="col_edges",
        )(slide_pixels, slide_pixels)
        col_a = lax.ppermute(col_a, "cols", swap_pairs(n_cols, False))
        col_b = lax.ppermute(col_b, "cols", swap_pairs(n_cols, True))
        rim = jax.ShapeDtypeStruct((3, 24, 640), bf16)
        row_a, row_b = pl.pallas_call(
            row_edges_kernel,
            grid=(1,),
            in_specs=[
                pl.BlockSpec((3, 32, 512), lambda i: (0, 0, 0)),
                pl.BlockSpec((3, 32, 512), lambda i: (0, 7, 0)),
                pl.BlockSpec((128, 128), lambda i: (0, 0)),
                pl.BlockSpec((128, 128), lambda i: (0, 0)),
            ],
            out_specs=[pl.BlockSpec((3, 24, 640), lambda i: (0, 0, 0))] * 2,
            out_shape=(rim, rim),
            name="row_edges",
        )(slide_pixels, slide_pixels, col_a, col_b)
        row_a = lax.ppermute(row_a, "rows", swap_pairs(n_rows, False))
        row_b = lax.ppermute(row_b, "rows", swap_pairs(n_rows, True))

        taps = stem_first.transpose(2, 0, 1, 3).reshape(TAPS1, 6, 64)
        taps = sum(
            jnp.pad(taps, ((0, 0), (top, 42 - top), (64 * side, 64 - 64 * side)))
            for top, side in ((0, 0), (4, 1), (24, 0), (28, 1))
        )
        latents = queries.shape[0]
        half = latents // 2
        any_spec = pl.BlockSpec(memory_space=pl.ANY)
        vmem_spec = pl.BlockSpec(memory_space=VMEM)
        keep, send = pl.pallas_call(
            functools.partial(main_kernel, col_last=n_cols - 1, row_last=n_rows - 1),
            in_specs=[vmem_spec] * 5 + [any_spec] * 6,
            out_specs=[vmem_spec] * 2,
            out_shape=(
                jax.ShapeDtypeStruct((half, 1024 + STAT), jnp.float32),
                jax.ShapeDtypeStruct((half, 1024 + STAT), bf16),
            ),
            scratch_shapes=[
                pltpu.VMEM((3, 256, 512), bf16),
                pltpu.VMEM((2304, 256), bf16),
                pltpu.VMEM((2304, 1024), bf16),
                pltpu.VMEM((1024, 1024), bf16),
                pltpu.VMEM((1024, 1024), bf16),
                pltpu.VMEM((latents, 1024), bf16),
                pltpu.SemaphoreType.DMA((6,)),
                pltpu.VMEM((TAPS1 * 128, BLOCK_LANES), bf16),
                pltpu.VMEM((BLOCKS, 3, 328, 128), jnp.float32),
                pltpu.VMEM((BLOCKS * ROWS1, TAPS1 * 128), bf16),
                pltpu.VMEM((BLOCKS, BLOCK_LANES // 128, 104, 128), jnp.float32),
                pltpu.VMEM((COLS2 * ROWS2, 2304), bf16),
                pltpu.VMEM((2, COLS2, ROWS2, 128), jnp.float32),
                pltpu.VMEM((128, 2304), bf16),
                pltpu.VMEM((128, 1024), jnp.float32),
                pltpu.VMEM((4, 256, 256), bf16),
                pltpu.VMEM((4, 256, 256), bf16),
                pltpu.VMEM((latents, 1024 + STAT), jnp.float32),
            ],
            compiler_params=pltpu.CompilerParams(vmem_limit_bytes=60 * 1024 * 1024),
            name="read",
        )(
            col_a, col_b, row_a, row_b, taps, slide_pixels,
            stem_second.reshape(2304, 256), stem_third.reshape(2304, 1024),
            key_weight, value_weight, order_queries(queries),
        )
        recv = exchange(send, -1)
        stages = len(orders[0])
        for stage in range(stages):
            keep, send = merge(keep, recv, bit_of(stage))
            recv = exchange(send, stage)
        return merge(keep, recv, None)

    placed = (P(None, "rows", "cols"), P(), P(), P(), P(), P(), P())
    return jax.shard_map(
        on_device, mesh=mesh, in_specs=placed, out_specs=P(("cols", "rows"), None), check_vma=False
    )
```

time: 332 us -> 82 us (0.25)
  waiting for transfers between devices: 112 us -> 15 us
  blocking collectives: 82.2 us -> 0 us
  local copies, waits for them, and re-layouts: 46.4 us -> 5.5 us
  Pallas kernels: 0 us -> 37.1 us
  matrix products: 35.3 us -> 0 us
  between operations: 13.8 us -> 0.09 us
  other arithmetic: 11.4 us -> 1.89 us
  starting transfers between devices: 28.8 us -> 22 us
    psum x1 -> x0, waiting for transfers between devices: 91.8 us -> none  [on_device(): weighted, row_total = lax.psum((weighted, row_total), ('cols', 'rows'))]
    pmax x1 -> x0, blocking collectives: 42.2 us -> none  [on_device(): peak_score = lax.pmax(jnp.max(scores, axis=2), ('cols', 'rows'))]
    psum x1 -> x0, blocking collectives: 40.1 us -> none  [on_device(): weighted, row_total = lax.psum((weighted, row_total), ('cols', 'rows'))]
    pallas_call x0 -> x8, Pallas kernels: none -> 37.1 us  [the longest x1 23 us: on_device(): pl.pallas_call(functools.partial(main_kernel, col_last=n_cols - 1, row_la...]
    conv_general_dilated x11 -> x0, local copies, waits for them, and re-layouts: 32.7 us -> none  [convolve(): lax.conv_general_dilated(features[None], kernel, (stride, stride), 'VALID...]
    conv_general_dilated x3 -> x0, matrix products: 27.6 us -> none  [convolve(): lax.conv_general_dilated(features[None], kernel, (stride, stride), 'VALID...]
    dot_general x4 -> x0, matrix products: 7.7 us -> none  [the longest x1 3.42 us: on_device(): jnp.einsum('hlt,thd->lhd', rounded, value_rows.reshape(tok_count, HEADS,...]
    ppermute x10 -> x9, starting transfers between devices: 28.8 us -> 22 us  [the longest x5 17.8 us: exchange(): return lax.ppermute(value, ('cols', 'rows'), pairs)]
  transfers between devices with their start and end apart: 11 -> 9, of which waited for: 9 -> 6; matrix products, arithmetic and copies ran while one was open for 1% -> 3% of each run, Pallas kernels for 0% -> 0%
where the time goes in v1:
time: 82 us; the launch traced here: 81.7 us
  Pallas kernels  37.1 us (45%)
  starting transfers between devices  22 us (27%)
  waiting for transfers between devices  15 us (18%)
  local copies, waits for them, and re-layouts  5.5 us (7%)
  other arithmetic  1.89 us (2%)
    pallas_call x1, Pallas kernels, on_device(): pl.pallas_call(functools.partial(main_kernel, col_last=n_cols - 1, row_la...  23 us
    ppermute x5, starting transfers between devices, exchange(): return lax.ppermute(value, ('cols', 'rows'), pairs)  17.8 us
    ppermute x5, waiting for transfers between devices, exchange(): return lax.ppermute(value, ('cols', 'rows'), pairs)  14.9 us
    pallas_call x5, Pallas kernels, merge(): pl.pallas_call(functools.partial(merge_kernel, bit_of=bit_of), out_shape=...  10.5 us
    unnamed x24, local copies, waits for them, and re-layouts  5.39 us
    ppermute x1, starting transfers between devices, on_device(): col_a = lax.ppermute(col_a, 'cols', swap_pairs(n_cols, False))  2.94 us
    pallas_call x1, Pallas kernels, on_device(): pl.pallas_call(col_edges_kernel, grid=(1,), in_specs=[pl.BlockSpec((3, 25...  1.9 us
    pallas_call x1, Pallas kernels, on_device(): pl.pallas_call(row_edges_kernel, grid=(1,), in_specs=[pl.BlockSpec((3, 32...  1.7 us
  transfers between devices with their start and end apart: 9, of which 6 were waited for; matrix products, arithmetic and copies ran while one was open for 3% of the time, Pallas kernels for 0%

profile of v1, /device:TPU:0, one launch (start us, length us, event | category | flops | bytes accessed | tf_op | source)
XLA Modules:
  0.0 81.7 jit_solution(2156740968360822315)
XLA Ops:
  0.0 1.9 %col_edges.1 = (bf16[128,128]{1,0:T(8,128)(2,1)}, bf16[128,128]{1,0:T(8,128)(2,1)}) custom-call(bf16[3,256,512]{2,1,0:T(8,128)(2,1)} %slide_hbm.1, bf16[3,256,512]{2,1,0:T(8,128)(2,1)} %slide_hbm.1), custom_call_target="tpu_custom_call" | custom-call | tf_op jit(solution)/shard_map/col_edges/pallas_call | solution.py:407
  1.9 2.9 %collective-permute-start = (bf16[128,128]{1,0:T(8,128)(2,1)}, bf16[128,128]{1,0:T(8,128)(2,1)S(1)}, u32[]{:S(2)}, u32[]{:S(2)}) collective-permute-start(bf16[128,128]{1,0:T(8,128)(2,1)} %get-tuple-element.19), channel_id=1, source_target_pairs={{0,4},{4,0},{8,12},{12,8},{16,20},{20,16},{24,28},{28,24},{1,5},{5... | collective-permute-start | bytes 98312 | tf_op jit(solution)/shard_map/ppermute | solution.py:418
  4.8 0.7 collective-permute-start.1
  5.7 1.1 %pad_maximum_fusion.q_hbm = bf16[512,1024]{1,0:T(8,128)(2,1)} fusion(bf16[256,1024]{1,0:T(8,128)(2,1)S(1)} %bitcast.17, bf16[256,1024]{1,0:T(8,128)(2,1)S(1)} %bitcast.16), kind=kLoop, calls=%fused_computation | loop fusion | flops 2097152 | bytes 2097152 | tf_op jit(solution)/shard_map/concatenate | solution.py:402
  6.8 0.1 collective-permute-done.ca_ref
  6.9 0.6 copy-done.4
  7.6 0.6 copy-done.5
  8.2 1.7 %row_edges.1 = (bf16[3,24,640]{2,1,0:T(8,128)(2,1)}, bf16[3,24,640]{2,1,0:T(8,128)(2,1)}) custom-call(bf16[3,256,512]{2,1,0:T(8,128)(2,1)} %slide_hbm.1, bf16[3,256,512]{2,1,0:T(8,128)(2,1)} %slide_hbm.1, bf16[128,128]{1,0:T(8,128)(2,1)} %copy-done.4, bf16[128,128]{1,0:T(8,128)(2,1)} %copy-done.5), custom_call_target="tpu_custom_call" | custom-call | tf_op jit(solution)/shard_map/row_edges/pallas_call | solution.py:421
  9.9 0.7 collective-permute-start.3
  10.5 0.8 pad_add_fusion.taps_ref
  11.4 0.6 copy-done.6
  12.0 23.0 %read.1 = (f32[256,1152]{1,0:T(8,128)}, bf16[256,1152]{1,0:T(8,128)(2,1)}) custom-call(bf16[128,128]{1,0:T(8,128)(2,1)} %copy-done.4, bf16[128,128]{1,0:T(8,128)(2,1)} %copy-done.5, bf16[3,24,640]{2,1,0:T(8,128)(2,1)} %copy-done.6, bf16[3,24,640]{2,1,0:T(8,128)(2,1)} %copy-done.7, bf16[18,48,128]{2,1,0:T(8,128)(2,1)} %pad_add_fusion.taps_ref, ...), custom_call_target="tpu_custom_call" | custom-call | tf_op jit(solution)/shard_map/read/pallas_call | solution.py:446
  35.0 5.1 %collective-permute-start.4 = (bf16[256,1152]{1,0:T(8,128)(2,1)}, bf16[256,1152]{1,0:T(8,128)(2,1)S(1)}, u32[]{:S(2)}, u32[]{:S(2)}) collective-permute-start(bf16[256,1152]{1,0:T(8,128)(2,1)} %get-tuple-element.24), channel_id=1, source_target_pairs={{0,1},{1,0},{2,3},{3,2},{4,5},{5,4},{6,7},{7,6},{8,9},{9,8},{10,11... | collective-permute-start | bytes 1769480 | tf_op jit(solution)/shard_map/ppermute | solution.py:377
  40.1 1.8 %collective-permute-done.4.recv_ref = bf16[256,1152]{1,0:T(8,128)(2,1)S(1)} collective-permute-done((bf16[256,1152]{1,0:T(8,128)(2,1)}, bf16[256,1152]{1,0:T(8,128)(2,1)S(1)}, u32[]{:S(2)}, u32[]{:S(2)}) %collective-permute-start.4) | collective-permute-done | bytes 589856 | tf_op jit(solution)/shard_map/ppermute | solution.py:377
  42.0 0.8 %copy-done.1 = bf16[256,1152]{1,0:T(8,128)(2,1)} copy-done((bf16[256,1152]{1,0:T(8,128)(2,1)}, bf16[256,1152]{1,0:T(8,128)(2,1)S(1)}, u32[]{:S(2)}) %copy-start.1) | copy-done | bytes 589848
  42.8 2.9 %merge.5 = (f32[128,1152]{1,0:T(8,128)}, bf16[128,1152]{1,0:T(8,128)(2,1)}) custom-call(f32[256,1152]{1,0:T(8,128)} %get-tuple-element.23.keep_ref, bf16[256,1152]{1,0:T(8,128)(2,1)} %copy-done.1), custom_call_target="tpu_custom_call" | custom-call | tf_op jit(solution)/shard_map/merge/pallas_call | solution.py:343
  45.6 1.9 %collective-permute-start.5 = (bf16[128,1152]{1,0:T(8,128)(2,1)}, bf16[128,1152]{1,0:T(8,128)(2,1)S(1)}, u32[]{:S(2)}, u32[]{:S(2)}) collective-permute-start(bf16[128,1152]{1,0:T(8,128)(2,1)} %get-tuple-element.26), channel_id=1, source_target_pairs={{0,2},{1,5},{2,0},{3,7},{4,6},{5,1},{6,4},{7,3},{8,10},{9,13},{10,... | collective-permute-start | bytes 884744 | tf_op jit(solution)/shard_map/ppermute | solution.py:377
  47.6 5.0 %collective-permute-done.5.recv_ref = bf16[128,1152]{1,0:T(8,128)(2,1)S(1)} collective-permute-done((bf16[128,1152]{1,0:T(8,128)(2,1)}, bf16[128,1152]{1,0:T(8,128)(2,1)S(1)}, u32[]{:S(2)}, u32[]{:S(2)}) %collective-permute-start.5) | collective-permute-done | bytes 294944 | tf_op jit(solution)/shard_map/ppermute | solution.py:377
  52.6 0.7 copy-done.2
  53.3 2.2 %merge.6 = (f32[64,1152]{1,0:T(8,128)}, bf16[64,1152]{1,0:T(8,128)(2,1)}) custom-call(f32[128,1152]{1,0:T(8,128)} %get-tuple-element.25.keep_ref, bf16[128,1152]{1,0:T(8,128)(2,1)} %copy-done.2), custom_call_target="tpu_custom_call" | custom-call | tf_op jit(solution)/shard_map/merge/pallas_call | solution.py:343
  55.5 4.3 %collective-permute-start.6 = (bf16[64,1152]{1,0:T(8,128)(2,1)}, bf16[64,1152]{1,0:T(8,128)(2,1)S(1)}, u32[]{:S(2)}, u32[]{:S(2)}) collective-permute-start(bf16[64,1152]{1,0:T(8,128)(2,1)} %get-tuple-element.28), channel_id=1, source_target_pairs={{0,4},{1,3},{2,6},{3,1},{4,0},{5,7},{6,2},{7,5},{8,12},{9,11},{10,... | collective-permute-start | bytes 442376 | tf_op jit(solution)/shard_map/ppermute | solution.py:377
  59.8 3.3 %collective-permute-done.6.recv_ref = bf16[64,1152]{1,0:T(8,128)(2,1)S(1)} collective-permute-done((bf16[64,1152]{1,0:T(8,128)(2,1)}, bf16[64,1152]{1,0:T(8,128)(2,1)S(1)}, u32[]{:S(2)}, u32[]{:S(2)}) %collective-permute-start.6) | collective-permute-done | bytes 147488 | tf_op jit(solution)/shard_map/ppermute | solution.py:377
  63.2 0.7 copy-done.3
  63.8 1.9 %merge.7 = (f32[32,1152]{1,0:T(8,128)}, bf16[32,1152]{1,0:T(8,128)(2,1)}) custom-call(f32[64,1152]{1,0:T(8,128)} %get-tuple-element.27.keep_ref, bf16[64,1152]{1,0:T(8,128)(2,1)} %copy-done.3), custom_call_target="tpu_custom_call" | custom-call | tf_op jit(solution)/shard_map/merge/pallas_call | solution.py:343
  65.8 3.5 %collective-permute-start.7 = (bf16[32,1152]{1,0:T(8,128)(2,1)}, bf16[32,1152]{1,0:T(8,128)(2,1)S(1)}, u32[]{:S(2)}, u32[]{:S(2)}) collective-permute-start(bf16[32,1152]{1,0:T(8,128)(2,1)} %get-tuple-element.30), channel_id=1, source_target_pairs={{0,8},{1,9},{2,10},{3,11},{4,12},{5,13},{6,14},{7,15},{8,0},{9,1},... | collective-permute-start | bytes 221192 | tf_op jit(solution)/shard_map/ppermute | solution.py:377
  69.2 2.5 %collective-permute-done.7.recv_ref = bf16[32,1152]{1,0:T(8,128)(2,1)S(1)} collective-permute-done((bf16[32,1152]{1,0:T(8,128)(2,1)}, bf16[32,1152]{1,0:T(8,128)(2,1)S(1)}, u32[]{:S(2)}, u32[]{:S(2)}) %collective-permute-start.7) | collective-permute-done | bytes 73760 | tf_op jit(solution)/shard_map/ppermute | solution.py:377
  71.8 0.6 copy-done.8
  72.4 1.8 %merge.8 = (f32[16,1152]{1,0:T(8,128)}, bf16[16,1152]{1,0:T(8,128)(2,1)}) custom-call(f32[32,1152]{1,0:T(8,128)} %get-tuple-element.29.keep_ref, bf16[32,1152]{1,0:T(8,128)(2,1)} %copy-done.8), custom_call_target="tpu_custom_call" | custom-call | tf_op jit(solution)/shard_map/merge/pallas_call | solution.py:343
  74.2 3.0 %collective-permute-start.8 = (bf16[16,1152]{1,0:T(8,128)(2,1)}, bf16[16,1152]{1,0:T(8,128)(2,1)S(1)}, u32[]{:S(2)}, u32[]{:S(2)}) collective-permute-start(bf16[16,1152]{1,0:T(8,128)(2,1)} %get-tuple-element.32), channel_id=1, source_target_pairs={{0,16},{1,17},{2,18},{3,19},{4,20},{5,21},{6,22},{7,23},{8,24},{9,... | collective-permute-start | bytes 110600 | tf_op jit(solution)/shard_map/ppermute | solution.py:377
  77.2 2.1 %collective-permute-done.8.recv_ref = bf16[16,1152]{1,0:T(8,128)(2,1)S(1)} collective-permute-done((bf16[16,1152]{1,0:T(8,128)(2,1)}, bf16[16,1152]{1,0:T(8,128)(2,1)S(1)}, u32[]{:S(2)}, u32[]{:S(2)}) %collective-permute-start.8) | collective-permute-done | bytes 36896 | tf_op jit(solution)/shard_map/ppermute | solution.py:377
  79.4 0.6 copy-done.9
  80.0 1.7 %merge.9 = bf16[16,1024]{1,0:T(8,128)(2,1)} custom-call(f32[16,1152]{1,0:T(8,128)} %get-tuple-element.31.keep_ref, bf16[16,1152]{1,0:T(8,128)(2,1)} %copy-done.9), custom_call_target="tpu_custom_call" | custom-call | tf_op jit(solution)/shard_map/merge/pallas_call | solution.py:343
  (22 shorter events, 0.3 us)
Async XLA Ops:
  0.0 5.5 %copy-start = (bf16[512,1024]{1,0:T(8,128)(2,1)S(1)}, bf16[512,1024]{1,0:T(8,128)(2,1)}, u32[]{:S(2)}) copy-start(bf16[512,1024]{1,0:T(8,128)(2,1)} %param.13) | copy-start | bytes 3145732
  1.9 5.0 %collective-permute-start = (bf16[128,128]{1,0:T(8,128)(2,1)}, bf16[128,128]{1,0:T(8,128)(2,1)S(1)}, u32[]{:S(2)}, u32[]{:S(2)}) collective-permute-start(bf16[128,128]{1,0:T(8,128)(2,1)} %get-tuple-element.19), channel_id=1, source_target_pairs={{0,4},{4,0},{8,12},{12,8},{16,20},{20,16},{24,28},{28,24},{1,5},{5... | collective-permute-start | bytes 98312 | tf_op jit(solution)/shard_map/ppermute | solution.py:418
  4.8 2.1 %collective-permute-start.1 = (bf16[128,128]{1,0:T(8,128)(2,1)}, bf16[128,128]{1,0:T(8,128)(2,1)S(1)}, u32[]{:S(2)}, u32[]{:S(2)}) collective-permute-start(bf16[128,128]{1,0:T(8,128)(2,1)} %get-tuple-element.20), channel_id=1, source_target_pairs={{4,8},{8,4},{12,16},{16,12},{20,24},{24,20},{5,9},{9,5},{13,17},{1... | collective-permute-start | bytes 98312 | tf_op jit(solution)/shard_map/ppermute | solution.py:419
  5.6 1.2 %copy-start.10 = (bf16[6,6,3,64]{3,2,1,0:T(4,128)(2,1)S(1)}, bf16[6,6,3,64]{3,2,1,0:T(4,128)(2,1)}, u32[]{:S(2)}) copy-start(bf16[6,6,3,64]{3,2,1,0:T(4,128)(2,1)} %param.8) | copy-start | bytes 41476
  6.9 0.6 copy-start.4
  7.6 0.6 copy-start.5
  9.9 1.5 %collective-permute-start.2 = (bf16[3,24,640]{2,1,0:T(8,128)(2,1)}, bf16[3,24,640]{2,1,0:T(8,128)(2,1)S(1)}, u32[]{:S(2)}, u32[]{:S(2)}) collective-permute-start(bf16[3,24,640]{2,1,0:T(8,128)(2,1)} %get-tuple-element.21), channel_id=1, source_target_pairs={{0,1},{1,0},{2,3},{3,2},{4,5},{5,4},{6,7},{7,6},{8,9},{9,8},{10,11... | collective-permute-start | bytes 276488 | tf_op jit(solution)/shard_map/ppermute | solution.py:434
  9.9 1.5 %collective-permute-start.3 = (bf16[3,24,640]{2,1,0:T(8,128)(2,1)}, bf16[3,24,640]{2,1,0:T(8,128)(2,1)S(1)}, u32[]{:S(2)}, u32[]{:S(2)}) collective-permute-start(bf16[3,24,640]{2,1,0:T(8,128)(2,1)} %get-tuple-element.22), channel_id=1, source_target_pairs={{1,2},{2,1},{5,6},{6,5},{9,10},{10,9},{13,14},{14,13},{17,18},{18,... | collective-permute-start | bytes 276488 | tf_op jit(solution)/shard_map/ppermute | solution.py:435
  11.4 0.6 copy-start.6
  11.4 0.7 copy-start.7
  35.0 6.9 %collective-permute-start.4 = (bf16[256,1152]{1,0:T(8,128)(2,1)}, bf16[256,1152]{1,0:T(8,128)(2,1)S(1)}, u32[]{:S(2)}, u32[]{:S(2)}) collective-permute-start(bf16[256,1152]{1,0:T(8,128)(2,1)} %get-tuple-element.24), channel_id=1, source_target_pairs={{0,1},{1,0},{2,3},{3,2},{4,5},{5,4},{6,7},{7,6},{8,9},{9,8},{10,11... | collective-permute-start | bytes 1769480 | tf_op jit(solution)/shard_map/ppermute | solution.py:377
  42.0 0.8 %copy-start.1 = (bf16[256,1152]{1,0:T(8,128)(2,1)}, bf16[256,1152]{1,0:T(8,128)(2,1)S(1)}, u32[]{:S(2)}) copy-start(bf16[256,1152]{1,0:T(8,128)(2,1)S(1)} %collective-permute-done.4.recv_ref) | copy-start | bytes 1769476
  45.6 6.9 %collective-permute-start.5 = (bf16[128,1152]{1,0:T(8,128)(2,1)}, bf16[128,1152]{1,0:T(8,128)(2,1)S(1)}, u32[]{:S(2)}, u32[]{:S(2)}) collective-permute-start(bf16[128,1152]{1,0:T(8,128)(2,1)} %get-tuple-element.26), channel_id=1, source_target_pairs={{0,2},{1,5},{2,0},{3,7},{4,6},{5,1},{6,4},{7,3},{8,10},{9,13},{10,... | collective-permute-start | bytes 884744 | tf_op jit(solution)/shard_map/ppermute | solution.py:377
  52.6 0.7 copy-start.2
  55.5 7.6 %collective-permute-start.6 = (bf16[64,1152]{1,0:T(8,128)(2,1)}, bf16[64,1152]{1,0:T(8,128)(2,1)S(1)}, u32[]{:S(2)}, u32[]{:S(2)}) collective-permute-start(bf16[64,1152]{1,0:T(8,128)(2,1)} %get-tuple-element.28), channel_id=1, source_target_pairs={{0,4},{1,3},{2,6},{3,1},{4,0},{5,7},{6,2},{7,5},{8,12},{9,11},{10,... | collective-permute-start | bytes 442376 | tf_op jit(solution)/shard_map/ppermute | solution.py:377
  63.2 0.7 copy-start.3
  65.8 6.0 %collective-permute-start.7 = (bf16[32,1152]{1,0:T(8,128)(2,1)}, bf16[32,1152]{1,0:T(8,128)(2,1)S(1)}, u32[]{:S(2)}, u32[]{:S(2)}) collective-permute-start(bf16[32,1152]{1,0:T(8,128)(2,1)} %get-tuple-element.30), channel_id=1, source_target_pairs={{0,8},{1,9},{2,10},{3,11},{4,12},{5,13},{6,14},{7,15},{8,0},{9,1},... | collective-permute-start | bytes 221192 | tf_op jit(solution)/shard_map/ppermute | solution.py:377
  71.8 0.6 copy-start.8
  74.2 5.2 %collective-permute-start.8 = (bf16[16,1152]{1,0:T(8,128)(2,1)}, bf16[16,1152]{1,0:T(8,128)(2,1)S(1)}, u32[]{:S(2)}, u32[]{:S(2)}) collective-permute-start(bf16[16,1152]{1,0:T(8,128)(2,1)} %get-tuple-element.32), channel_id=1, source_target_pairs={{0,16},{1,17},{2,18},{3,19},{4,20},{5,21},{6,22},{7,23},{8,24},{9,... | collective-permute-start | bytes 110600 | tf_op jit(solution)/shard_map/ppermute | solution.py:377
  79.4 0.6 copy-start.9

commit v2 on v1

v2 whole, which is shorter than its diff:
```python
import functools
import math

import jax
import jax.numpy as jnp
from jax import lax
from jax.experimental import pallas as pl
from jax.experimental.pallas import tpu as pltpu
from jax.sharding import PartitionSpec as P

HEADS = 8
BEFORE, AFTER = 21, 5
TAPS1 = 18
BLOCK_COLS = 28
BLOCKS = 5
BLOCK_LANES = BLOCK_COLS * 64
ROWS1 = 80
ROWS2 = 24
COLS2 = 34
STAT = 128
RIM = 24
STRIP = 144
VMEM = pltpu.MemorySpace.VMEM


def gelu(x):
    inner = x * (0.7978845608028654 + 0.035677408136300125 * (x * x))
    half = 0.5 * x
    return half + half * jnp.tanh(inner)


def lanes_of(shape):
    return lax.broadcasted_iota(jnp.int32, shape, len(shape) - 1)


def row_edges_kernel(slide, a_ref, b_ref):
    even = lax.axis_index("rows") % 2 == 0
    for c in range(3):
        top = slide[c, 0:RIM, :]
        bottom = slide[c, 224:256, :].astype(jnp.float32)[8:32].astype(jnp.bfloat16)

        @pl.when(even)
        def _():
            a_ref[c] = bottom
            b_ref[c] = top

        @pl.when(jnp.logical_not(even))
        def _():
            a_ref[c] = top
            b_ref[c] = bottom


def rims(c, ra_ref, rb_ref, lanes):
    even = lax.axis_index("rows") % 2 == 0
    ra = ra_ref[c, :, lanes].astype(jnp.float32)
    rb = rb_ref[c, :, lanes].astype(jnp.float32)
    return jnp.where(even, rb, ra), jnp.where(even, ra, rb)[0:8]


def col_edges_kernel(slide, ra_ref, rb_ref, a_ref, b_ref):
    even = lax.axis_index("cols") % 2 == 0
    lane = lanes_of((STRIP, 128))
    first = jnp.zeros((STRIP, 128), jnp.float32)
    last = jnp.zeros((STRIP, 128), jnp.float32)
    for c in range(3):
        sides = []
        for lanes in (slice(0, 128), slice(384, 512)):
            above, below = rims(c, ra_ref, rb_ref, lanes)
            sides.append(jnp.concatenate([above, slide[c, :, lanes].astype(jnp.float32), below], axis=0))
        for half in range(2):
            g = BEFORE * (2 * c + half)
            rows = slice(half * STRIP, half * STRIP + STRIP)
            lo = pltpu.roll(sides[0][rows], g, 1) if g else sides[0][rows]
            hi = pltpu.roll(sides[1][rows], (g + BEFORE) % 128, 1)
            first = jnp.where((lane >= g) & (lane < g + AFTER), lo, first)
            last = jnp.where((lane >= g) & (lane < g + BEFORE), hi, last)
    a_ref[...] = jnp.where(even, last, first).astype(jnp.bfloat16)
    b_ref[...] = jnp.where(even, first, last).astype(jnp.bfloat16)


def band_kernel(taps_ref, toep):
    def band(k, carry):
        base = pl.multiple_of(k * 128, 128)
        toep[pl.ds(base, 128), :] = jnp.zeros((128, BLOCK_LANES), jnp.bfloat16)
        p0 = taps_ref[k, 0:16, :]
        p1 = taps_ref[k, 16:32, :]
        p2 = taps_ref[k, 32:48, :]
        for m in range(BLOCK_LANES // 256):
            toep[pl.ds(base + 16 * m, 16), 256 * m : 256 * m + 128] = p0
            toep[pl.ds(base + 16 * m, 16), 256 * m + 128 : 256 * m + 256] = p1
            toep[pl.ds(base + 16 * m + 16, 16), 256 * m + 128 : 256 * m + 256] = p2
        return carry

    lax.fori_loop(0, TAPS1, band, 0)


def windows(refs, c, row0, main):
    n = main.shape[0]
    lane = lanes_of((n, 128))
    moved = pltpu.roll(main, BEFORE, 1)
    tiles = [moved[:, 128 * k : 128 * k + 128] for k in range(4)]
    tiles.append(jnp.where(lane < BEFORE, tiles[0], 0.0))
    for b, (ref, at) in enumerate(refs):
        t, s = divmod(4 * BLOCK_COLS * b, 128)
        value = tiles[t]
        if s:
            value = jnp.where(lane < 128 - s, pltpu.roll(value, 128 - s, 1), pltpu.roll(tiles[t + 1], 128 - s, 1))
        ref[at, c, pl.ds(row0, n), :] = value


def patch_rows(ref, at, lhs1, slot):
    for c in range(3):
        for kh in range(6):
            k = 6 * c + kh
            lhs1[ROWS1 * slot : ROWS1 * slot + ROWS1, 128 * k : 128 * k + 128] = ref[
                at, c, pl.ds(RIM - BEFORE + kh, ROWS1, stride=4), :
            ].astype(jnp.bfloat16)


def inner_kernel(slide, ra_ref, rb_ref, toep, edge, fmap, inner, lhs1):
    refs = [(edge, 0), (inner, 0), (inner, 1), (inner, 2), (edge, 1)]
    for c in range(3):
        above, below = rims(c, ra_ref, rb_ref, slice(None))
        windows(refs, c, 0, above)
        windows(refs, c, 280, below)
        for ref, at in refs:
            ref[at, c, 288:328, :] = jnp.zeros((40, 128), jnp.float32)

        def part(k, carry, c=c):
            r = pl.multiple_of(k * 32, 32)
            windows(refs, c, RIM + r, slide[c, pl.ds(r, 32), :].astype(jnp.float32))
            return carry

        lax.fori_loop(0, 8, part, 0)
    for b, (ref, at) in enumerate(refs):
        patch_rows(ref, at, lhs1, b)

    def first(n, carry):
        lanes = pl.ds(pl.multiple_of(n * 256, 256), 256)
        acc = gelu(jnp.dot(lhs1[...], toep[:, lanes], preferred_element_type=jnp.float32))
        for b in range(BLOCKS):
            for u in range(2):
                fmap[b, 2 * n + u, 0:ROWS1, :] = acc[ROWS1 * b : ROWS1 * b + ROWS1, 128 * u : 128 * u + 128]
        return carry

    lax.fori_loop(0, BLOCK_LANES // 256, first, 0)


def stem_kernel(
    ca_ref, cb_ref, edge_in, fmap_in, toep, w2, w3, wk, wv,
    edge, fmap, kv,
    lhs1, lhs2, smap, lhs3, third,
    *, col_last, row_last,
):
    col = lax.axis_index("cols")
    row = lax.axis_index("rows")
    even_col = col % 2 == 0
    lane = lanes_of((STRIP, 128))
    ca = ca_ref[...].astype(jnp.float32)
    cb = cb_ref[...].astype(jnp.float32)
    left_all = jnp.where(even_col, cb, ca)
    right_all = jnp.where(even_col, ca, cb)
    at_right = 512 + BEFORE - 4 * BLOCK_COLS * (BLOCKS - 1)
    for c in range(3):
        for half in range(2):
            g = BEFORE * (2 * c + half)
            rows = slice(half * STRIP, half * STRIP + STRIP)
            left = pltpu.roll(left_all, 128 - g, 1) if g else left_all
            right = pltpu.roll(right_all, (at_right - g) % 128, 1)
            edge[0, c, rows, :] = jnp.where(lane < BEFORE, left, edge_in[0, c, rows, :])
            edge[1, c, rows, :] = jnp.where(
                (lane >= at_right) & (lane < at_right + AFTER), right, edge_in[1, c, rows, :]
            )
    patch_rows(edge, 0, lhs1, 0)
    patch_rows(edge, 1, lhs1, 1)
    for slot, b, tiles in ((0, 0, (0, 1)), (1, BLOCKS - 1, (5,))):
        for n in tiles:
            acc = gelu(
                jnp.dot(
                    lhs1[ROWS1 * slot : ROWS1 * slot + ROWS1, :],
                    toep[:, 256 * n : 256 * n + 256],
                    preferred_element_type=jnp.float32,
                )
            )
            for u in range(2):
                fmap[b, 2 * n + u, 0:ROWS1, :] = acc[:, 128 * u : 128 * u + 128]

    @pl.when(row == 0)
    def _():
        for b in range(BLOCKS):
            fmap[b, :, 0:5, :] = jnp.zeros((BLOCK_LANES // 128, 5, 128), jnp.float32)

    @pl.when(row == row_last)
    def _():
        for b in range(BLOCKS):
            fmap[b, :, 69:70, :] = jnp.zeros((BLOCK_LANES // 128, 1, 128), jnp.float32)

    @pl.when(col == 0)
    def _():
        fmap[0, 0:2, 0:ROWS1, :] = jnp.zeros((2, ROWS1, 128), jnp.float32)
        fmap[0, 2, 0:ROWS1, 0:64] = jnp.zeros((ROWS1, 64), jnp.float32)

    @pl.when(col == col_last)
    def _():
        tile, side = divmod(133 - 4 * BLOCK_COLS, 2)
        fmap[4, tile, 0:ROWS1, 64 * side : 64 * side + 64] = jnp.zeros((ROWS1, 64), jnp.float32)

    for kh in range(6):
        for pair in range(COLS2 // 2):
            both = []
            for j in (2 * pair, 2 * pair + 1):
                b, t = divmod(j, 7)
                rows = pl.ds(kh, ROWS2, stride=4)
                tiles = [divmod(14 * b + 2 * t + u, 14) for u in range(3)]
                both.append([fmap[block, tile, rows, :] for block, tile in tiles])
            for u in range(3):
                lhs2[48 * pair : 48 * pair + 48, 384 * kh + 128 * u : 384 * kh + 128 * u + 128] = jnp.concatenate(
                    [both[0][u], both[1][u]], axis=0
                ).astype(jnp.bfloat16)
    for start, size in ((0, 288), (288, 288), (576, 240)):
        acc = gelu(jnp.dot(lhs2[start : start + size, :], w2[...], preferred_element_type=jnp.float32))
        for u in range(2):
            smap[u, start // ROWS2 : (start + size) // ROWS2] = acc[:, 128 * u : 128 * u + 128].reshape(
                size // ROWS2, ROWS2, 128
            )

    @pl.when(row == 0)
    def _():
        smap[:, :, 0:1, :] = jnp.zeros((2, COLS2, 1, 128), jnp.float32)

    @pl.when(col == 0)
    def _():
        smap[:, 0] = jnp.zeros((2, ROWS2, 128), jnp.float32)

    for kh in range(3):
        for kw in range(3):
            k = 3 * kh + kw
            for pair in range(8):
                for u in range(2):
                    lhs3[16 * pair : 16 * pair + 16, 256 * k + 128 * u : 256 * k + 128 * u + 128] = jnp.concatenate(
                        [
                            smap[u, 4 * pair + 2 * v + kw, pl.ds(kh, 8, stride=2), :]
                            for v in range(2)
                        ],
                        axis=0,
                    ).astype(jnp.bfloat16)

    def conv3(n, carry):
        lanes = pl.ds(pl.multiple_of(n * 256, 256), 256)
        third[:, lanes] = jnp.dot(lhs3[...], w3[:, lanes], preferred_element_type=jnp.float32)
        return carry

    lax.fori_loop(0, 4, conv3, 0)
    tokens = third[...]
    centred = tokens - jnp.mean(tokens, axis=-1, keepdims=True)
    var = jnp.mean(centred * centred, axis=-1, keepdims=True)
    lhs3[:, 0:1024] = (centred * lax.rsqrt(var + 1e-05)).astype(jnp.bfloat16)

    def project(n, carry):
        start = pl.multiple_of(n * 256, 256)
        for i, w in enumerate((wk, wv)):
            rows = jnp.dot(lhs3[:, 0:1024], w[:, pl.ds(start, 256)], preferred_element_type=jnp.float32)
            kv[:, pl.ds(1024 * i + start, 256)] = rows.astype(jnp.bfloat16)
        return carry

    lax.fori_loop(0, 4, project, 0)


def attend_kernel(q, mine, theirs, out, *, bit_of, keep):
    n = out.shape[0]
    quarter = 2 * (lax.axis_index("rows") % 2) + (bit_of() if keep else 1 - bit_of())
    rows = pl.ds(pl.multiple_of(quarter * n, n), n)
    scale = 1.0 / math.sqrt(128)
    lane = lanes_of((n, 128))
    stat = jnp.zeros((n, 128), jnp.float32)
    for h in range(HEADS):
        lanes = slice(128 * h, 128 * h + 128)
        past = slice(1024 + 128 * h, 1024 + 128 * h + 128)
        keys = jnp.concatenate([mine[:, lanes], theirs[:, lanes]], axis=0)
        values = jnp.concatenate([mine[:, past], theirs[:, past]], axis=0)
        scores = lax.dot_general(
            q[rows, lanes], keys, (((1,), (1,)), ((), ())), preferred_element_type=jnp.float32
        ) * scale
        peak = jnp.max(scores, axis=1, keepdims=True)
        w = jnp.exp(scores - peak)
        total = jnp.sum(w, axis=1, keepdims=True)
        o = jnp.dot(w.astype(jnp.bfloat16), values, preferred_element_type=jnp.float32)
        out[:, lanes] = (o * (1.0 / total)).astype(out.dtype)
        stat = jnp.where(lane == h, peak + jnp.log(total), stat)
    out[:, 1024:1152] = stat if keep else pack_stat(stat)


def pack_stat(stat):
    lane = lanes_of(stat.shape)
    stat = jnp.where(lane < HEADS, stat, 0.0)
    high = stat.astype(jnp.bfloat16).astype(jnp.float32)
    rest = stat - high
    mid = rest.astype(jnp.bfloat16).astype(jnp.float32)
    low = rest - mid
    return (high + pltpu.roll(mid, HEADS, 1) + pltpu.roll(low, 2 * HEADS, 1)).astype(jnp.bfloat16)


def unpack_stat(stat):
    stat = stat.astype(jnp.float32)
    return stat + pltpu.roll(stat, 128 - HEADS, 1) + pltpu.roll(stat, 128 - 2 * HEADS, 1)


def merge_kernel(keep_ref, recv_ref, *outs, bit_of):
    n = keep_ref.shape[0]
    mine = keep_ref[:, 1024:1152]
    theirs = unpack_stat(recv_ref[:, 1024:1152])
    peak = jnp.maximum(mine, theirs)
    em = jnp.exp(mine - peak)
    total = em + jnp.exp(theirs - peak)
    share = em / total
    stat = peak + jnp.log(total)
    merged = []
    for h in range(HEADS):
        lanes = slice(128 * h, 128 * h + 128)
        a = keep_ref[:, lanes]
        b = recv_ref[:, lanes].astype(jnp.float32)
        merged.append(b + jnp.broadcast_to(share[:, h : h + 1], (n, 128)) * (a - b))
    if bit_of is None:
        for h in range(HEADS):
            outs[0][:, 128 * h : 128 * h + 128] = merged[h].astype(jnp.bfloat16)
        return
    upper = bit_of() == 1
    half = n // 2
    for h in range(HEADS):
        lanes = slice(128 * h, 128 * h + 128)
        outs[0][:, lanes] = jnp.where(upper, merged[h][half:], merged[h][:half])
        outs[1][:, lanes] = jnp.where(upper, merged[h][:half], merged[h][half:]).astype(jnp.bfloat16)
    outs[0][:, 1024:1152] = jnp.where(upper, stat[half:], stat[:half])
    outs[1][:, 1024:1152] = pack_stat(jnp.where(upper, stat[:half], stat[half:]))


def near(x):
    return pltpu.with_memory_space_constraint(x, VMEM)


def call(kernel, name, args, outs, scratch=(), aliases=None, flops=0, moved=0, limit=None):
    spec = pl.BlockSpec(memory_space=VMEM)
    return pl.pallas_call(
        kernel,
        in_specs=[spec] * len(args),
        out_specs=[spec] * len(outs),
        out_shape=tuple(outs),
        scratch_shapes=list(scratch),
        input_output_aliases=aliases or {},
        cost_estimate=pl.CostEstimate(flops=flops, bytes_accessed=moved, transcendentals=0),
        compiler_params=pltpu.CompilerParams(vmem_limit_bytes=limit),
        name=name,
    )(*[near(x) for x in args])


def merge(keep, recv, bit_of):
    n, width = keep.shape
    if bit_of is None:
        outs = (jax.ShapeDtypeStruct((n, 1024), jnp.bfloat16),)
    else:
        outs = (VMEM((n // 2, width), jnp.float32), VMEM((n // 2, width), jnp.bfloat16))
    out = call(functools.partial(merge_kernel, bit_of=bit_of), "merge", (keep, recv), outs, limit=8 << 20)
    return out[0] if bit_of is None else out


def swap_pairs(size, odd):
    pairs = []
    for i in range(1 if odd else 0, size - 1, 2):
        pairs += [(i, i + 1), (i + 1, i)]
    return pairs


def bits_of(size):
    return size.bit_length() - 1


def plan(mesh):
    n_rows, n_cols = mesh.shape["rows"], mesh.shape["cols"]
    row_bits = [("rows", k) for k in range(1, bits_of(n_rows))]
    col_bits = [("cols", k) for k in range(bits_of(n_cols))]
    return row_bits + col_bits, col_bits[:1] + row_bits + col_bits[1:]


def solution(mesh):
    n_rows, n_cols = mesh.shape["rows"], mesh.shape["cols"]
    orders = plan(mesh)

    def partner(index, stage):
        col, row = divmod(index, n_rows)
        axis, k = orders[row & 1][stage]
        return col * n_rows + (row ^ (1 << k)) if axis == "rows" else (col ^ (1 << k)) * n_rows + row

    def exchange(value, stage):
        pairs = [(i, partner(i, stage)) for i in range(n_rows * n_cols)]
        return lax.ppermute(value, ("cols", "rows"), pairs)

    def bit_of(stage):
        def read():
            row = lax.axis_index("rows")
            (axis0, k0), (axis1, k1) = orders[0][stage], orders[1][stage]
            return jnp.where(
                row % 2 == 0, (lax.axis_index(axis0) >> k0) & 1, (lax.axis_index(axis1) >> k1) & 1
            )

        return read

    def order_queries(queries):
        latents, width = queries.shape
        share = latents // (n_rows * n_cols)
        names = [("cols", k) for k in reversed(range(bits_of(n_cols)))]
        names += [("rows", k) for k in reversed(range(bits_of(n_rows)))]
        split = queries.reshape([2] * len(names) + [share, width])
        at = names.index(("rows", 0))
        rest = names[:at] + names[at + 1 :]
        halves = []
        for core in range(2):
            part = lax.index_in_dim(split, core, at, keepdims=False)
            axes = [rest.index(name) for name in orders[core]]
            halves.append(part.transpose(axes + [len(rest), len(rest) + 1]).reshape(latents // 2, width))
        return jnp.concatenate(halves, axis=0)

    def on_device(slide_pixels, stem_first, stem_second, stem_third, key_weight, value_weight, queries):
        bf16, f32 = jnp.bfloat16, jnp.float32
        rim = VMEM((3, RIM, 512), bf16)
        row_a, row_b = call(row_edges_kernel, "row_edges", (slide_pixels,), (rim, rim), limit=8 << 20)
        row_a = lax.ppermute(row_a, "rows", swap_pairs(n_rows, False))
        row_b = lax.ppermute(row_b, "rows", swap_pairs(n_rows, True))
        strip = VMEM((STRIP, 128), bf16)
        col_a, col_b = call(
            col_edges_kernel, "col_edges", (slide_pixels, row_a, row_b), (strip, strip), limit=8 << 20
        )
        col_a = lax.ppermute(col_a, "cols", swap_pairs(n_cols, False))
        col_b = lax.ppermute(col_b, "cols", swap_pairs(n_cols, True))

        taps = stem_first.transpose(2, 0, 1, 3).reshape(TAPS1, 6, 64)
        taps = sum(
            jnp.pad(taps, ((0, 0), (top, 42 - top), (64 * side, 64 - 64 * side)))
            for top, side in ((0, 0), (4, 1), (24, 0), (28, 1))
        )
        (toep,) = call(
            band_kernel, "band", (taps,), (VMEM((TAPS1 * 128, BLOCK_LANES), bf16),), moved=4 << 20, limit=2 << 20
        )
        edge_shape = VMEM((2, 3, 328, 128), f32)
        fmap_shape = VMEM((BLOCKS, BLOCK_LANES // 128, 104, 128), f32)
        edge, fmap = call(
            inner_kernel,
            "inner",
            (slide_pixels, row_a, row_b, toep),
            (edge_shape, fmap_shape),
            scratch=[pltpu.VMEM((3, 3, 328, 128), f32), pltpu.VMEM((BLOCKS * ROWS1, TAPS1 * 128), bf16)],
            flops=2 * BLOCKS * ROWS1 * TAPS1 * 128 * BLOCK_LANES,
            moved=16 << 20,
            limit=16 << 20,
        )
        _, _, kv = call(
            functools.partial(stem_kernel, col_last=n_cols - 1, row_last=n_rows - 1),
            "stem",
            (
                col_a, col_b, edge, fmap, toep,
                stem_second.reshape(2304, 256), stem_third.reshape(2304, 1024), key_weight, value_weight,
            ),
            (edge_shape, fmap_shape, VMEM((128, 2048), bf16)),
            scratch=[
                pltpu.VMEM((2 * ROWS1, TAPS1 * 128), bf16),
                pltpu.VMEM((COLS2 * ROWS2, 2304), bf16),
                pltpu.VMEM((2, COLS2, ROWS2, 128), f32),
                pltpu.VMEM((128, 2304), bf16),
                pltpu.VMEM((128, 1024), f32),
            ],
            aliases={2: 0, 3: 1},
            flops=3 << 30,
            limit=16 << 20,
        )
        kv_other = lax.ppermute(kv, "rows", swap_pairs(n_rows, False))
        ordered = order_queries(queries)
        quarter = queries.shape[0] // 4
        width = 1024 + STAT

        def attend(q, keep, dtype):
            return call(
                functools.partial(attend_kernel, bit_of=bit_of(0), keep=keep),
                "attend",
                (q, kv, kv_other),
                (VMEM((quarter, width), dtype),),
                flops=1 << 30,
                limit=8 << 20,
            )[0]

        send = attend(ordered, False, bf16)
        ordered, send = lax.optimization_barrier((ordered, send))
        recv = exchange(send, 0)
        keep = attend(ordered, True, f32)
        for stage in range(1, len(orders[0])):
            keep, send = merge(keep, recv, bit_of(stage))
            recv = exchange(send, stage)
        return merge(keep, recv, None)

    placed = (P(None, "rows", "cols"), P(), P(), P(), P(), P(), P())
    return jax.shard_map(
        on_device, mesh=mesh, in_specs=placed, out_specs=P(("cols", "rows"), None), check_vma=False
    )
```

time: 82 us -> 54.1 us (0.66)
  Pallas kernels: 37.1 us -> 19.4 us
  starting transfers between devices: 22 us -> 18 us
  local copies, waits for them, and re-layouts: 5.5 us -> 2.41 us
  other arithmetic: 1.89 us -> 0.19 us
  waiting for transfers between devices: 15 us -> 13.6 us
    pallas_call x8 -> x11, Pallas kernels: 37.1 us -> 19.4 us  [call(): pl.pallas_call(kernel, in_specs=[spec] * len(args), out_specs=[spec] * le...]
    ppermute x5 -> x4, starting transfers between devices: 17.8 us -> 10.2 us  [exchange(): return lax.ppermute(value, ('cols', 'rows'), pairs)]
    unnamed x24 -> x18, local copies, waits for them, and re-layouts: 5.39 us -> 1.55 us
    ppermute x0 -> x1, starting transfers between devices: none -> 3.2 us  [on_device(): kv_other = lax.ppermute(kv, 'rows', swap_pairs(n_rows, False))]
    ppermute x5 -> x4, waiting for transfers between devices: 14.9 us -> 12.3 us  [exchange(): return lax.ppermute(value, ('cols', 'rows'), pairs)]
    ppermute x0 -> x1, waiting for transfers between devices: none -> 1.29 us  [on_device(): kv_other = lax.ppermute(kv, 'rows', swap_pairs(n_rows, False))]
    concatenate x1, other arithmetic: 1.08 us -> 0.07 us  [order_queries(): return jnp.concatenate(halves, axis=0)]
  transfers between devices with their start and end apart: 9 -> 9, of which waited for: 6 -> 5; matrix products, arithmetic and copies ran while one was open for 3% -> 2% of each run, Pallas kernels for 0% -> 21%
where the time goes in v2:
time: 54.1 us; the launch traced here: 53.9 us
  Pallas kernels  19.4 us (36%)
  starting transfers between devices  18 us (33%)
  waiting for transfers between devices  13.6 us (25%)
  local copies, waits for them, and re-layouts  2.41 us (4%)
    pallas_call x11, Pallas kernels, call(): pl.pallas_call(kernel, in_specs=[spec] * len(args), out_specs=[spec] * le...  19.4 us
    ppermute x4, waiting for transfers between devices, exchange(): return lax.ppermute(value, ('cols', 'rows'), pairs)  12.3 us
    ppermute x4, starting transfers between devices, exchange(): return lax.ppermute(value, ('cols', 'rows'), pairs)  10.2 us
    ppermute x1, starting transfers between devices, on_device(): kv_other = lax.ppermute(kv, 'rows', swap_pairs(n_rows, False))  3.2 us
    ppermute x1, starting transfers between devices, on_device(): col_a = lax.ppermute(col_a, 'cols', swap_pairs(n_cols, False))  2.58 us
    unnamed x18, local copies, waits for them, and re-layouts  1.55 us
    ppermute x1, waiting for transfers between devices, on_device(): kv_other = lax.ppermute(kv, 'rows', swap_pairs(n_rows, False))  1.29 us
  transfers between devices with their start and end apart: 9, of which 5 were waited for; matrix products, arithmetic and copies ran while one was open for 2% of the time, Pallas kernels for 21%

profile of v2, /device:TPU:0, one launch (start us, length us, event | category | flops | bytes accessed | tf_op | source)
XLA Modules:
  0.0 53.9 jit_solution(15860000542375871582)
XLA Ops:
  0.0 1.1 %copy-done = bf16[3,256,512]{2,1,0:T(8,128)(2,1)S(1)} copy-done((bf16[3,256,512]{2,1,0:T(8,128)(2,1)S(1)}, bf16[3,256,512]{2,1,0:T(8,128)(2,1)}, u32[]{:S(2)}) %copy-start) | copy-done | bytes 786456
  1.2 0.5 collective-permute-start
  1.7 0.7 %collective-permute-start.1 = (bf16[3,24,512]{2,1,0:T(8,128)(2,1)S(1)}, bf16[3,24,512]{2,1,0:T(8,128)(2,1)S(1)}, u32[]{:S(2)}, u32[]{:S(2)}) collective-permute-start(bf16[3,24,512]{2,1,0:T(8,128)(2,1)S(1)} %get-tuple-element.21), channel_id=1, source_target_pairs={{1,2},{2,1},{5,6},{6,5},{9,10},{10,9},{13,14},{14,13},{17,18},{18,... | collective-permute-start | bytes 221192 | tf_op jit(solution)/shard_map/ppermute | solution.py:427
  2.3 0.8 %copy.12 = bf16[3,6,6,64]{3,2,1,0:T(8,128)(2,1)S(1)} copy(bf16[3,6,6,64]{3,0,2,1:T(4,128)(2,1)} %bitcast.23) | data formatting | bytes 27648 | tf_op jit(solution)/shard_map/transpose | solution.py:435
  3.1 0.1 pad_add_fusion.taps_ref
  3.3 0.8 %band.1.toep = bf16[2304,1792]{1,0:T(8,128)(2,1)S(1)} custom-call(bf16[18,48,128]{2,1,0:T(8,128)(2,1)S(1)} %pad_add_fusion.taps_ref), custom_call_target="tpu_custom_call" | custom-call | bytes 4194304 | tf_op jit(solution)/shard_map/band/pallas_call | solution.py:343
  4.1 0.3 copy-done.1
  4.4 0.2 col_edges.1
  4.6 2.6 %collective-permute-start.2 = (bf16[144,128]{1,0:T(8,128)(2,1)S(1)}, bf16[144,128]{1,0:T(8,128)(2,1)S(1)}, u32[]{:S(2)}, u32[]{:S(2)}) collective-permute-start(bf16[144,128]{1,0:T(8,128)(2,1)S(1)} %get-tuple-element.22), channel_id=1, source_target_pairs={{0,4},{4,0},{8,12},{12,8},{16,20},{20,16},{24,28},{28,24},{1,5},{5... | collective-permute-start | bytes 110600 | tf_op jit(solution)/shard_map/ppermute | solution.py:432
  7.2 0.0 copy-start.4
  7.2 0.8 %collective-permute-start.3 = (bf16[144,128]{1,0:T(8,128)(2,1)S(1)}, bf16[144,128]{1,0:T(8,128)(2,1)S(1)}, u32[]{:S(2)}, u32[]{:S(2)}) collective-permute-start(bf16[144,128]{1,0:T(8,128)(2,1)S(1)} %get-tuple-element.23), channel_id=1, source_target_pairs={{4,8},{8,4},{12,16},{16,12},{20,24},{24,20},{5,9},{9,5},{13,17},{1... | collective-permute-start | bytes 110600 | tf_op jit(solution)/shard_map/ppermute | solution.py:433
  8.0 9.4 %inner.1 = (f32[2,3,328,128]{3,2,1,0:T(8,128)S(1)}, f32[5,14,104,128]{3,2,1,0:T(8,128)S(1)}) custom-call(bf16[3,256,512]{2,1,0:T(8,128)(2,1)S(1)} %copy-done.1, bf16[3,24,512]{2,1,0:T(8,128)(2,1)S(1)} %collective-permute-done.ra_ref, bf16[3,24,512]{2,1,0:T(8,128)(2,1)S(1)} %collective-permute-done.1.rb_ref, bf16[2304,1792]{1,0:T(8,128)(2,1)S(1)} %band.1.toep), custom_call_target="tpu_custom_call" | custom-call | flops 3303014400 | bytes 16777216 | tf_op jit(solution)/shard_map/inner/pallas_call | solution.py:343
  17.5 0.0 copy-start.5
  17.5 5.6 %stem.1 = (f32[2,3,328,128]{3,2,1,0:T(8,128)S(1)}, f32[5,14,104,128]{3,2,1,0:T(8,128)S(1)}, bf16[128,2048]{1,0:T(8,128)(2,1)S(1)}) custom-call(bf16[144,128]{1,0:T(8,128)(2,1)S(1)} %collective-permute-done.2.ca_ref, bf16[144,128]{1,0:T(8,128)(2,1)S(1)} %collective-permute-done.3.cb_ref, ...), custom_call_target="tpu_custom_call", output_to_operand_aliasing={{0}: (2, {}), {1}: (3, {})} | custom-call | flops 3221225472 | tf_op jit(solution)/shard_map/stem/pallas_call | solution.py:343
  23.1 3.2 %collective-permute-start.4 = (bf16[128,2048]{1,0:T(8,128)(2,1)S(1)}, bf16[128,2048]{1,0:T(8,128)(2,1)S(1)}, u32[]{:S(2)}, u32[]{:S(2)}) collective-permute-start(bf16[128,2048]{1,0:T(8,128)(2,1)S(1)} %get-tuple-element.26.mine), channel_id=1, source_target_pairs={{0,1},{1,0},{2,3},{3,2},{4,5},{5,4},{6,7},{7,6},{8,9},{9,8},{10,11... | collective-permute-start | bytes 1572872 | tf_op jit(solution)/shard_map/ppermute | solution.py:474
  26.3 0.1 fusion
  26.5 0.1 pad_maximum_fusion.q
  26.6 1.3 %collective-permute-done.4.theirs = bf16[128,2048]{1,0:T(8,128)(2,1)S(1)} collective-permute-done((bf16[128,2048]{1,0:T(8,128)(2,1)S(1)}, bf16[128,2048]{1,0:T(8,128)(2,1)S(1)}, u32[]{:S(2)}, u32[]{:S(2)}) %collective-permute-start.4) | collective-permute-done | bytes 524320 | tf_op jit(solution)/shard_map/ppermute | solution.py:474
  27.9 0.9 %attend.2 = bf16[128,1152]{1,0:T(8,128)(2,1)S(1)} custom-call(bf16[512,1024]{1,0:T(8,128)(2,1)S(1)} %pad_maximum_fusion.q, bf16[128,2048]{1,0:T(8,128)(2,1)S(1)} %get-tuple-element.26.mine, bf16[128,2048]{1,0:T(8,128)(2,1)S(1)} %collective-permute-done.4.theirs), custom_call_target="tpu_custom_call" | custom-call | flops 1073741824 | tf_op jit(solution)/shard_map/attend/pallas_call | solution.py:343
  28.8 1.8 %collective-permute-start.5 = (bf16[128,1152]{1,0:T(8,128)(2,1)S(1)}, bf16[128,1152]{1,0:T(8,128)(2,1)S(1)}, u32[]{:S(2)}, u32[]{:S(2)}) collective-permute-start(bf16[128,1152]{1,0:T(8,128)(2,1)S(1)} %attend.2), channel_id=1, source_target_pairs={{0,2},{1,5},{2,0},{3,7},{4,6},{5,1},{6,4},{7,3},{8,10},{9,13},{10,... | collective-permute-start | bytes 884744 | tf_op jit(solution)/shard_map/ppermute | solution.py:395
  30.6 0.9 %attend.3.keep_ref = f32[128,1152]{1,0:T(8,128)S(1)} custom-call(bf16[512,1024]{1,0:T(8,128)(2,1)S(1)} %pad_maximum_fusion.q, bf16[128,2048]{1,0:T(8,128)(2,1)S(1)} %get-tuple-element.26.mine, bf16[128,2048]{1,0:T(8,128)(2,1)S(1)} %collective-permute-done.4.theirs), custom_call_target="tpu_custom_call" | custom-call | flops 1073741824 | tf_op jit(solution)/shard_map/attend/pallas_call | solution.py:343
  31.4 4.2 %collective-permute-done.5.recv_ref = bf16[128,1152]{1,0:T(8,128)(2,1)S(1)} collective-permute-done((bf16[128,1152]{1,0:T(8,128)(2,1)S(1)}, bf16[128,1152]{1,0:T(8,128)(2,1)S(1)}, u32[]{:S(2)}, u32[]{:S(2)}) %collective-permute-start.5) | collective-permute-done | bytes 294944 | tf_op jit(solution)/shard_map/ppermute | solution.py:395
  35.6 0.3 merge.4
  36.0 4.2 %collective-permute-start.6 = (bf16[64,1152]{1,0:T(8,128)(2,1)S(1)}, bf16[64,1152]{1,0:T(8,128)(2,1)S(1)}, u32[]{:S(2)}, u32[]{:S(2)}) collective-permute-start(bf16[64,1152]{1,0:T(8,128)(2,1)S(1)} %get-tuple-element.30), channel_id=1, source_target_pairs={{0,4},{1,3},{2,6},{3,1},{4,0},{5,7},{6,2},{7,5},{8,12},{9,11},{10,... | collective-permute-start | bytes 442376 | tf_op jit(solution)/shard_map/ppermute | solution.py:395
  40.1 3.1 %collective-permute-done.6.recv_ref = bf16[64,1152]{1,0:T(8,128)(2,1)S(1)} collective-permute-done((bf16[64,1152]{1,0:T(8,128)(2,1)S(1)}, bf16[64,1152]{1,0:T(8,128)(2,1)S(1)}, u32[]{:S(2)}, u32[]{:S(2)}) %collective-permute-start.6) | collective-permute-done | bytes 147488 | tf_op jit(solution)/shard_map/ppermute | solution.py:395
  43.3 0.2 merge.5
  43.5 1.6 %collective-permute-start.7 = (bf16[32,1152]{1,0:T(8,128)(2,1)S(1)}, bf16[32,1152]{1,0:T(8,128)(2,1)S(1)}, u32[]{:S(2)}, u32[]{:S(2)}) collective-permute-start(bf16[32,1152]{1,0:T(8,128)(2,1)S(1)} %get-tuple-element.32), channel_id=1, source_target_pairs={{0,8},{1,9},{2,10},{3,11},{4,12},{5,13},{6,14},{7,15},{8,0},{9,1},... | collective-permute-start | bytes 221192 | tf_op jit(solution)/shard_map/ppermute | solution.py:395
  45.2 2.8 %collective-permute-done.7.recv_ref = bf16[32,1152]{1,0:T(8,128)(2,1)S(1)} collective-permute-done((bf16[32,1152]{1,0:T(8,128)(2,1)S(1)}, bf16[32,1152]{1,0:T(8,128)(2,1)S(1)}, u32[]{:S(2)}, u32[]{:S(2)}) %collective-permute-start.7) | collective-permute-done | bytes 73760 | tf_op jit(solution)/shard_map/ppermute | solution.py:395
  47.9 0.2 merge.6
  48.1 2.7 %collective-permute-start.8 = (bf16[16,1152]{1,0:T(8,128)(2,1)S(1)}, bf16[16,1152]{1,0:T(8,128)(2,1)S(1)}, u32[]{:S(2)}, u32[]{:S(2)}) collective-permute-start(bf16[16,1152]{1,0:T(8,128)(2,1)S(1)} %get-tuple-element.34), channel_id=1, source_target_pairs={{0,16},{1,17},{2,18},{3,19},{4,20},{5,21},{6,22},{7,23},{8,24},{9,... | collective-permute-start | bytes 110600 | tf_op jit(solution)/shard_map/ppermute | solution.py:395
  50.8 2.3 %collective-permute-done.8.recv_ref = bf16[16,1152]{1,0:T(8,128)(2,1)S(1)} collective-permute-done((bf16[16,1152]{1,0:T(8,128)(2,1)S(1)}, bf16[16,1152]{1,0:T(8,128)(2,1)S(1)}, u32[]{:S(2)}, u32[]{:S(2)}) %collective-permute-start.8) | collective-permute-done | bytes 36896 | tf_op jit(solution)/shard_map/ppermute | solution.py:395
  53.1 0.8 %merge.7 = bf16[16,1024]{1,0:T(8,128)(2,1)} custom-call(f32[16,1152]{1,0:T(8,128)S(1)} %get-tuple-element.33.keep_ref, bf16[16,1152]{1,0:T(8,128)(2,1)S(1)} %collective-permute-done.8.recv_ref), custom_call_target="tpu_custom_call" | custom-call | tf_op jit(solution)/shard_map/merge/pallas_call | solution.py:343
  (20 shorter events, 0.1 us)
Async XLA Ops:
  0.0 1.1 %copy-start = (bf16[3,256,512]{2,1,0:T(8,128)(2,1)S(1)}, bf16[3,256,512]{2,1,0:T(8,128)(2,1)}, u32[]{:S(2)}) copy-start(bf16[3,256,512]{2,1,0:T(8,128)(2,1)} %slide.5) | copy-start | bytes 2359300
  1.2 2.9 %collective-permute-start = (bf16[3,24,512]{2,1,0:T(8,128)(2,1)S(1)}, bf16[3,24,512]{2,1,0:T(8,128)(2,1)S(1)}, u32[]{:S(2)}, u32[]{:S(2)}) collective-permute-start(bf16[3,24,512]{2,1,0:T(8,128)(2,1)S(1)} %get-tuple-element.20), channel_id=1, source_target_pairs={{0,1},{1,0},{2,3},{3,2},{4,5},{5,4},{6,7},{7,6},{8,9},{9,8},{10,11... | collective-permute-start | bytes 221192 | tf_op jit(solution)/shard_map/ppermute | solution.py:426
  1.7 2.4 %collective-permute-start.1 = (bf16[3,24,512]{2,1,0:T(8,128)(2,1)S(1)}, bf16[3,24,512]{2,1,0:T(8,128)(2,1)S(1)}, u32[]{:S(2)}, u32[]{:S(2)}) collective-permute-start(bf16[3,24,512]{2,1,0:T(8,128)(2,1)S(1)} %get-tuple-element.21), channel_id=1, source_target_pairs={{1,2},{2,1},{5,6},{6,5},{9,10},{10,9},{13,14},{14,13},{17,18},{18,... | collective-permute-start | bytes 221192 | tf_op jit(solution)/shard_map/ppermute | solution.py:427
  3.2 1.1 %copy-start.1 = (bf16[3,256,512]{2,1,0:T(8,128)(2,1)S(1)}, bf16[3,256,512]{2,1,0:T(8,128)(2,1)}, u32[]{:S(2)}) copy-start(bf16[3,256,512]{2,1,0:T(8,128)(2,1)} %slide.5) | copy-start | bytes 2359300
  4.6 12.9 %collective-permute-start.2 = (bf16[144,128]{1,0:T(8,128)(2,1)S(1)}, bf16[144,128]{1,0:T(8,128)(2,1)S(1)}, u32[]{:S(2)}, u32[]{:S(2)}) collective-permute-start(bf16[144,128]{1,0:T(8,128)(2,1)S(1)} %get-tuple-element.22), channel_id=1, source_target_pairs={{0,4},{4,0},{8,12},{12,8},{16,20},{20,16},{24,28},{28,24},{1,5},{5... | collective-permute-start | bytes 110600 | tf_op jit(solution)/shard_map/ppermute | solution.py:432
  7.1 10.3 %slice-start = ((s8[4718592]{0:T(1024)(128)(4,1)}), s8[4194304]{0:T(1024)(128)(4,1)S(1)}, s32[]{:S(2)}) async-start(s8[4718592]{0:T(1024)(128)(4,1)} %bitcast.15), calls=%async_computation | async-start | bytes 8388608
  7.2 10.3 %slice-start.1 = ((s8[4718592]{0:T(1024)(128)(4,1)}), s8[524288]{0:T(1024)(128)(4,1)S(1)}, s32[]{:S(2)}) async-start(s8[4718592]{0:T(1024)(128)(4,1)} %bitcast.15), calls=%async_computation.1 | async-start | bytes 1048576
  7.2 10.3 %copy-start.2 = (bf16[1024,1024]{1,0:T(8,128)(2,1)S(1)}, bf16[1024,1024]{1,0:T(8,128)(2,1)}, u32[]{:S(2)}) copy-start(bf16[1024,1024]{1,0:T(8,128)(2,1)} %wk.1) | copy-start | bytes 6291460
  7.2 10.3 %copy-start.3 = (bf16[1024,1024]{1,0:T(8,128)(2,1)S(1)}, bf16[1024,1024]{1,0:T(8,128)(2,1)}, u32[]{:S(2)}) copy-start(bf16[1024,1024]{1,0:T(8,128)(2,1)} %wv.1) | copy-start | bytes 6291460
  7.2 10.3 %copy-start.4 = (bf16[6,6,64,256]{3,2,1,0:T(8,128)(2,1)S(1)}, bf16[6,6,64,256]{3,2,1,0:T(8,128)(2,1)}, u32[]{:S(2)}) copy-start(bf16[6,6,64,256]{3,2,1,0:T(8,128)(2,1)} %param.9) | copy-start | bytes 3538948
  7.2 10.3 %collective-permute-start.3 = (bf16[144,128]{1,0:T(8,128)(2,1)S(1)}, bf16[144,128]{1,0:T(8,128)(2,1)S(1)}, u32[]{:S(2)}, u32[]{:S(2)}) collective-permute-start(bf16[144,128]{1,0:T(8,128)(2,1)S(1)} %get-tuple-element.23), channel_id=1, source_target_pairs={{4,8},{8,4},{12,16},{16,12},{20,24},{24,20},{5,9},{9,5},{13,17},{1... | collective-permute-start | bytes 110600 | tf_op jit(solution)/shard_map/ppermute | solution.py:433
  17.5 8.8 %copy-start.5 = (bf16[512,1024]{1,0:T(8,128)(2,1)S(1)}, bf16[512,1024]{1,0:T(8,128)(2,1)}, u32[]{:S(2)}) copy-start(bf16[512,1024]{1,0:T(8,128)(2,1)} %param.13) | copy-start | bytes 3145732
  23.1 4.7 %collective-permute-start.4 = (bf16[128,2048]{1,0:T(8,128)(2,1)S(1)}, bf16[128,2048]{1,0:T(8,128)(2,1)S(1)}, u32[]{:S(2)}, u32[]{:S(2)}) collective-permute-start(bf16[128,2048]{1,0:T(8,128)(2,1)S(1)} %get-tuple-element.26.mine), channel_id=1, source_target_pairs={{0,1},{1,0},{2,3},{3,2},{4,5},{5,4},{6,7},{7,6},{8,9},{9,8},{10,11... | collective-permute-start | bytes 1572872 | tf_op jit(solution)/shard_map/ppermute | solution.py:474
  28.8 6.8 %collective-permute-start.5 = (bf16[128,1152]{1,0:T(8,128)(2,1)S(1)}, bf16[128,1152]{1,0:T(8,128)(2,1)S(1)}, u32[]{:S(2)}, u32[]{:S(2)}) collective-permute-start(bf16[128,1152]{1,0:T(8,128)(2,1)S(1)} %attend.2), channel_id=1, source_target_pairs={{0,2},{1,5},{2,0},{3,7},{4,6},{5,1},{6,4},{7,3},{8,10},{9,13},{10,... | collective-permute-start | bytes 884744 | tf_op jit(solution)/shard_map/ppermute | solution.py:395
  36.0 7.3 %collective-permute-start.6 = (bf16[64,1152]{1,0:T(8,128)(2,1)S(1)}, bf16[64,1152]{1,0:T(8,128)(2,1)S(1)}, u32[]{:S(2)}, u32[]{:S(2)}) collective-permute-start(bf16[64,1152]{1,0:T(8,128)(2,1)S(1)} %get-tuple-element.30), channel_id=1, source_target_pairs={{0,4},{1,3},{2,6},{3,1},{4,0},{5,7},{6,2},{7,5},{8,12},{9,11},{10,... | collective-permute-start | bytes 442376 | tf_op jit(solution)/shard_map/ppermute | solution.py:395
  43.5 4.4 %collective-permute-start.7 = (bf16[32,1152]{1,0:T(8,128)(2,1)S(1)}, bf16[32,1152]{1,0:T(8,128)(2,1)S(1)}, u32[]{:S(2)}, u32[]{:S(2)}) collective-permute-start(bf16[32,1152]{1,0:T(8,128)(2,1)S(1)} %get-tuple-element.32), channel_id=1, source_target_pairs={{0,8},{1,9},{2,10},{3,11},{4,12},{5,13},{6,14},{7,15},{8,0},{9,1},... | collective-permute-start | bytes 221192 | tf_op jit(solution)/shard_map/ppermute | solution.py:395
  48.1 4.9 %collective-permute-start.8 = (bf16[16,1152]{1,0:T(8,128)(2,1)S(1)}, bf16[16,1152]{1,0:T(8,128)(2,1)S(1)}, u32[]{:S(2)}, u32[]{:S(2)}) collective-permute-start(bf16[16,1152]{1,0:T(8,128)(2,1)S(1)} %get-tuple-element.34), channel_id=1, source_target_pairs={{0,16},{1,17},{2,18},{3,19},{4,20},{5,21},{6,22},{7,23},{8,24},{9,... | collective-permute-start | bytes 110600 | tf_op jit(solution)/shard_map/ppermute | solution.py:395

commit v3 on v2

--- a/solution.py
+++ b/solution.py
@@ -19,6 +19,8 @@
 COLS2 = 34
 STAT = 128
 RIM = 24
+EDGE, MID = 16, 48
+ROWS_ALL = (MID + EDGE) * 5 + 48
 STRIP = 144
 VMEM = pltpu.MemorySpace.VMEM
 
@@ -33,21 +35,27 @@
     return lax.broadcasted_iota(jnp.int32, shape, len(shape) - 1)
 
 
-def row_edges_kernel(slide, a_ref, b_ref):
+def row_edges_kernel(slide_hbm, a_ref, b_ref, sems):
     even = lax.axis_index("rows") % 2 == 0
-    for c in range(3):
-        top = slide[c, 0:RIM, :]
-        bottom = slide[c, 224:256, :].astype(jnp.float32)[8:32].astype(jnp.bfloat16)
-
-        @pl.when(even)
-        def _():
-            a_ref[c] = bottom
-            b_ref[c] = top
-
-        @pl.when(jnp.logical_not(even))
-        def _():
-            a_ref[c] = top
-            b_ref[c] = bottom
+    height = slide_hbm.shape[1]
+
+    def send(first, second):
+        copies = [
+            pltpu.make_async_copy(slide_hbm.at[:, pl.ds(height - RIM, RIM), :], first, sems.at[0]),
+            pltpu.make_async_copy(slide_hbm.at[:, pl.ds(0, RIM), :], second, sems.at[1]),
+        ]
+        for copy in copies:
+            copy.start()
+        for copy in copies:
+            copy.wait()
+
+    @pl.when(even)
+    def _():
+        send(a_ref, b_ref)
+
+    @pl.when(jnp.logical_not(even))
+    def _():
+        send(b_ref, a_ref)
 
 
 def rims(c, ra_ref, rb_ref, lanes):
@@ -94,18 +102,36 @@
     lax.fori_loop(0, TAPS1, band, 0)
 
 
-def windows(refs, c, row0, main):
-    n = main.shape[0]
-    lane = lanes_of((n, 128))
-    moved = pltpu.roll(main, BEFORE, 1)
-    tiles = [moved[:, 128 * k : 128 * k + 128] for k in range(4)]
-    tiles.append(jnp.where(lane < BEFORE, tiles[0], 0.0))
-    for b, (ref, at) in enumerate(refs):
-        t, s = divmod(4 * BLOCK_COLS * b, 128)
-        value = tiles[t]
-        if s:
-            value = jnp.where(lane < 128 - s, pltpu.roll(value, 128 - s, 1), pltpu.roll(tiles[t + 1], 128 - s, 1))
-        ref[at, c, pl.ds(row0, n), :] = value
+def picks(first):
+    lane = lax.broadcasted_iota(jnp.int32, (256, 128), 1)
+    source = lax.broadcasted_iota(jnp.int32, (256, 128), 0)
+    out = []
+    for b, start in zip(range(BLOCKS), (0, 0, 128, 256, 256)):
+        if b in first:
+            hit = source + start == lane + (4 * BLOCK_COLS * b - BEFORE)
+            out.append(jnp.where(hit, 1.0, 0.0).astype(jnp.bfloat16))
+    return jnp.concatenate(out, axis=1)
+
+
+def cut(rows):
+    parts = []
+    for blocks, start in (((0, 1), 0), ((2,), 128), ((3, 4), 256)):
+        moved = jnp.dot(rows[:, start : start + 256], picks(blocks), preferred_element_type=jnp.float32)
+        parts += [moved[:, 128 * i : 128 * i + 128] for i in range(len(blocks))]
+    return parts
+
+
+def window_kernel(slide, xb, lhs1):
+    for c in range(3):
+        for b, part in enumerate(cut(slide[c])):
+            xb[b, c, RIM : RIM + 256, :] = part
+    for b in range(BLOCKS):
+        for c in range(3):
+            for kh in range(6):
+                k = 6 * c + kh
+                lhs1[MID * b : MID * b + MID, 128 * k : 128 * k + 128] = xb[
+                    b, c, pl.ds(RIM - BEFORE + kh + 4 * EDGE, MID, stride=4), :
+                ].astype(jnp.bfloat16)
 
 
 def patch_rows(ref, at, lhs1, slot):
@@ -117,41 +143,47 @@
             ].astype(jnp.bfloat16)
 
 
-def inner_kernel(slide, ra_ref, rb_ref, toep, edge, fmap, inner, lhs1):
-    refs = [(edge, 0), (inner, 0), (inner, 1), (inner, 2), (edge, 1)]
+def inner_kernel(ra_ref, rb_ref, toep, xb_in, lhs1_in, xb, fmap, lhs1):
+    outer = []
     for c in range(3):
-        above, below = rims(c, ra_ref, rb_ref, slice(None))
-        windows(refs, c, 0, above)
-        windows(refs, c, 280, below)
-        for ref, at in refs:
-            ref[at, c, 288:328, :] = jnp.zeros((40, 128), jnp.float32)
-
-        def part(k, carry, c=c):
-            r = pl.multiple_of(k * 32, 32)
-            windows(refs, c, RIM + r, slide[c, pl.ds(r, 32), :].astype(jnp.float32))
-            return carry
-
-        lax.fori_loop(0, 8, part, 0)
-    for b, (ref, at) in enumerate(refs):
-        patch_rows(ref, at, lhs1, b)
-
-    def first(n, carry):
-        lanes = pl.ds(pl.multiple_of(n * 256, 256), 256)
-        acc = gelu(jnp.dot(lhs1[...], toep[:, lanes], preferred_element_type=jnp.float32))
+        outer += rims(c, ra_ref, rb_ref, slice(None))
+    parts = cut(jnp.concatenate(outer, axis=0).astype(jnp.bfloat16))
+    for b in range(BLOCKS):
+        for c in range(3):
+            xb[b, c, 0:RIM, :] = parts[b][32 * c : 32 * c + RIM]
+            xb[b, c, 280:288, :] = parts[b][32 * c + RIM : 32 * c + 32]
+            xb[b, c, 288:328, :] = jnp.zeros((40, 128), jnp.float32)
+    top, bottom = MID * BLOCKS, (MID + EDGE) * BLOCKS
+    for c in range(3):
+        for kh in range(6):
+            lanes = slice(128 * (6 * c + kh), 128 * (6 * c + kh) + 128)
+            low = []
+            for b in range(BLOCKS):
+                lhs1[top + EDGE * b : top + EDGE * b + EDGE, lanes] = xb[
+                    b, c, pl.ds(RIM - BEFORE + kh, EDGE, stride=4), :
+                ].astype(jnp.bfloat16)
+                low.append(xb[b, c, pl.ds(RIM - BEFORE + kh + 4 * (EDGE + MID), 8, stride=4), :])
+            low.append(jnp.zeros((8, 128), jnp.float32))
+            lhs1[bottom : bottom + 48, lanes] = jnp.concatenate(low, axis=0).astype(jnp.bfloat16)
+    for n in range(BLOCK_LANES // 256):
+        acc = gelu(jnp.dot(lhs1[...], toep[:, 256 * n : 256 * n + 256], preferred_element_type=jnp.float32))
         for b in range(BLOCKS):
             for u in range(2):
-                fmap[b, 2 * n + u, 0:ROWS1, :] = acc[ROWS1 * b : ROWS1 * b + ROWS1, 128 * u : 128 * u + 128]
-        return carry
-
-    lax.fori_loop(0, BLOCK_LANES // 256, first, 0)
+                half = slice(128 * u, 128 * u + 128)
+                fmap[b, 2 * n + u, 0:EDGE, :] = acc[top + EDGE * b : top + EDGE * b + EDGE, half]
+                fmap[b, 2 * n + u, EDGE : EDGE + MID, :] = acc[MID * b : MID * b + MID, half]
+                fmap[b, 2 * n + u, EDGE + MID : EDGE + MID + 8, :] = acc[bottom + 8 * b : bottom + 8 * b + 8, half]
 
 
 def stem_kernel(
-    ca_ref, cb_ref, edge_in, fmap_in, toep, w2, w3, wk, wv,
-    edge, fmap, kv,
-    lhs1, lhs2, smap, lhs3, third,
+    ca_ref, cb_ref, xb_in, fmap_in, toep, w2, w3, wk_far, wv_far,
+    xb, fmap, normed, wk, wv,
+    lhs1, lhs2, smap, lhs3, third, sems,
     *, col_last, row_last,
 ):
+    copies = [pltpu.make_async_copy(wk_far, wk, sems.at[0]), pltpu.make_async_copy(wv_far, wv, sems.at[1])]
+    for copy in copies:
+        copy.start()
     col = lax.axis_index("cols")
     row = lax.axis_index("rows")
     even_col = col % 2 == 0
@@ -167,12 +199,12 @@
             rows = slice(half * STRIP, half * STRIP + STRIP)
             left = pltpu.roll(left_all, 128 - g, 1) if g else left_all
             right = pltpu.roll(right_all, (at_right - g) % 128, 1)
-            edge[0, c, rows, :] = jnp.where(lane < BEFORE, left, edge_in[0, c, rows, :])
-            edge[1, c, rows, :] = jnp.where(
-                (lane >= at_right) & (lane < at_right + AFTER), right, edge_in[1, c, rows, :]
+            xb[0, c, rows, :] = jnp.where(lane < BEFORE, left, xb[0, c, rows, :])
+            xb[BLOCKS - 1, c, rows, :] = jnp.where(
+                (lane >= at_right) & (lane < at_right + AFTER), right, xb[BLOCKS - 1, c, rows, :]
             )
-    patch_rows(edge, 0, lhs1, 0)
-    patch_rows(edge, 1, lhs1, 1)
+    patch_rows(xb, 0, lhs1, 0)
+    patch_rows(xb, BLOCKS - 1, lhs1, 1)
     for slot, b, tiles in ((0, 0, (0, 1)), (1, BLOCKS - 1, (5,))):
         for n in tiles:
             acc = gelu(
@@ -245,28 +277,28 @@
                         axis=0,
                     ).astype(jnp.bfloat16)
 
-    def conv3(n, carry):
-        lanes = pl.ds(pl.multiple_of(n * 256, 256), 256)
+    for n in range(4):
+        lanes = slice(256 * n, 256 * n + 256)
         third[:, lanes] = jnp.dot(lhs3[...], w3[:, lanes], preferred_element_type=jnp.float32)
-        return carry
-
-    lax.fori_loop(0, 4, conv3, 0)
     tokens = third[...]
     centred = tokens - jnp.mean(tokens, axis=-1, keepdims=True)
     var = jnp.mean(centred * centred, axis=-1, keepdims=True)
-    lhs3[:, 0:1024] = (centred * lax.rsqrt(var + 1e-05)).astype(jnp.bfloat16)
-
-    def project(n, carry):
-        start = pl.multiple_of(n * 256, 256)
-        for i, w in enumerate((wk, wv)):
-            rows = jnp.dot(lhs3[:, 0:1024], w[:, pl.ds(start, 256)], preferred_element_type=jnp.float32)
-            kv[:, pl.ds(1024 * i + start, 256)] = rows.astype(jnp.bfloat16)
-        return carry
-
-    lax.fori_loop(0, 4, project, 0)
-
-
-def attend_kernel(q, mine, theirs, out, *, bit_of, keep):
+    normed[...] = (centred * lax.rsqrt(var + 1e-05)).astype(jnp.bfloat16)
+    for copy in copies:
+        copy.wait()
+
+
+def project_kernel(mine, theirs, wk, wv, kv, tokens):
+    half = mine.shape[0]
+    tokens[0:half] = mine[...]
+    tokens[half:] = theirs[...]
+    for i, w in enumerate((wk, wv)):
+        for n in range(4):
+            rows = jnp.dot(tokens[...], w[:, 256 * n : 256 * n + 256], preferred_element_type=jnp.float32)
+            kv[:, 1024 * i + 256 * n : 1024 * i + 256 * n + 256] = rows.astype(jnp.bfloat16)
+
+
+def attend_kernel(q, kv, out, *, bit_of, keep):
     n = out.shape[0]
     quarter = 2 * (lax.axis_index("rows") % 2) + (bit_of() if keep else 1 - bit_of())
     rows = pl.ds(pl.multiple_of(quarter * n, n), n)
@@ -276,15 +308,13 @@
     for h in range(HEADS):
         lanes = slice(128 * h, 128 * h + 128)
         past = slice(1024 + 128 * h, 1024 + 128 * h + 128)
-        keys = jnp.concatenate([mine[:, lanes], theirs[:, lanes]], axis=0)
-        values = jnp.concatenate([mine[:, past], theirs[:, past]], axis=0)
         scores = lax.dot_general(
-            q[rows, lanes], keys, (((1,), (1,)), ((), ())), preferred_element_type=jnp.float32
+            q[rows, lanes], kv[:, lanes], (((1,), (1,)), ((), ())), preferred_element_type=jnp.float32
         ) * scale
         peak = jnp.max(scores, axis=1, keepdims=True)
         w = jnp.exp(scores - peak)
         total = jnp.sum(w, axis=1, keepdims=True)
-        o = jnp.dot(w.astype(jnp.bfloat16), values, preferred_element_type=jnp.float32)
+        o = jnp.dot(w.astype(jnp.bfloat16), kv[:, past], preferred_element_type=jnp.float32)
         out[:, lanes] = (o * (1.0 / total)).astype(out.dtype)
         stat = jnp.where(lane == h, peak + jnp.log(total), stat)
     out[:, 1024:1152] = stat if keep else pack_stat(stat)
@@ -334,15 +364,12 @@
     outs[1][:, 1024:1152] = pack_stat(jnp.where(upper, stat[:half], stat[half:]))
 
 
-def near(x):
-    return pltpu.with_memory_space_constraint(x, VMEM)
-
-
-def call(kernel, name, args, outs, scratch=(), aliases=None, flops=0, moved=0, limit=None):
+def call(kernel, name, args, outs, scratch=(), aliases=None, flops=0, moved=0, limit=None, far=()):
     spec = pl.BlockSpec(memory_space=VMEM)
+    far_spec = pl.BlockSpec(memory_space=pltpu.HBM)
     return pl.pallas_call(
         kernel,
-        in_specs=[spec] * len(args),
+        in_specs=[far_spec if i in far else spec for i in range(len(args))],
         out_specs=[spec] * len(outs),
         out_shape=tuple(outs),
         scratch_shapes=list(scratch),
@@ -350,7 +377,7 @@
         cost_estimate=pl.CostEstimate(flops=flops, bytes_accessed=moved, transcendentals=0),
         compiler_params=pltpu.CompilerParams(vmem_limit_bytes=limit),
         name=name,
-    )(*[near(x) for x in args])
+    )(*[pltpu.with_memory_space_constraint(x, pltpu.HBM if i in far else VMEM) for i, x in enumerate(args)])
 
 
 def merge(keep, recv, bit_of):
@@ -422,7 +449,15 @@
     def on_device(slide_pixels, stem_first, stem_second, stem_third, key_weight, value_weight, queries):
         bf16, f32 = jnp.bfloat16, jnp.float32
         rim = VMEM((3, RIM, 512), bf16)
-        row_a, row_b = call(row_edges_kernel, "row_edges", (slide_pixels,), (rim, rim), limit=8 << 20)
+        row_a, row_b = call(
+            row_edges_kernel,
+            "row_edges",
+            (slide_pixels,),
+            (rim, rim),
+            scratch=[pltpu.SemaphoreType.DMA((2,))],
+            limit=8 << 20,
+            far=(0,),
+        )
         row_a = lax.ppermute(row_a, "rows", swap_pairs(n_rows, False))
         row_b = lax.ppermute(row_b, "rows", swap_pairs(n_rows, True))
         strip = VMEM((STRIP, 128), bf16)
@@ -440,38 +475,53 @@
         (toep,) = call(
             band_kernel, "band", (taps,), (VMEM((TAPS1 * 128, BLOCK_LANES), bf16),), moved=4 << 20, limit=2 << 20
         )
-        edge_shape = VMEM((2, 3, 328, 128), f32)
+        xb_shape = VMEM((BLOCKS, 3, 328, 128), f32)
+        lhs1_shape = VMEM((ROWS_ALL, TAPS1 * 128), bf16)
         fmap_shape = VMEM((BLOCKS, BLOCK_LANES // 128, 104, 128), f32)
-        edge, fmap = call(
+        xb, lhs1 = call(
+            window_kernel, "windows", (slide_pixels,), (xb_shape, lhs1_shape), flops=1 << 28, moved=4 << 20, limit=8 << 20
+        )
+        xb, fmap, _ = call(
             inner_kernel,
             "inner",
-            (slide_pixels, row_a, row_b, toep),
-            (edge_shape, fmap_shape),
-            scratch=[pltpu.VMEM((3, 3, 328, 128), f32), pltpu.VMEM((BLOCKS * ROWS1, TAPS1 * 128), bf16)],
-            flops=2 * BLOCKS * ROWS1 * TAPS1 * 128 * BLOCK_LANES,
+            (row_a, row_b, toep, xb, lhs1),
+            (xb_shape, fmap_shape, lhs1_shape),
+            aliases={3: 0, 4: 2},
+            flops=2 * ROWS_ALL * TAPS1 * 128 * BLOCK_LANES,
             moved=16 << 20,
-            limit=16 << 20,
-        )
-        _, _, kv = call(
+            limit=8 << 20,
+        )
+        _, _, normed, key_near, value_near = call(
             functools.partial(stem_kernel, col_last=n_cols - 1, row_last=n_rows - 1),
             "stem",
             (
-                col_a, col_b, edge, fmap, toep,
-                stem_second.reshape(2304, 256), stem_third.reshape(2304, 1024), key_weight, value_weight,
+                col_a, col_b, xb, fmap, toep, stem_second.reshape(2304, 256), stem_third.reshape(2304, 1024),
+                key_weight, value_weight,
             ),
-            (edge_shape, fmap_shape, VMEM((128, 2048), bf16)),
+            (xb_shape, fmap_shape, VMEM((128, 1024), bf16), VMEM((1024, 1024), bf16), VMEM((1024, 1024), bf16)),
             scratch=[
                 pltpu.VMEM((2 * ROWS1, TAPS1 * 128), bf16),
                 pltpu.VMEM((COLS2 * ROWS2, 2304), bf16),
                 pltpu.VMEM((2, COLS2, ROWS2, 128), f32),
                 pltpu.VMEM((128, 2304), bf16),
                 pltpu.VMEM((128, 1024), f32),
+                pltpu.SemaphoreType.DMA((2,)),
             ],
             aliases={2: 0, 3: 1},
+            far=(7, 8),
             flops=3 << 30,
             limit=16 << 20,
         )
-        kv_other = lax.ppermute(kv, "rows", swap_pairs(n_rows, False))
+        normed_other = lax.ppermute(normed, "rows", swap_pairs(n_rows, False))
+        (kv,) = call(
+            project_kernel,
+            "project",
+            (normed, normed_other, key_near, value_near),
+            (VMEM((256, 2048), bf16),),
+            scratch=[pltpu.VMEM((256, 1024), bf16)],
+            flops=1 << 30,
+            limit=8 << 20,
+        )
         ordered = order_queries(queries)
         quarter = queries.shape[0] // 4
         width = 1024 + STAT
@@ -480,7 +530,7 @@
             return call(
                 functools.partial(attend_kernel, bit_of=bit_of(0), keep=keep),
                 "attend",
-                (q, kv, kv_other),
+                (q, kv),
                 (VMEM((quarter, width), dtype),),
                 flops=1 << 30,
                 limit=8 << 20,

time: 54.1 us -> 46.5 us (0.86)
  Pallas kernels: 19.4 us -> 14.1 us
  local copies, waits for them, and re-layouts: 2.41 us -> 1.29 us
  waiting for transfers between devices: 13.6 us -> 12.9 us
    pallas_call x11 -> x13, Pallas kernels: 19.4 us -> 14.1 us  [call(): pl.pallas_call(kernel, in_specs=[far_spec if i in far else spec for i in...]
    unnamed x18 -> x12, local copies, waits for them, and re-layouts: 1.55 us -> 0.44 us
    ppermute x1, starting transfers between devices: 3.2 us -> 2.64 us  [on_device(): normed_other = lax.ppermute(normed, 'rows', swap_pairs(n_rows, False))]
  transfers between devices with their start and end apart: 9 -> 9, of which waited for: 5 -> 5; matrix products, arithmetic and copies ran while one was open for 2% -> 2% of each run, Pallas kernels for 21% -> 12%
where the time goes in v3:
time: 46.5 us; the launch traced here: 46.3 us
  starting transfers between devices  17.5 us (38%)
  Pallas kernels  14.1 us (30%)
  waiting for transfers between devices  12.9 us (28%)
  local copies, waits for them, and re-layouts  1.29 us (3%)
    pallas_call x13, Pallas kernels, call(): pl.pallas_call(kernel, in_specs=[far_spec if i in far else spec for i in...  14.1 us
    ppermute x4, waiting for transfers between devices, exchange(): return lax.ppermute(value, ('cols', 'rows'), pairs)  12 us
    ppermute x4, starting transfers between devices, exchange(): return lax.ppermute(value, ('cols', 'rows'), pairs)  10.4 us
    ppermute x1, starting transfers between devices, on_device(): normed_other = lax.ppermute(normed, 'rows', swap_pairs(n_rows, False))  2.64 us
    ppermute x1, starting transfers between devices, on_device(): col_a = lax.ppermute(col_a, 'cols', swap_pairs(n_cols, False))  2.58 us
  transfers between devices with their start and end apart: 9, of which 5 were waited for; matrix products, arithmetic and copies ran while one was open for 2% of the time, Pallas kernels for 12%

profile of v3, /device:TPU:0, one launch (start us, length us, event | category | flops | bytes accessed | tf_op | source)
XLA Modules:
  0.0 46.3 jit_solution(1200419869201377416)
XLA Ops:
  0.0 0.9 %row_edges.1 = (bf16[3,24,512]{2,1,0:T(8,128)(2,1)S(1)}, bf16[3,24,512]{2,1,0:T(8,128)(2,1)S(1)}) custom-call(bf16[3,256,512]{2,1,0:T(8,128)(2,1)} %slide.3), custom_call_target="tpu_custom_call" | custom-call | tf_op jit(solution)/shard_map/row_edges/pallas_call | solution.py:370
  0.9 0.5 %collective-permute-start = (bf16[3,24,512]{2,1,0:T(8,128)(2,1)S(1)}, bf16[3,24,512]{2,1,0:T(8,128)(2,1)S(1)}, u32[]{:S(2)}, u32[]{:S(2)}) collective-permute-start(bf16[3,24,512]{2,1,0:T(8,128)(2,1)S(1)} %get-tuple-element.24), channel_id=1, source_target_pairs={{0,1},{1,0},{2,3},{3,2},{4,5},{5,4},{6,7},{7,6},{8,9},{9,8},{10,11... | collective-permute-start | bytes 221192 | tf_op jit(solution)/shard_map/ppermute | solution.py:461
  1.5 0.7 %collective-permute-start.1 = (bf16[3,24,512]{2,1,0:T(8,128)(2,1)S(1)}, bf16[3,24,512]{2,1,0:T(8,128)(2,1)S(1)}, u32[]{:S(2)}, u32[]{:S(2)}) collective-permute-start(bf16[3,24,512]{2,1,0:T(8,128)(2,1)S(1)} %get-tuple-element.25), channel_id=1, source_target_pairs={{1,2},{2,1},{5,6},{6,5},{9,10},{10,9},{13,14},{14,13},{17,18},{18,... | collective-permute-start | bytes 221192 | tf_op jit(solution)/shard_map/ppermute | solution.py:462
  2.1 0.8 %copy.14 = bf16[3,6,6,64]{3,2,1,0:T(8,128)(2,1)S(1)} copy(bf16[3,6,6,64]{3,0,2,1:T(4,128)(2,1)} %bitcast.23) | data formatting | bytes 27648 | tf_op jit(solution)/shard_map/transpose | solution.py:470
  2.9 0.1 pad_add_fusion.taps_ref
  3.0 0.8 %band.1.toep = bf16[2304,1792]{1,0:T(8,128)(2,1)S(1)} custom-call(bf16[18,48,128]{2,1,0:T(8,128)(2,1)S(1)} %pad_add_fusion.taps_ref), custom_call_target="tpu_custom_call" | custom-call | bytes 4194304 | tf_op jit(solution)/shard_map/band/pallas_call | solution.py:370
  3.8 0.3 copy-done
  4.2 0.6 %windows.1 = (f32[5,3,328,128]{3,2,1,0:T(8,128)S(1)}, bf16[368,2304]{1,0:T(8,128)(2,1)S(1)}) custom-call(bf16[3,256,512]{2,1,0:T(8,128)(2,1)S(1)} %copy-done), custom_call_target="tpu_custom_call" | custom-call | flops 268435456 | bytes 4194304 | tf_op jit(solution)/shard_map/windows/pallas_call | solution.py:370
  4.8 0.2 col_edges.1
  4.9 2.6 %collective-permute-start.2 = (bf16[144,128]{1,0:T(8,128)(2,1)S(1)}, bf16[144,128]{1,0:T(8,128)(2,1)S(1)}, u32[]{:S(2)}, u32[]{:S(2)}) collective-permute-start(bf16[144,128]{1,0:T(8,128)(2,1)S(1)} %get-tuple-element.26), channel_id=1, source_target_pairs={{0,4},{4,0},{8,12},{12,8},{16,20},{20,16},{24,28},{28,24},{1,5},{5... | collective-permute-start | bytes 110600 | tf_op jit(solution)/shard_map/ppermute | solution.py:467
  7.5 0.7 %collective-permute-start.3 = (bf16[144,128]{1,0:T(8,128)(2,1)S(1)}, bf16[144,128]{1,0:T(8,128)(2,1)S(1)}, u32[]{:S(2)}, u32[]{:S(2)}) collective-permute-start(bf16[144,128]{1,0:T(8,128)(2,1)S(1)} %get-tuple-element.27), channel_id=1, source_target_pairs={{4,8},{8,4},{12,16},{16,12},{20,24},{24,20},{5,9},{9,5},{13,17},{1... | collective-permute-start | bytes 110600 | tf_op jit(solution)/shard_map/ppermute | solution.py:468
  8.2 3.5 %inner.1 = (f32[5,3,328,128]{3,2,1,0:T(8,128)S(1)}, f32[5,14,104,128]{3,2,1,0:T(8,128)S(1)}, bf16[368,2304]{1,0:T(8,128)(2,1)S(1)}) custom-call(bf16[3,24,512]{2,1,0:T(8,128)(2,1)S(1)} %collective-permute-done.ra_ref, bf16[3,24,512]{2,1,0:T(8,128)(2,1)S(1)} %collective-permute-done.1.rb_ref, ...), custom_call_target="tpu_custom_call", output_to_operand_aliasing={{0}: (3, {}), {2}: (4, {})} | custom-call | flops 3038773248 | bytes 16777216 | tf_op jit(solution)/shard_map/inner/pallas_call | solution.py:370
  11.8 3.5 %stem.1 = (f32[5,3,328,128]{3,2,1,0:T(8,128)S(1)}, f32[5,14,104,128]{3,2,1,0:T(8,128)S(1)}, bf16[128,1024]{1,0:T(8,128)(2,1)S(1)}, bf16[1024,1024]{1,0:T(8,128)(2,1)S(1)}, bf16[1024,1024]{1,0:T(8,128)(2,1)S(1)}) custom-call(bf16[144,128]{1,0:T(8,128)(2,1)S(1)} %collective-permute-done.2.ca_ref, ...), custom_call_target="tpu_custom_call", output_to_operand_aliasing={{0}: (2, {}), {1}: (3, {})} | custom-call | flops 3221225472 | tf_op jit(solution)/shard_map/stem/pallas_call | solution.py:370
  15.3 2.6 %collective-permute-start.4 = (bf16[128,1024]{1,0:T(8,128)(2,1)S(1)}, bf16[128,1024]{1,0:T(8,128)(2,1)S(1)}, u32[]{:S(2)}, u32[]{:S(2)}) collective-permute-start(bf16[128,1024]{1,0:T(8,128)(2,1)S(1)} %get-tuple-element.32.mine), channel_id=1, source_target_pairs={{0,1},{1,0},{2,3},{3,2},{4,5},{5,4},{6,7},{7,6},{8,9},{9,8},{10,11... | collective-permute-start | bytes 786440 | tf_op jit(solution)/shard_map/ppermute | solution.py:515
  18.0 0.1 fusion
  18.1 0.1 pad_maximum_fusion.q
  18.2 0.9 %collective-permute-done.4.theirs = bf16[128,1024]{1,0:T(8,128)(2,1)S(1)} collective-permute-done((bf16[128,1024]{1,0:T(8,128)(2,1)S(1)}, bf16[128,1024]{1,0:T(8,128)(2,1)S(1)}, u32[]{:S(2)}, u32[]{:S(2)}) %collective-permute-start.4) | collective-permute-done | bytes 262176 | tf_op jit(solution)/shard_map/ppermute | solution.py:515
  19.1 1.3 %project.1.kv = bf16[256,2048]{1,0:T(8,128)(2,1)S(1)} custom-call(bf16[128,1024]{1,0:T(8,128)(2,1)S(1)} %get-tuple-element.32.mine, bf16[128,1024]{1,0:T(8,128)(2,1)S(1)} %collective-permute-done.4.theirs, bf16[1024,1024]{1,0:T(8,128)(2,1)S(1)} %get-tuple-element.33.wk, bf16[1024,1024]{1,0:T(8,128)(2,1)S(1)} %get-tuple-element.34.wv), custom_call_target="tpu_custom_call" | custom-call | flops 1073741824 | tf_op jit(solution)/shard_map/project/pallas_call | solution.py:370
  20.4 0.9 %attend.2 = bf16[128,1152]{1,0:T(8,128)(2,1)S(1)} custom-call(bf16[512,1024]{1,0:T(8,128)(2,1)S(1)} %pad_maximum_fusion.q, bf16[256,2048]{1,0:T(8,128)(2,1)S(1)} %project.1.kv), custom_call_target="tpu_custom_call" | custom-call | flops 1073741824 | tf_op jit(solution)/shard_map/attend/pallas_call | solution.py:370
  21.3 1.7 %collective-permute-start.5 = (bf16[128,1152]{1,0:T(8,128)(2,1)S(1)}, bf16[128,1152]{1,0:T(8,128)(2,1)S(1)}, u32[]{:S(2)}, u32[]{:S(2)}) collective-permute-start(bf16[128,1152]{1,0:T(8,128)(2,1)S(1)} %attend.2), channel_id=1, source_target_pairs={{0,2},{1,5},{2,0},{3,7},{4,6},{5,1},{6,4},{7,3},{8,10},{9,13},{10,... | collective-permute-start | bytes 884744 | tf_op jit(solution)/shard_map/ppermute | solution.py:422
  23.1 0.9 %attend.3.keep_ref = f32[128,1152]{1,0:T(8,128)S(1)} custom-call(bf16[512,1024]{1,0:T(8,128)(2,1)S(1)} %pad_maximum_fusion.q, bf16[256,2048]{1,0:T(8,128)(2,1)S(1)} %project.1.kv), custom_call_target="tpu_custom_call" | custom-call | flops 1073741824 | tf_op jit(solution)/shard_map/attend/pallas_call | solution.py:370
  23.9 4.2 %collective-permute-done.5.recv_ref = bf16[128,1152]{1,0:T(8,128)(2,1)S(1)} collective-permute-done((bf16[128,1152]{1,0:T(8,128)(2,1)S(1)}, bf16[128,1152]{1,0:T(8,128)(2,1)S(1)}, u32[]{:S(2)}, u32[]{:S(2)}) %collective-permute-start.5) | collective-permute-done | bytes 294944 | tf_op jit(solution)/shard_map/ppermute | solution.py:422
  28.1 0.3 merge.4
  28.5 4.1 %collective-permute-start.6 = (bf16[64,1152]{1,0:T(8,128)(2,1)S(1)}, bf16[64,1152]{1,0:T(8,128)(2,1)S(1)}, u32[]{:S(2)}, u32[]{:S(2)}) collective-permute-start(bf16[64,1152]{1,0:T(8,128)(2,1)S(1)} %get-tuple-element.38), channel_id=1, source_target_pairs={{0,4},{1,3},{2,6},{3,1},{4,0},{5,7},{6,2},{7,5},{8,12},{9,11},{10,... | collective-permute-start | bytes 442376 | tf_op jit(solution)/shard_map/ppermute | solution.py:422
  32.5 3.1 %collective-permute-done.6.recv_ref = bf16[64,1152]{1,0:T(8,128)(2,1)S(1)} collective-permute-done((bf16[64,1152]{1,0:T(8,128)(2,1)S(1)}, bf16[64,1152]{1,0:T(8,128)(2,1)S(1)}, u32[]{:S(2)}, u32[]{:S(2)}) %collective-permute-start.6) | collective-permute-done | bytes 147488 | tf_op jit(solution)/shard_map/ppermute | solution.py:422
  35.6 0.2 merge.5
  35.9 1.8 %collective-permute-start.7 = (bf16[32,1152]{1,0:T(8,128)(2,1)S(1)}, bf16[32,1152]{1,0:T(8,128)(2,1)S(1)}, u32[]{:S(2)}, u32[]{:S(2)}) collective-permute-start(bf16[32,1152]{1,0:T(8,128)(2,1)S(1)} %get-tuple-element.40), channel_id=1, source_target_pairs={{0,8},{1,9},{2,10},{3,11},{4,12},{5,13},{6,14},{7,15},{8,0},{9,1},... | collective-permute-start | bytes 221192 | tf_op jit(solution)/shard_map/ppermute | solution.py:422
  37.7 2.6 %collective-permute-done.7.recv_ref = bf16[32,1152]{1,0:T(8,128)(2,1)S(1)} collective-permute-done((bf16[32,1152]{1,0:T(8,128)(2,1)S(1)}, bf16[32,1152]{1,0:T(8,128)(2,1)S(1)}, u32[]{:S(2)}, u32[]{:S(2)}) %collective-permute-start.7) | collective-permute-done | bytes 73760 | tf_op jit(solution)/shard_map/ppermute | solution.py:422
  40.3 0.2 merge.6
  40.5 2.8 %collective-permute-start.8 = (bf16[16,1152]{1,0:T(8,128)(2,1)S(1)}, bf16[16,1152]{1,0:T(8,128)(2,1)S(1)}, u32[]{:S(2)}, u32[]{:S(2)}) collective-permute-start(bf16[16,1152]{1,0:T(8,128)(2,1)S(1)} %get-tuple-element.42), channel_id=1, source_target_pairs={{0,16},{1,17},{2,18},{3,19},{4,20},{5,21},{6,22},{7,23},{8,24},{9,... | collective-permute-start | bytes 110600 | tf_op jit(solution)/shard_map/ppermute | solution.py:422
  43.4 2.1 %collective-permute-done.8.recv_ref = bf16[16,1152]{1,0:T(8,128)(2,1)S(1)} collective-permute-done((bf16[16,1152]{1,0:T(8,128)(2,1)S(1)}, bf16[16,1152]{1,0:T(8,128)(2,1)S(1)}, u32[]{:S(2)}, u32[]{:S(2)}) %collective-permute-start.8) | collective-permute-done | bytes 36896 | tf_op jit(solution)/shard_map/ppermute | solution.py:422
  45.4 0.8 %merge.7 = bf16[16,1024]{1,0:T(8,128)(2,1)} custom-call(f32[16,1152]{1,0:T(8,128)S(1)} %get-tuple-element.41.keep_ref, bf16[16,1152]{1,0:T(8,128)(2,1)S(1)} %collective-permute-done.8.recv_ref), custom_call_target="tpu_custom_call" | custom-call | tf_op jit(solution)/shard_map/merge/pallas_call | solution.py:370
  (16 shorter events, 0.1 us)
Async XLA Ops:
  0.9 3.8 %collective-permute-start = (bf16[3,24,512]{2,1,0:T(8,128)(2,1)S(1)}, bf16[3,24,512]{2,1,0:T(8,128)(2,1)S(1)}, u32[]{:S(2)}, u32[]{:S(2)}) collective-permute-start(bf16[3,24,512]{2,1,0:T(8,128)(2,1)S(1)} %get-tuple-element.24), channel_id=1, source_target_pairs={{0,1},{1,0},{2,3},{3,2},{4,5},{5,4},{6,7},{7,6},{8,9},{9,8},{10,11... | collective-permute-start | bytes 221192 | tf_op jit(solution)/shard_map/ppermute | solution.py:461
  1.5 3.3 %collective-permute-start.1 = (bf16[3,24,512]{2,1,0:T(8,128)(2,1)S(1)}, bf16[3,24,512]{2,1,0:T(8,128)(2,1)S(1)}, u32[]{:S(2)}, u32[]{:S(2)}) collective-permute-start(bf16[3,24,512]{2,1,0:T(8,128)(2,1)S(1)} %get-tuple-element.25), channel_id=1, source_target_pairs={{1,2},{2,1},{5,6},{6,5},{9,10},{10,9},{13,14},{14,13},{17,18},{18,... | collective-permute-start | bytes 221192 | tf_op jit(solution)/shard_map/ppermute | solution.py:462
  3.0 1.1 %copy-start = (bf16[3,256,512]{2,1,0:T(8,128)(2,1)S(1)}, bf16[3,256,512]{2,1,0:T(8,128)(2,1)}, u32[]{:S(2)}) copy-start(bf16[3,256,512]{2,1,0:T(8,128)(2,1)} %slide.3) | copy-start | bytes 2359300
  4.9 6.8 %collective-permute-start.2 = (bf16[144,128]{1,0:T(8,128)(2,1)S(1)}, bf16[144,128]{1,0:T(8,128)(2,1)S(1)}, u32[]{:S(2)}, u32[]{:S(2)}) collective-permute-start(bf16[144,128]{1,0:T(8,128)(2,1)S(1)} %get-tuple-element.26), channel_id=1, source_target_pairs={{0,4},{4,0},{8,12},{12,8},{16,20},{20,16},{24,28},{28,24},{1,5},{5... | collective-permute-start | bytes 110600 | tf_op jit(solution)/shard_map/ppermute | solution.py:467
  7.5 4.2 %collective-permute-start.3 = (bf16[144,128]{1,0:T(8,128)(2,1)S(1)}, bf16[144,128]{1,0:T(8,128)(2,1)S(1)}, u32[]{:S(2)}, u32[]{:S(2)}) collective-permute-start(bf16[144,128]{1,0:T(8,128)(2,1)S(1)} %get-tuple-element.27), channel_id=1, source_target_pairs={{4,8},{8,4},{12,16},{16,12},{20,24},{24,20},{5,9},{9,5},{13,17},{1... | collective-permute-start | bytes 110600 | tf_op jit(solution)/shard_map/ppermute | solution.py:468
  8.2 3.5 %slice-start = ((s8[4718592]{0:T(1024)(128)(4,1)}), s8[4194304]{0:T(1024)(128)(4,1)S(1)}, s32[]{:S(2)}) async-start(s8[4718592]{0:T(1024)(128)(4,1)} %bitcast.15), calls=%async_computation | async-start | bytes 8388608
  8.2 3.5 %slice-start.1 = ((s8[4718592]{0:T(1024)(128)(4,1)}), s8[524288]{0:T(1024)(128)(4,1)S(1)}, s32[]{:S(2)}) async-start(s8[4718592]{0:T(1024)(128)(4,1)} %bitcast.15), calls=%async_computation.1 | async-start | bytes 1048576
  8.2 3.5 %copy-start.1 = (bf16[6,6,64,256]{3,2,1,0:T(8,128)(2,1)S(1)}, bf16[6,6,64,256]{3,2,1,0:T(8,128)(2,1)}, u32[]{:S(2)}) copy-start(bf16[6,6,64,256]{3,2,1,0:T(8,128)(2,1)} %param.9) | copy-start | bytes 3538948
  11.8 6.2 %copy-start.2 = (bf16[512,1024]{1,0:T(8,128)(2,1)S(1)}, bf16[512,1024]{1,0:T(8,128)(2,1)}, u32[]{:S(2)}) copy-start(bf16[512,1024]{1,0:T(8,128)(2,1)} %param.13) | copy-start | bytes 3145732
  15.3 3.8 %collective-permute-start.4 = (bf16[128,1024]{1,0:T(8,128)(2,1)S(1)}, bf16[128,1024]{1,0:T(8,128)(2,1)S(1)}, u32[]{:S(2)}, u32[]{:S(2)}) collective-permute-start(bf16[128,1024]{1,0:T(8,128)(2,1)S(1)} %get-tuple-element.32.mine), channel_id=1, source_target_pairs={{0,1},{1,0},{2,3},{3,2},{4,5},{5,4},{6,7},{7,6},{8,9},{9,8},{10,11... | collective-permute-start | bytes 786440 | tf_op jit(solution)/shard_map/ppermute | solution.py:515
  21.3 6.8 %collective-permute-start.5 = (bf16[128,1152]{1,0:T(8,128)(2,1)S(1)}, bf16[128,1152]{1,0:T(8,128)(2,1)S(1)}, u32[]{:S(2)}, u32[]{:S(2)}) collective-permute-start(bf16[128,1152]{1,0:T(8,128)(2,1)S(1)} %attend.2), channel_id=1, source_target_pairs={{0,2},{1,5},{2,0},{3,7},{4,6},{5,1},{6,4},{7,3},{8,10},{9,13},{10,... | collective-permute-start | bytes 884744 | tf_op jit(solution)/shard_map/ppermute | solution.py:422
  28.5 7.2 %collective-permute-start.6 = (bf16[64,1152]{1,0:T(8,128)(2,1)S(1)}, bf16[64,1152]{1,0:T(8,128)(2,1)S(1)}, u32[]{:S(2)}, u32[]{:S(2)}) collective-permute-start(bf16[64,1152]{1,0:T(8,128)(2,1)S(1)} %get-tuple-element.38), channel_id=1, source_target_pairs={{0,4},{1,3},{2,6},{3,1},{4,0},{5,7},{6,2},{7,5},{8,12},{9,11},{10,... | collective-permute-start | bytes 442376 | tf_op jit(solution)/shard_map/ppermute | solution.py:422
  35.9 4.4 %collective-permute-start.7 = (bf16[32,1152]{1,0:T(8,128)(2,1)S(1)}, bf16[32,1152]{1,0:T(8,128)(2,1)S(1)}, u32[]{:S(2)}, u32[]{:S(2)}) collective-permute-start(bf16[32,1152]{1,0:T(8,128)(2,1)S(1)} %get-tuple-element.40), channel_id=1, source_target_pairs={{0,8},{1,9},{2,10},{3,11},{4,12},{5,13},{6,14},{7,15},{8,0},{9,1},... | collective-permute-start | bytes 221192 | tf_op jit(solution)/shard_map/ppermute | solution.py:422
  40.5 4.9 %collective-permute-start.8 = (bf16[16,1152]{1,0:T(8,128)(2,1)S(1)}, bf16[16,1152]{1,0:T(8,128)(2,1)S(1)}, u32[]{:S(2)}, u32[]{:S(2)}) collective-permute-start(bf16[16,1152]{1,0:T(8,128)(2,1)S(1)} %get-tuple-element.42), channel_id=1, source_target_pairs={{0,16},{1,17},{2,18},{3,19},{4,20},{5,21},{6,22},{7,23},{8,24},{9,... | collective-permute-start | bytes 110600 | tf_op jit(solution)/shard_map/ppermute | solution.py:422

commit v4 on v3

--- a/solution.py
+++ b/solution.py
@@ -298,10 +298,17 @@
             kv[:, 1024 * i + 256 * n : 1024 * i + 256 * n + 256] = rows.astype(jnp.bfloat16)
 
 
-def attend_kernel(q, kv, out, *, bit_of, keep):
-    n = out.shape[0]
+def attend_kernel(q, kv, lead, lag, *, bit_of, chunk_of, keep):
+    half = lead.shape[0]
+    n = 2 * half
     quarter = 2 * (lax.axis_index("rows") % 2) + (bit_of() if keep else 1 - bit_of())
     rows = pl.ds(pl.multiple_of(quarter * n, n), n)
+    upper = chunk_of() == 1
+
+    def put(lanes, value):
+        lead[:, lanes] = jnp.where(upper, value[:half], value[half:]).astype(lead.dtype)
+        lag[:, lanes] = jnp.where(upper, value[half:], value[:half]).astype(lag.dtype)
+
     scale = 1.0 / math.sqrt(128)
     lane = lanes_of((n, 128))
     stat = jnp.zeros((n, 128), jnp.float32)
@@ -315,9 +322,9 @@
         w = jnp.exp(scores - peak)
         total = jnp.sum(w, axis=1, keepdims=True)
         o = jnp.dot(w.astype(jnp.bfloat16), kv[:, past], preferred_element_type=jnp.float32)
-        out[:, lanes] = (o * (1.0 / total)).astype(out.dtype)
+        put(lanes, o * (1.0 / total))
         stat = jnp.where(lane == h, peak + jnp.log(total), stat)
-    out[:, 1024:1152] = stat if keep else pack_stat(stat)
+    put(slice(1024, 1152), stat if keep else pack_stat(stat).astype(jnp.float32))
 
 
 def pack_stat(stat):
@@ -350,9 +357,11 @@
         a = keep_ref[:, lanes]
         b = recv_ref[:, lanes].astype(jnp.float32)
         merged.append(b + jnp.broadcast_to(share[:, h : h + 1], (n, 128)) * (a - b))
-    if bit_of is None:
+    if not callable(bit_of):
         for h in range(HEADS):
-            outs[0][:, 128 * h : 128 * h + 128] = merged[h].astype(jnp.bfloat16)
+            outs[0][:, 128 * h : 128 * h + 128] = merged[h].astype(outs[0].dtype)
+        if bit_of != "result":
+            outs[0][:, 1024:1152] = pack_stat(stat) if bit_of == "send" else stat
         return
     upper = bit_of() == 1
     half = n // 2
@@ -382,12 +391,14 @@
 
 def merge(keep, recv, bit_of):
     n, width = keep.shape
-    if bit_of is None:
+    if bit_of == "result":
         outs = (jax.ShapeDtypeStruct((n, 1024), jnp.bfloat16),)
+    elif not callable(bit_of):
+        outs = (VMEM((n, width), jnp.bfloat16 if bit_of == "send" else jnp.float32),)
     else:
         outs = (VMEM((n // 2, width), jnp.float32), VMEM((n // 2, width), jnp.bfloat16))
     out = call(functools.partial(merge_kernel, bit_of=bit_of), "merge", (keep, recv), outs, limit=8 << 20)
-    return out[0] if bit_of is None else out
+    return out if callable(bit_of) else out[0]
 
 
 def swap_pairs(size, odd):
@@ -442,7 +453,8 @@
         halves = []
         for core in range(2):
             part = lax.index_in_dim(split, core, at, keepdims=False)
-            axes = [rest.index(name) for name in orders[core]]
+            order = orders[core]
+            axes = [rest.index(name) for name in order[:1] + order[2:3] + order[1:2] + order[3:]]
             halves.append(part.transpose(axes + [len(rest), len(rest) + 1]).reshape(latents // 2, width))
         return jnp.concatenate(halves, axis=0)
 
@@ -523,27 +535,33 @@
             limit=8 << 20,
         )
         ordered = order_queries(queries)
-        quarter = queries.shape[0] // 4
+        eighth = queries.shape[0] // 8
         width = 1024 + STAT
 
-        def attend(q, keep, dtype):
+        def attend(q, keep):
+            shape = VMEM((eighth, width), f32 if keep else bf16)
             return call(
-                functools.partial(attend_kernel, bit_of=bit_of(0), keep=keep),
+                functools.partial(attend_kernel, bit_of=bit_of(0), chunk_of=bit_of(2), keep=keep),
                 "attend",
                 (q, kv),
-                (VMEM((quarter, width), dtype),),
+                (shape, shape),
                 flops=1 << 30,
                 limit=8 << 20,
-            )[0]
-
-        send = attend(ordered, False, bf16)
-        ordered, send = lax.optimization_barrier((ordered, send))
-        recv = exchange(send, 0)
-        keep = attend(ordered, True, f32)
-        for stage in range(1, len(orders[0])):
+            )
+
+        sends = attend(ordered, False)
+        ordered, lead, lag = lax.optimization_barrier((ordered, *sends))
+        recvs = [exchange(lead, 0), exchange(lag, 0)]
+        keeps = list(attend(ordered, True))
+        for i in range(2):
+            keeps[i], send = merge(keeps[i], recvs[i], bit_of(1))
+            recvs[i] = exchange(send, 1)
+        recv = exchange(merge(keeps[0], recvs[0], "send"), 2)
+        keep = merge(keeps[1], recvs[1], "keep")
+        for stage in range(3, len(orders[0])):
             keep, send = merge(keep, recv, bit_of(stage))
             recv = exchange(send, stage)
-        return merge(keep, recv, None)
+        return merge(keep, recv, "result")
 
     placed = (P(None, "rows", "cols"), P(), P(), P(), P(), P(), P())
     return jax.shard_map(

time: 46.5 us -> 44 us (0.946)
  waiting for transfers between devices: 12.9 us -> 8.04 us
  starting transfers between devices: 17.5 us -> 19.5 us
    ppermute x4 -> x6, waiting for transfers between devices: 12 us -> 7.12 us  [exchange(): return lax.ppermute(value, ('cols', 'rows'), pairs)]
    ppermute x4 -> x6, starting transfers between devices: 10.4 us -> 12.5 us  [exchange(): return lax.ppermute(value, ('cols', 'rows'), pairs)]
    pallas_call x13 -> x15, Pallas kernels: 14.1 us -> 14.5 us  [call(): pl.pallas_call(kernel, in_specs=[far_spec if i in far else spec for i in...]
  transfers between devices with their start and end apart: 9 -> 11, of which waited for: 5 -> 6; matrix products, arithmetic and copies ran while one was open for 2% -> 3% of each run, Pallas kernels for 12% -> 15%
where the time goes in v4:
time: 44 us; the launch traced here: 43.8 us
  starting transfers between devices  19.5 us (44%)
  Pallas kernels  14.5 us (33%)
  waiting for transfers between devices  8.04 us (18%)
  local copies, waits for them, and re-layouts  1.29 us (3%)
    pallas_call x15, Pallas kernels, call(): pl.pallas_call(kernel, in_specs=[far_spec if i in far else spec for i in...  14.5 us
    ppermute x6, starting transfers between devices, exchange(): return lax.ppermute(value, ('cols', 'rows'), pairs)  12.5 us
    ppermute x6, waiting for transfers between devices, exchange(): return lax.ppermute(value, ('cols', 'rows'), pairs)  7.12 us
    ppermute x1, starting transfers between devices, on_device(): normed_other = lax.ppermute(normed, 'rows', swap_pairs(n_rows, False))  2.64 us
    ppermute x1, starting transfers between devices, on_device(): col_a = lax.ppermute(col_a, 'cols', swap_pairs(n_cols, False))  2.58 us
    ppermute x1, waiting for transfers between devices, on_device(): normed_other = lax.ppermute(normed, 'rows', swap_pairs(n_rows, False))  0.91 us
  transfers between devices with their start and end apart: 11, of which 6 were waited for; matrix products, arithmetic and copies ran while one was open for 3% of the time, Pallas kernels for 15%

profile of v4, /device:TPU:0, one launch (start us, length us, event | category | flops | bytes accessed | tf_op | source)
XLA Modules:
  0.0 43.8 jit_solution(2170413481761710634)
XLA Ops:
  0.0 0.9 %row_edges.1 = (bf16[3,24,512]{2,1,0:T(8,128)(2,1)S(1)}, bf16[3,24,512]{2,1,0:T(8,128)(2,1)S(1)}) custom-call(bf16[3,256,512]{2,1,0:T(8,128)(2,1)} %slide.3), custom_call_target="tpu_custom_call" | custom-call | tf_op jit(solution)/shard_map/row_edges/pallas_call | solution.py:379
  0.9 0.5 %collective-permute-start = (bf16[3,24,512]{2,1,0:T(8,128)(2,1)S(1)}, bf16[3,24,512]{2,1,0:T(8,128)(2,1)S(1)}, u32[]{:S(2)}, u32[]{:S(2)}) collective-permute-start(bf16[3,24,512]{2,1,0:T(8,128)(2,1)S(1)} %get-tuple-element.29), channel_id=1, source_target_pairs={{0,1},{1,0},{2,3},{3,2},{4,5},{5,4},{6,7},{7,6},{8,9},{9,8},{10,11... | collective-permute-start | bytes 221192 | tf_op jit(solution)/shard_map/ppermute | solution.py:473
  1.5 0.7 %collective-permute-start.1 = (bf16[3,24,512]{2,1,0:T(8,128)(2,1)S(1)}, bf16[3,24,512]{2,1,0:T(8,128)(2,1)S(1)}, u32[]{:S(2)}, u32[]{:S(2)}) collective-permute-start(bf16[3,24,512]{2,1,0:T(8,128)(2,1)S(1)} %get-tuple-element.30), channel_id=1, source_target_pairs={{1,2},{2,1},{5,6},{6,5},{9,10},{10,9},{13,14},{14,13},{17,18},{18,... | collective-permute-start | bytes 221192 | tf_op jit(solution)/shard_map/ppermute | solution.py:474
  2.1 0.8 %copy.14 = bf16[3,6,6,64]{3,2,1,0:T(8,128)(2,1)S(1)} copy(bf16[3,6,6,64]{3,0,2,1:T(4,128)(2,1)} %bitcast.23) | data formatting | bytes 27648 | tf_op jit(solution)/shard_map/transpose | solution.py:482
  3.0 0.8 %band.1.toep = bf16[2304,1792]{1,0:T(8,128)(2,1)S(1)} custom-call(bf16[18,48,128]{2,1,0:T(8,128)(2,1)S(1)} %pad_add_fusion.taps_ref), custom_call_target="tpu_custom_call" | custom-call | bytes 4194304 | tf_op jit(solution)/shard_map/band/pallas_call | solution.py:379
  3.8 0.3 copy-done
  4.2 0.6 %windows.1 = (f32[5,3,328,128]{3,2,1,0:T(8,128)S(1)}, bf16[368,2304]{1,0:T(8,128)(2,1)S(1)}) custom-call(bf16[3,256,512]{2,1,0:T(8,128)(2,1)S(1)} %copy-done), custom_call_target="tpu_custom_call" | custom-call | flops 268435456 | bytes 4194304 | tf_op jit(solution)/shard_map/windows/pallas_call | solution.py:379
  4.9 2.6 %collective-permute-start.2 = (bf16[144,128]{1,0:T(8,128)(2,1)S(1)}, bf16[144,128]{1,0:T(8,128)(2,1)S(1)}, u32[]{:S(2)}, u32[]{:S(2)}) collective-permute-start(bf16[144,128]{1,0:T(8,128)(2,1)S(1)} %get-tuple-element.31), channel_id=1, source_target_pairs={{0,4},{4,0},{8,12},{12,8},{16,20},{20,16},{24,28},{28,24},{1,5},{5... | collective-permute-start | bytes 110600 | tf_op jit(solution)/shard_map/ppermute | solution.py:479
  7.5 0.7 %collective-permute-start.3 = (bf16[144,128]{1,0:T(8,128)(2,1)S(1)}, bf16[144,128]{1,0:T(8,128)(2,1)S(1)}, u32[]{:S(2)}, u32[]{:S(2)}) collective-permute-start(bf16[144,128]{1,0:T(8,128)(2,1)S(1)} %get-tuple-element.32), channel_id=1, source_target_pairs={{4,8},{8,4},{12,16},{16,12},{20,24},{24,20},{5,9},{9,5},{13,17},{1... | collective-permute-start | bytes 110600 | tf_op jit(solution)/shard_map/ppermute | solution.py:480
  8.2 3.5 %inner.1 = (f32[5,3,328,128]{3,2,1,0:T(8,128)S(1)}, f32[5,14,104,128]{3,2,1,0:T(8,128)S(1)}, bf16[368,2304]{1,0:T(8,128)(2,1)S(1)}) custom-call(bf16[3,24,512]{2,1,0:T(8,128)(2,1)S(1)} %collective-permute-done.ra_ref, bf16[3,24,512]{2,1,0:T(8,128)(2,1)S(1)} %collective-permute-done.1.rb_ref, ...), custom_call_target="tpu_custom_call", output_to_operand_aliasing={{0}: (3, {}), {2}: (4, {})} | custom-call | flops 3038773248 | bytes 16777216 | tf_op jit(solution)/shard_map/inner/pallas_call | solution.py:379
  11.8 3.5 %stem.1 = (f32[5,3,328,128]{3,2,1,0:T(8,128)S(1)}, f32[5,14,104,128]{3,2,1,0:T(8,128)S(1)}, bf16[128,1024]{1,0:T(8,128)(2,1)S(1)}, bf16[1024,1024]{1,0:T(8,128)(2,1)S(1)}, bf16[1024,1024]{1,0:T(8,128)(2,1)S(1)}) custom-call(bf16[144,128]{1,0:T(8,128)(2,1)S(1)} %collective-permute-done.2.ca_ref, ...), custom_call_target="tpu_custom_call", output_to_operand_aliasing={{0}: (2, {}), {1}: (3, {})} | custom-call | flops 3221225472 | tf_op jit(solution)/shard_map/stem/pallas_call | solution.py:379
  15.3 2.6 %collective-permute-start.4 = (bf16[128,1024]{1,0:T(8,128)(2,1)S(1)}, bf16[128,1024]{1,0:T(8,128)(2,1)S(1)}, u32[]{:S(2)}, u32[]{:S(2)}) collective-permute-start(bf16[128,1024]{1,0:T(8,128)(2,1)S(1)} %get-tuple-element.37.mine), channel_id=1, source_target_pairs={{0,1},{1,0},{2,3},{3,2},{4,5},{5,4},{6,7},{7,6},{8,9},{9,8},{10,11... | collective-permute-start | bytes 786440 | tf_op jit(solution)/shard_map/ppermute | solution.py:527
  18.2 0.9 %collective-permute-done.4.theirs = bf16[128,1024]{1,0:T(8,128)(2,1)S(1)} collective-permute-done((bf16[128,1024]{1,0:T(8,128)(2,1)S(1)}, bf16[128,1024]{1,0:T(8,128)(2,1)S(1)}, u32[]{:S(2)}, u32[]{:S(2)}) %collective-permute-start.4) | collective-permute-done | bytes 262176 | tf_op jit(solution)/shard_map/ppermute | solution.py:527
  19.1 1.3 %project.1.kv = bf16[256,2048]{1,0:T(8,128)(2,1)S(1)} custom-call(bf16[128,1024]{1,0:T(8,128)(2,1)S(1)} %get-tuple-element.37.mine, bf16[128,1024]{1,0:T(8,128)(2,1)S(1)} %collective-permute-done.4.theirs, bf16[1024,1024]{1,0:T(8,128)(2,1)S(1)} %get-tuple-element.38.wk, bf16[1024,1024]{1,0:T(8,128)(2,1)S(1)} %get-tuple-element.39.wv), custom_call_target="tpu_custom_call" | custom-call | flops 1073741824 | tf_op jit(solution)/shard_map/project/pallas_call | solution.py:379
  20.4 0.9 %attend.2 = (bf16[64,1152]{1,0:T(8,128)(2,1)S(1)}, bf16[64,1152]{1,0:T(8,128)(2,1)S(1)}) custom-call(bf16[512,1024]{1,0:T(8,128)(2,1)S(1)} %pad_maximum_fusion.q, bf16[256,2048]{1,0:T(8,128)(2,1)S(1)} %project.1.kv), custom_call_target="tpu_custom_call" | custom-call | flops 1073741824 | tf_op jit(solution)/shard_map/attend/pallas_call | solution.py:379
  21.4 1.7 %collective-permute-start.7 = (bf16[64,1152]{1,0:T(8,128)(2,1)S(1)}, bf16[64,1152]{1,0:T(8,128)(2,1)S(1)}, u32[]{:S(2)}, u32[]{:S(2)}) collective-permute-start(bf16[64,1152]{1,0:T(8,128)(2,1)S(1)} %get-tuple-element.48), channel_id=1, source_target_pairs={{0,2},{1,5},{2,0},{3,7},{4,6},{5,1},{6,4},{7,3},{8,10},{9,13},{10,... | collective-permute-start | bytes 442376 | tf_op jit(solution)/shard_map/ppermute | solution.py:433
  23.1 0.4 collective-permute-start.5
  23.4 0.9 %attend.3 = (f32[64,1152]{1,0:T(8,128)S(1)}, f32[64,1152]{1,0:T(8,128)S(1)}) custom-call(bf16[512,1024]{1,0:T(8,128)(2,1)S(1)} %pad_maximum_fusion.q, bf16[256,2048]{1,0:T(8,128)(2,1)S(1)} %project.1.kv), custom_call_target="tpu_custom_call" | custom-call | flops 1073741824 | tf_op jit(solution)/shard_map/attend/pallas_call | solution.py:379
  24.3 2.2 %collective-permute-done.7.recv_ref = bf16[64,1152]{1,0:T(8,128)(2,1)S(1)} collective-permute-done((bf16[64,1152]{1,0:T(8,128)(2,1)S(1)}, bf16[64,1152]{1,0:T(8,128)(2,1)S(1)}, u32[]{:S(2)}, u32[]{:S(2)}) %collective-permute-start.7) | collective-permute-done | bytes 147488 | tf_op jit(solution)/shard_map/ppermute | solution.py:433
  26.6 0.2 merge.8
  26.8 4.1 %collective-permute-start.8 = (bf16[32,1152]{1,0:T(8,128)(2,1)S(1)}, bf16[32,1152]{1,0:T(8,128)(2,1)S(1)}, u32[]{:S(2)}, u32[]{:S(2)}) collective-permute-start(bf16[32,1152]{1,0:T(8,128)(2,1)S(1)} %get-tuple-element.50), channel_id=1, source_target_pairs={{0,4},{1,3},{2,6},{3,1},{4,0},{5,7},{6,2},{7,5},{8,12},{9,11},{10,... | collective-permute-start | bytes 221192 | tf_op jit(solution)/shard_map/ppermute | solution.py:433
  30.9 0.2 merge.6
  31.1 1.7 %collective-permute-start.6 = (bf16[32,1152]{1,0:T(8,128)(2,1)S(1)}, bf16[32,1152]{1,0:T(8,128)(2,1)S(1)}, u32[]{:S(2)}, u32[]{:S(2)}) collective-permute-start(bf16[32,1152]{1,0:T(8,128)(2,1)S(1)} %get-tuple-element.46), channel_id=1, source_target_pairs={{0,4},{1,3},{2,6},{3,1},{4,0},{5,7},{6,2},{7,5},{8,12},{9,11},{10,... | collective-permute-start | bytes 221192 | tf_op jit(solution)/shard_map/ppermute | solution.py:433
  32.8 0.4 collective-permute-done.8.recv_ref
  33.2 0.2 merge.9
  33.4 1.8 %collective-permute-start.9 = (bf16[32,1152]{1,0:T(8,128)(2,1)S(1)}, bf16[32,1152]{1,0:T(8,128)(2,1)S(1)}, u32[]{:S(2)}, u32[]{:S(2)}) collective-permute-start(bf16[32,1152]{1,0:T(8,128)(2,1)S(1)} %merge.9), channel_id=1, source_target_pairs={{0,8},{1,9},{2,10},{3,11},{4,12},{5,13},{6,14},{7,15},{8,0},{9,1},... | collective-permute-start | bytes 221192 | tf_op jit(solution)/shard_map/ppermute | solution.py:433
  35.2 0.3 collective-permute-done.6.recv_ref
  35.7 2.1 %collective-permute-done.9.recv_ref = bf16[32,1152]{1,0:T(8,128)(2,1)S(1)} collective-permute-done((bf16[32,1152]{1,0:T(8,128)(2,1)S(1)}, bf16[32,1152]{1,0:T(8,128)(2,1)S(1)}, u32[]{:S(2)}, u32[]{:S(2)}) %collective-permute-start.9) | collective-permute-done | bytes 73760 | tf_op jit(solution)/shard_map/ppermute | solution.py:433
  37.8 0.2 merge.10
  38.0 2.8 %collective-permute-start.10 = (bf16[16,1152]{1,0:T(8,128)(2,1)S(1)}, bf16[16,1152]{1,0:T(8,128)(2,1)S(1)}, u32[]{:S(2)}, u32[]{:S(2)}) collective-permute-start(bf16[16,1152]{1,0:T(8,128)(2,1)S(1)} %get-tuple-element.52), channel_id=1, source_target_pairs={{0,16},{1,17},{2,18},{3,19},{4,20},{5,21},{6,22},{7,23},{8,24},{9,... | collective-permute-start | bytes 110600 | tf_op jit(solution)/shard_map/ppermute | solution.py:433
  40.9 2.1 %collective-permute-done.10.recv_ref = bf16[16,1152]{1,0:T(8,128)(2,1)S(1)} collective-permute-done((bf16[16,1152]{1,0:T(8,128)(2,1)S(1)}, bf16[16,1152]{1,0:T(8,128)(2,1)S(1)}, u32[]{:S(2)}, u32[]{:S(2)}) %collective-permute-start.10) | collective-permute-done | bytes 36896 | tf_op jit(solution)/shard_map/ppermute | solution.py:433
  43.0 0.8 %merge.11 = bf16[16,1024]{1,0:T(8,128)(2,1)} custom-call(f32[16,1152]{1,0:T(8,128)S(1)} %get-tuple-element.51.keep_ref, bf16[16,1152]{1,0:T(8,128)(2,1)S(1)} %collective-permute-done.10.recv_ref), custom_call_target="tpu_custom_call" | custom-call | tf_op jit(solution)/shard_map/merge/pallas_call | solution.py:379
  (22 shorter events, 0.8 us)
Async XLA Ops:
  0.9 3.8 %collective-permute-start = (bf16[3,24,512]{2,1,0:T(8,128)(2,1)S(1)}, bf16[3,24,512]{2,1,0:T(8,128)(2,1)S(1)}, u32[]{:S(2)}, u32[]{:S(2)}) collective-permute-start(bf16[3,24,512]{2,1,0:T(8,128)(2,1)S(1)} %get-tuple-element.29), channel_id=1, source_target_pairs={{0,1},{1,0},{2,3},{3,2},{4,5},{5,4},{6,7},{7,6},{8,9},{9,8},{10,11... | collective-permute-start | bytes 221192 | tf_op jit(solution)/shard_map/ppermute | solution.py:473
  1.5 3.3 %collective-permute-start.1 = (bf16[3,24,512]{2,1,0:T(8,128)(2,1)S(1)}, bf16[3,24,512]{2,1,0:T(8,128)(2,1)S(1)}, u32[]{:S(2)}, u32[]{:S(2)}) collective-permute-start(bf16[3,24,512]{2,1,0:T(8,128)(2,1)S(1)} %get-tuple-element.30), channel_id=1, source_target_pairs={{1,2},{2,1},{5,6},{6,5},{9,10},{10,9},{13,14},{14,13},{17,18},{18,... | collective-permute-start | bytes 221192 | tf_op jit(solution)/shard_map/ppermute | solution.py:474
  3.0 1.1 %copy-start = (bf16[3,256,512]{2,1,0:T(8,128)(2,1)S(1)}, bf16[3,256,512]{2,1,0:T(8,128)(2,1)}, u32[]{:S(2)}) copy-start(bf16[3,256,512]{2,1,0:T(8,128)(2,1)} %slide.3) | copy-start | bytes 2359300
  4.9 6.8 %collective-permute-start.2 = (bf16[144,128]{1,0:T(8,128)(2,1)S(1)}, bf16[144,128]{1,0:T(8,128)(2,1)S(1)}, u32[]{:S(2)}, u32[]{:S(2)}) collective-permute-start(bf16[144,128]{1,0:T(8,128)(2,1)S(1)} %get-tuple-element.31), channel_id=1, source_target_pairs={{0,4},{4,0},{8,12},{12,8},{16,20},{20,16},{24,28},{28,24},{1,5},{5... | collective-permute-start | bytes 110600 | tf_op jit(solution)/shard_map/ppermute | solution.py:479
  7.5 4.2 %collective-permute-start.3 = (bf16[144,128]{1,0:T(8,128)(2,1)S(1)}, bf16[144,128]{1,0:T(8,128)(2,1)S(1)}, u32[]{:S(2)}, u32[]{:S(2)}) collective-permute-start(bf16[144,128]{1,0:T(8,128)(2,1)S(1)} %get-tuple-element.32), channel_id=1, source_target_pairs={{4,8},{8,4},{12,16},{16,12},{20,24},{24,20},{5,9},{9,5},{13,17},{1... | collective-permute-start | bytes 110600 | tf_op jit(solution)/shard_map/ppermute | solution.py:480
  8.2 3.5 %slice-start = ((s8[4718592]{0:T(1024)(128)(4,1)}), s8[4194304]{0:T(1024)(128)(4,1)S(1)}, s32[]{:S(2)}) async-start(s8[4718592]{0:T(1024)(128)(4,1)} %bitcast.15), calls=%async_computation | async-start | bytes 8388608
  8.2 3.5 %slice-start.1 = ((s8[4718592]{0:T(1024)(128)(4,1)}), s8[524288]{0:T(1024)(128)(4,1)S(1)}, s32[]{:S(2)}) async-start(s8[4718592]{0:T(1024)(128)(4,1)} %bitcast.15), calls=%async_computation.1 | async-start | bytes 1048576
  8.2 3.5 %copy-start.1 = (bf16[6,6,64,256]{3,2,1,0:T(8,128)(2,1)S(1)}, bf16[6,6,64,256]{3,2,1,0:T(8,128)(2,1)}, u32[]{:S(2)}) copy-start(bf16[6,6,64,256]{3,2,1,0:T(8,128)(2,1)} %param.9) | copy-start | bytes 3538948
  11.8 6.2 %copy-start.2 = (bf16[512,1024]{1,0:T(8,128)(2,1)S(1)}, bf16[512,1024]{1,0:T(8,128)(2,1)}, u32[]{:S(2)}) copy-start(bf16[512,1024]{1,0:T(8,128)(2,1)} %param.13) | copy-start | bytes 3145732
  15.3 3.8 %collective-permute-start.4 = (bf16[128,1024]{1,0:T(8,128)(2,1)S(1)}, bf16[128,1024]{1,0:T(8,128)(2,1)S(1)}, u32[]{:S(2)}, u32[]{:S(2)}) collective-permute-start(bf16[128,1024]{1,0:T(8,128)(2,1)S(1)} %get-tuple-element.37.mine), channel_id=1, source_target_pairs={{0,1},{1,0},{2,3},{3,2},{4,5},{5,4},{6,7},{7,6},{8,9},{9,8},{10,11... | collective-permute-start | bytes 786440 | tf_op jit(solution)/shard_map/ppermute | solution.py:527
  21.4 5.2 %collective-permute-start.7 = (bf16[64,1152]{1,0:T(8,128)(2,1)S(1)}, bf16[64,1152]{1,0:T(8,128)(2,1)S(1)}, u32[]{:S(2)}, u32[]{:S(2)}) collective-permute-start(bf16[64,1152]{1,0:T(8,128)(2,1)S(1)} %get-tuple-element.48), channel_id=1, source_target_pairs={{0,2},{1,5},{2,0},{3,7},{4,6},{5,1},{6,4},{7,3},{8,10},{9,13},{10,... | collective-permute-start | bytes 442376 | tf_op jit(solution)/shard_map/ppermute | solution.py:433
  23.1 7.8 %collective-permute-start.5 = (bf16[64,1152]{1,0:T(8,128)(2,1)S(1)}, bf16[64,1152]{1,0:T(8,128)(2,1)S(1)}, u32[]{:S(2)}, u32[]{:S(2)}) collective-permute-start(bf16[64,1152]{1,0:T(8,128)(2,1)S(1)} %get-tuple-element.44), channel_id=1, source_target_pairs={{0,2},{1,5},{2,0},{3,7},{4,6},{5,1},{6,4},{7,3},{8,10},{9,13},{10,... | collective-permute-start | bytes 442376 | tf_op jit(solution)/shard_map/ppermute | solution.py:433
  26.8 6.4 %collective-permute-start.8 = (bf16[32,1152]{1,0:T(8,128)(2,1)S(1)}, bf16[32,1152]{1,0:T(8,128)(2,1)S(1)}, u32[]{:S(2)}, u32[]{:S(2)}) collective-permute-start(bf16[32,1152]{1,0:T(8,128)(2,1)S(1)} %get-tuple-element.50), channel_id=1, source_target_pairs={{0,4},{1,3},{2,6},{3,1},{4,0},{5,7},{6,2},{7,5},{8,12},{9,11},{10,... | collective-permute-start | bytes 221192 | tf_op jit(solution)/shard_map/ppermute | solution.py:433
  31.1 4.4 %collective-permute-start.6 = (bf16[32,1152]{1,0:T(8,128)(2,1)S(1)}, bf16[32,1152]{1,0:T(8,128)(2,1)S(1)}, u32[]{:S(2)}, u32[]{:S(2)}) collective-permute-start(bf16[32,1152]{1,0:T(8,128)(2,1)S(1)} %get-tuple-element.46), channel_id=1, source_target_pairs={{0,4},{1,3},{2,6},{3,1},{4,0},{5,7},{6,2},{7,5},{8,12},{9,11},{10,... | collective-permute-start | bytes 221192 | tf_op jit(solution)/shard_map/ppermute | solution.py:433
  33.4 4.4 %collective-permute-start.9 = (bf16[32,1152]{1,0:T(8,128)(2,1)S(1)}, bf16[32,1152]{1,0:T(8,128)(2,1)S(1)}, u32[]{:S(2)}, u32[]{:S(2)}) collective-permute-start(bf16[32,1152]{1,0:T(8,128)(2,1)S(1)} %merge.9), channel_id=1, source_target_pairs={{0,8},{1,9},{2,10},{3,11},{4,12},{5,13},{6,14},{7,15},{8,0},{9,1},... | collective-permute-start | bytes 221192 | tf_op jit(solution)/shard_map/ppermute | solution.py:433
  38.0 4.9 %collective-permute-start.10 = (bf16[16,1152]{1,0:T(8,128)(2,1)S(1)}, bf16[16,1152]{1,0:T(8,128)(2,1)S(1)}, u32[]{:S(2)}, u32[]{:S(2)}) collective-permute-start(bf16[16,1152]{1,0:T(8,128)(2,1)S(1)} %get-tuple-element.52), channel_id=1, source_target_pairs={{0,16},{1,17},{2,18},{3,19},{4,20},{5,21},{6,22},{7,23},{8,24},{9,... | collective-permute-start | bytes 110600 | tf_op jit(solution)/shard_map/ppermute | solution.py:433

commit v5 on v4

--- a/solution.py
+++ b/solution.py
@@ -14,13 +14,15 @@
 BLOCK_COLS = 28
 BLOCKS = 5
 BLOCK_LANES = BLOCK_COLS * 64
+HALF_LANES = BLOCK_LANES // 2
+DEPTH1 = TAPS1 * 64
 ROWS1 = 80
 ROWS2 = 24
 COLS2 = 34
 STAT = 128
 RIM = 24
 EDGE, MID = 16, 48
-ROWS_ALL = (MID + EDGE) * 5 + 48
+MID_ALL, EDGE_ALL = MID * 5, EDGE * 5 + 48
 STRIP = 144
 VMEM = pltpu.MemorySpace.VMEM
 
@@ -35,7 +37,9 @@
     return lax.broadcasted_iota(jnp.int32, shape, len(shape) - 1)
 
 
-def row_edges_kernel(slide_hbm, a_ref, b_ref, sems):
+def row_edges_kernel(slide_hbm, kernel_far, a_ref, b_ref, kernel, sems):
+    extra = pltpu.make_async_copy(kernel_far, kernel, sems.at[2])
+    extra.start()
     even = lax.axis_index("rows") % 2 == 0
     height = slide_hbm.shape[1]
 
@@ -56,6 +60,8 @@
     @pl.when(jnp.logical_not(even))
     def _():
         send(b_ref, a_ref)
+
+    extra.wait()
 
 
 def rims(c, ra_ref, rb_ref, lanes):
@@ -86,99 +92,167 @@
     b_ref[...] = jnp.where(even, first, last).astype(jnp.bfloat16)
 
 
-def band_kernel(taps_ref, toep):
+def band_kernel(kernel_ref, toep, taps):
+    taps[...] = jnp.zeros(taps.shape, jnp.float32)
+    for kh in range(6):
+        for kw in range(6):
+            rows = kernel_ref[kh, kw].astype(jnp.float32)
+            for c in range(3):
+                for top, side in ((0, 0), (4, 1), (24, 0), (28, 1)):
+                    taps[6 * c + kh, top + kw : top + kw + 1, 64 * side : 64 * side + 64] = rows[c : c + 1]
+
     def band(k, carry):
-        base = pl.multiple_of(k * 128, 128)
-        toep[pl.ds(base, 128), :] = jnp.zeros((128, BLOCK_LANES), jnp.bfloat16)
-        p0 = taps_ref[k, 0:16, :]
-        p1 = taps_ref[k, 16:32, :]
-        p2 = taps_ref[k, 32:48, :]
-        for m in range(BLOCK_LANES // 256):
-            toep[pl.ds(base + 16 * m, 16), 256 * m : 256 * m + 128] = p0
-            toep[pl.ds(base + 16 * m, 16), 256 * m + 128 : 256 * m + 256] = p1
-            toep[pl.ds(base + 16 * m + 16, 16), 256 * m + 128 : 256 * m + 256] = p2
+        channel, kh = k // 6, k % 6
+        base = pl.multiple_of((3 * channel + kh % 3) * 128 + (kh // 3) * 64, 64)
+        toep[pl.ds(base, 64), :] = jnp.zeros((64, HALF_LANES), jnp.bfloat16)
+        p0 = taps[k, 0:16, :].astype(jnp.bfloat16)
+        p1 = taps[k, 16:32, :].astype(jnp.bfloat16)
+        p2 = taps[k, 32:48, :].astype(jnp.bfloat16)
+        for m in range(HALF_LANES // 128):
+            lanes = slice(128 * m, 128 * m + 128)
+            if m % 2 == 0:
+                toep[pl.ds(base + 8 * m, 16), lanes] = p0
+            else:
+                toep[pl.ds(base + 8 * m - 8, 16), lanes] = p1
+                toep[pl.ds(base + 8 * m + 8, 16), lanes] = p2
         return carry
 
     lax.fori_loop(0, TAPS1, band, 0)
 
 
-def picks(first):
+def picks(blocks, start):
     lane = lax.broadcasted_iota(jnp.int32, (256, 128), 1)
-    source = lax.broadcasted_iota(jnp.int32, (256, 128), 0)
+    source = lax.broadcasted_iota(jnp.int32, (256, 128), 0) + (start + BEFORE)
     out = []
-    for b, start in zip(range(BLOCKS), (0, 0, 128, 256, 256)):
-        if b in first:
-            hit = source + start == lane + (4 * BLOCK_COLS * b - BEFORE)
-            out.append(jnp.where(hit, 1.0, 0.0).astype(jnp.bfloat16))
+    for b in blocks:
+        at = 4 * BLOCK_COLS * b
+        for low, high in ((0, 56), (56, 0)):
+            want = jnp.where(lane < 64, lane + (at + low), lane + (at + high - 64))
+            out.append(jnp.where(source == want, 1.0, 0.0).astype(jnp.bfloat16))
     return jnp.concatenate(out, axis=1)
 
 
 def cut(rows):
     parts = []
     for blocks, start in (((0, 1), 0), ((2,), 128), ((3, 4), 256)):
-        moved = jnp.dot(rows[:, start : start + 256], picks(blocks), preferred_element_type=jnp.float32)
-        parts += [moved[:, 128 * i : 128 * i + 128] for i in range(len(blocks))]
+        moved = jnp.dot(rows[:, start : start + 256], picks(blocks, start), preferred_element_type=jnp.float32)
+        parts += [
+            (moved[:, 256 * i : 256 * i + 128], moved[:, 256 * i + 128 : 256 * i + 256]) for i in range(len(blocks))
+        ]
     return parts
 
 
-def window_kernel(slide, xb, lhs1):
+def patches(xb, b, half, c, pair, start, count):
+    low = lanes_of((count, 128)) < 64
+    first = xb[half, b, c, pl.ds(RIM - BEFORE + start + pair, count, stride=4), :]
+    second = xb[1 - half, b, c, pl.ds(RIM - BEFORE + start + pair + 3, count, stride=4), :]
+    return jnp.where(low, first, second)
+
+
+def window_kernel(slide, toep, xb, fmap, lhs1):
     for c in range(3):
         for b, part in enumerate(cut(slide[c])):
-            xb[b, c, RIM : RIM + 256, :] = part
-    for b in range(BLOCKS):
-        for c in range(3):
-            for kh in range(6):
-                k = 6 * c + kh
-                lhs1[MID * b : MID * b + MID, 128 * k : 128 * k + 128] = xb[
-                    b, c, pl.ds(RIM - BEFORE + kh + 4 * EDGE, MID, stride=4), :
-                ].astype(jnp.bfloat16)
-
-
-def patch_rows(ref, at, lhs1, slot):
-    for c in range(3):
-        for kh in range(6):
-            k = 6 * c + kh
-            lhs1[ROWS1 * slot : ROWS1 * slot + ROWS1, 128 * k : 128 * k + 128] = ref[
-                at, c, pl.ds(RIM - BEFORE + kh, ROWS1, stride=4), :
-            ].astype(jnp.bfloat16)
-
-
-def inner_kernel(ra_ref, rb_ref, toep, xb_in, lhs1_in, xb, fmap, lhs1):
+            for order in range(2):
+                xb[order, b, c, RIM : RIM + 256, :] = part[order]
+    for half in range(2):
+        for b in range(BLOCKS):
+            row0 = MID_ALL * half + MID * b
+            for k in range(9):
+                lhs1[row0 : row0 + MID, 128 * k : 128 * k + 128] = patches(
+                    xb, b, half, k // 3, k % 3, 4 * EDGE, MID
+                ).astype(jnp.bfloat16)
+    for start in range(0, HALF_LANES, 256):
+        size = min(256, HALF_LANES - start)
+        acc = gelu(jnp.dot(lhs1[...], toep[:, start : start + size], preferred_element_type=jnp.float32))
+        for half in range(2):
+            for b in range(BLOCKS):
+                row0 = MID_ALL * half + MID * b
+                for u in range(size // 128):
+                    tile = (HALF_LANES * half + start) // 128 + u
+                    fmap[b, tile, EDGE : EDGE + MID, :] = acc[row0 : row0 + MID, 128 * u : 128 * u + 128]
+
+
+def inner_kernel(ra_ref, rb_ref, toep, xb_in, fmap_in, xb, fmap, lhs1, *, row_last):
     outer = []
     for c in range(3):
         outer += rims(c, ra_ref, rb_ref, slice(None))
     parts = cut(jnp.concatenate(outer, axis=0).astype(jnp.bfloat16))
     for b in range(BLOCKS):
         for c in range(3):
-            xb[b, c, 0:RIM, :] = parts[b][32 * c : 32 * c + RIM]
-            xb[b, c, 280:288, :] = parts[b][32 * c + RIM : 32 * c + 32]
-            xb[b, c, 288:328, :] = jnp.zeros((40, 128), jnp.float32)
-    top, bottom = MID * BLOCKS, (MID + EDGE) * BLOCKS
-    for c in range(3):
-        for kh in range(6):
-            lanes = slice(128 * (6 * c + kh), 128 * (6 * c + kh) + 128)
+            for order in range(2):
+                xb[order, b, c, 0:RIM, :] = parts[b][order][32 * c : 32 * c + RIM]
+                xb[order, b, c, 280:288, :] = parts[b][order][32 * c + RIM : 32 * c + 32]
+                xb[order, b, c, 288:328, :] = jnp.zeros((40, 128), jnp.float32)
+    for half in range(2):
+        top = EDGE_ALL * half
+        bottom = top + EDGE * BLOCKS
+        for k in range(9):
+            lanes = slice(128 * k, 128 * k + 128)
             low = []
             for b in range(BLOCKS):
-                lhs1[top + EDGE * b : top + EDGE * b + EDGE, lanes] = xb[
-                    b, c, pl.ds(RIM - BEFORE + kh, EDGE, stride=4), :
-                ].astype(jnp.bfloat16)
-                low.append(xb[b, c, pl.ds(RIM - BEFORE + kh + 4 * (EDGE + MID), 8, stride=4), :])
+                lhs1[top + EDGE * b : top + EDGE * b + EDGE, lanes] = patches(
+                    xb, b, half, k // 3, k % 3, 0, EDGE
+                ).astype(jnp.bfloat16)
+                low.append(patches(xb, b, half, k // 3, k % 3, 4 * (EDGE + MID), 8))
             low.append(jnp.zeros((8, 128), jnp.float32))
             lhs1[bottom : bottom + 48, lanes] = jnp.concatenate(low, axis=0).astype(jnp.bfloat16)
-    for n in range(BLOCK_LANES // 256):
-        acc = gelu(jnp.dot(lhs1[...], toep[:, 256 * n : 256 * n + 256], preferred_element_type=jnp.float32))
-        for b in range(BLOCKS):
+    for start in range(0, HALF_LANES, 256):
+        size = min(256, HALF_LANES - start)
+        acc = gelu(jnp.dot(lhs1[...], toep[:, start : start + size], preferred_element_type=jnp.float32))
+        for half in range(2):
+            top = EDGE_ALL * half
+            bottom = top + EDGE * BLOCKS
+            for b in range(BLOCKS):
+                for u in range(size // 128):
+                    tile = (HALF_LANES * half + start) // 128 + u
+                    lanes = slice(128 * u, 128 * u + 128)
+                    fmap[b, tile, 0:EDGE, :] = acc[top + EDGE * b : top + EDGE * b + EDGE, lanes]
+                    fmap[b, tile, EDGE + MID : EDGE + MID + 8, :] = acc[bottom + 8 * b : bottom + 8 * b + 8, lanes]
+    blank_rows(fmap, range(BLOCKS), row_last)
+
+
+def blank_rows(fmap, blocks, row_last):
+    row = lax.axis_index("rows")
+
+    @pl.when(row == 0)
+    def _():
+        for b in blocks:
+            fmap[b, :, 0:5, :] = jnp.zeros((BLOCK_LANES // 128, 5, 128), jnp.float32)
+
+    @pl.when(row == row_last)
+    def _():
+        for b in blocks:
+            fmap[b, :, 69:70, :] = jnp.zeros((BLOCK_LANES // 128, 1, 128), jnp.float32)
+
+
+def second_map(cols, fmap, w2, lhs2, smap):
+    for kh in range(6):
+        rows = pl.ds(kh, ROWS2, stride=4)
+        for i, col in enumerate(cols):
+            for u in range(3):
+                tiles = [divmod(2 * j + u, BLOCK_LANES // 128) for j in (col, col + 1)]
+                lhs2[48 * i : 48 * i + 48, 384 * kh + 128 * u : 384 * kh + 128 * u + 128] = jnp.concatenate(
+                    [fmap[block, tile, rows, :] for block, tile in tiles], axis=0
+                ).astype(jnp.bfloat16)
+    step = 5
+    for start in range(0, len(cols), step):
+        some = cols[start : start + step]
+        acc = gelu(
+            jnp.dot(lhs2[48 * start : 48 * (start + len(some)), :], w2[...], preferred_element_type=jnp.float32)
+        )
+        for i, col in enumerate(some):
             for u in range(2):
-                half = slice(128 * u, 128 * u + 128)
-                fmap[b, 2 * n + u, 0:EDGE, :] = acc[top + EDGE * b : top + EDGE * b + EDGE, half]
-                fmap[b, 2 * n + u, EDGE : EDGE + MID, :] = acc[MID * b : MID * b + MID, half]
-                fmap[b, 2 * n + u, EDGE + MID : EDGE + MID + 8, :] = acc[bottom + 8 * b : bottom + 8 * b + 8, half]
+                smap[u, col : col + 2] = acc[48 * i : 48 * i + 48, 128 * u : 128 * u + 128].reshape(2, ROWS2, 128)
+
+
+def middle_kernel(fmap, w2, smap, lhs2):
+    second_map(range(2, COLS2 - 2, 2), fmap, w2, lhs2, smap)
 
 
 def stem_kernel(
-    ca_ref, cb_ref, xb_in, fmap_in, toep, w2, w3, wk_far, wv_far,
-    xb, fmap, normed, wk, wv,
-    lhs1, lhs2, smap, lhs3, third, sems,
+    ca_ref, cb_ref, xb_in, fmap_in, smap_in, toep, w2, w3, wk_far, wv_far,
+    xb, fmap, smap, normed, wk, wv,
+    lhs1, lhs2, lhs3, third, sems,
     *, col_last, row_last,
 ):
     copies = [pltpu.make_async_copy(wk_far, wk, sems.at[0]), pltpu.make_async_copy(wv_far, wv, sems.at[1])]
@@ -192,40 +266,32 @@
     cb = cb_ref[...].astype(jnp.float32)
     left_all = jnp.where(even_col, cb, ca)
     right_all = jnp.where(even_col, ca, cb)
-    at_right = 512 + BEFORE - 4 * BLOCK_COLS * (BLOCKS - 1)
+    at_right = 512 + BEFORE - 4 * BLOCK_COLS * (BLOCKS - 1) - 56
     for c in range(3):
         for half in range(2):
             g = BEFORE * (2 * c + half)
             rows = slice(half * STRIP, half * STRIP + STRIP)
-            left = pltpu.roll(left_all, 128 - g, 1) if g else left_all
-            right = pltpu.roll(right_all, (at_right - g) % 128, 1)
-            xb[0, c, rows, :] = jnp.where(lane < BEFORE, left, xb[0, c, rows, :])
-            xb[BLOCKS - 1, c, rows, :] = jnp.where(
-                (lane >= at_right) & (lane < at_right + AFTER), right, xb[BLOCKS - 1, c, rows, :]
-            )
-    patch_rows(xb, 0, lhs1, 0)
-    patch_rows(xb, BLOCKS - 1, lhs1, 1)
-    for slot, b, tiles in ((0, 0, (0, 1)), (1, BLOCKS - 1, (5,))):
-        for n in tiles:
-            acc = gelu(
-                jnp.dot(
-                    lhs1[ROWS1 * slot : ROWS1 * slot + ROWS1, :],
-                    toep[:, 256 * n : 256 * n + 256],
-                    preferred_element_type=jnp.float32,
-                )
-            )
-            for u in range(2):
-                fmap[b, 2 * n + u, 0:ROWS1, :] = acc[:, 128 * u : 128 * u + 128]
-
-    @pl.when(row == 0)
-    def _():
-        for b in range(BLOCKS):
-            fmap[b, :, 0:5, :] = jnp.zeros((BLOCK_LANES // 128, 5, 128), jnp.float32)
-
-    @pl.when(row == row_last)
-    def _():
-        for b in range(BLOCKS):
-            fmap[b, :, 69:70, :] = jnp.zeros((BLOCK_LANES // 128, 1, 128), jnp.float32)
+            for order in range(2):
+                at = 64 * order
+                left = pltpu.roll(left_all, (at - g) % 128, 1) if at != g else left_all
+                here = (lane >= at) & (lane < at + BEFORE)
+                xb[order, 0, c, rows, :] = jnp.where(here, left, xb[order, 0, c, rows, :])
+                at = at_right + 64 * (1 - order)
+                right = pltpu.roll(right_all, (at - g) % 128, 1)
+                here = (lane >= at) & (lane < at + AFTER)
+                xb[order, BLOCKS - 1, c, rows, :] = jnp.where(here, right, xb[order, BLOCKS - 1, c, rows, :])
+    for k in range(9):
+        for half, b in ((0, 0), (1, BLOCKS - 1)):
+            lhs1[ROWS1 * half : ROWS1 * half + ROWS1, 128 * k : 128 * k + 128] = patches(
+                xb, b, half, k // 3, k % 3, 0, ROWS1
+            ).astype(jnp.bfloat16)
+    for n in range(2):
+        acc = gelu(jnp.dot(lhs1[...], toep[:, 256 * n : 256 * n + 256], preferred_element_type=jnp.float32))
+        for u in range(2):
+            fmap[0, 2 * n + u, 0:ROWS1, :] = acc[0:ROWS1, 128 * u : 128 * u + 128]
+    fmap[BLOCKS - 1, 10, 0:ROWS1, :] = acc[ROWS1:, 128:256]
+
+    blank_rows(fmap, (0, BLOCKS - 1), row_last)
 
     @pl.when(col == 0)
     def _():
@@ -237,24 +303,7 @@
         tile, side = divmod(133 - 4 * BLOCK_COLS, 2)
         fmap[4, tile, 0:ROWS1, 64 * side : 64 * side + 64] = jnp.zeros((ROWS1, 64), jnp.float32)
 
-    for kh in range(6):
-        for pair in range(COLS2 // 2):
-            both = []
-            for j in (2 * pair, 2 * pair + 1):
-                b, t = divmod(j, 7)
-                rows = pl.ds(kh, ROWS2, stride=4)
-                tiles = [divmod(14 * b + 2 * t + u, 14) for u in range(3)]
-                both.append([fmap[block, tile, rows, :] for block, tile in tiles])
-            for u in range(3):
-                lhs2[48 * pair : 48 * pair + 48, 384 * kh + 128 * u : 384 * kh + 128 * u + 128] = jnp.concatenate(
-                    [both[0][u], both[1][u]], axis=0
-                ).astype(jnp.bfloat16)
-    for start, size in ((0, 288), (288, 288), (576, 240)):
-        acc = gelu(jnp.dot(lhs2[start : start + size, :], w2[...], preferred_element_type=jnp.float32))
-        for u in range(2):
-            smap[u, start // ROWS2 : (start + size) // ROWS2] = acc[:, 128 * u : 128 * u + 128].reshape(
-                size // ROWS2, ROWS2, 128
-            )
+    second_map((0, COLS2 - 2), fmap, w2, lhs2, smap)
 
     @pl.when(row == 0)
     def _():
@@ -461,14 +510,14 @@
     def on_device(slide_pixels, stem_first, stem_second, stem_third, key_weight, value_weight, queries):
         bf16, f32 = jnp.bfloat16, jnp.float32
         rim = VMEM((3, RIM, 512), bf16)
-        row_a, row_b = call(
+        row_a, row_b, first_near = call(
             row_edges_kernel,
             "row_edges",
-            (slide_pixels,),
-            (rim, rim),
-            scratch=[pltpu.SemaphoreType.DMA((2,))],
+            (slide_pixels, stem_first),
+            (rim, rim, VMEM(stem_first.shape, bf16)),
+            scratch=[pltpu.SemaphoreType.DMA((3,))],
             limit=8 << 20,
-            far=(0,),
+            far=(0, 1),
         )
         row_a = lax.ppermute(row_a, "rows", swap_pairs(n_rows, False))
         row_b = lax.ppermute(row_b, "rows", swap_pairs(n_rows, True))
@@ -479,50 +528,72 @@
         col_a = lax.ppermute(col_a, "cols", swap_pairs(n_cols, False))
         col_b = lax.ppermute(col_b, "cols", swap_pairs(n_cols, True))
 
-        taps = stem_first.transpose(2, 0, 1, 3).reshape(TAPS1, 6, 64)
-        taps = sum(
-            jnp.pad(taps, ((0, 0), (top, 42 - top), (64 * side, 64 - 64 * side)))
-            for top, side in ((0, 0), (4, 1), (24, 0), (28, 1))
-        )
         (toep,) = call(
-            band_kernel, "band", (taps,), (VMEM((TAPS1 * 128, BLOCK_LANES), bf16),), moved=4 << 20, limit=2 << 20
-        )
-        xb_shape = VMEM((BLOCKS, 3, 328, 128), f32)
-        lhs1_shape = VMEM((ROWS_ALL, TAPS1 * 128), bf16)
+            band_kernel,
+            "band",
+            (first_near,),
+            (VMEM((DEPTH1, HALF_LANES), bf16),),
+            scratch=[pltpu.VMEM((TAPS1, 48, 128), f32)],
+            moved=1 << 20,
+            limit=4 << 20,
+        )
+        xb_shape = VMEM((2, BLOCKS, 3, 328, 128), f32)
         fmap_shape = VMEM((BLOCKS, BLOCK_LANES // 128, 104, 128), f32)
-        xb, lhs1 = call(
-            window_kernel, "windows", (slide_pixels,), (xb_shape, lhs1_shape), flops=1 << 28, moved=4 << 20, limit=8 << 20
-        )
-        xb, fmap, _ = call(
-            inner_kernel,
+        xb, fmap = call(
+            window_kernel,
+            "windows",
+            (slide_pixels, toep),
+            (xb_shape, fmap_shape),
+            scratch=[pltpu.VMEM((2 * MID_ALL, DEPTH1), bf16)],
+            flops=2 * MID_ALL * DEPTH1 * BLOCK_LANES,
+            moved=4 << 20,
+            limit=8 << 20,
+        )
+        xb, fmap = call(
+            functools.partial(inner_kernel, row_last=n_rows - 1),
             "inner",
-            (row_a, row_b, toep, xb, lhs1),
-            (xb_shape, fmap_shape, lhs1_shape),
-            aliases={3: 0, 4: 2},
-            flops=2 * ROWS_ALL * TAPS1 * 128 * BLOCK_LANES,
+            (row_a, row_b, toep, xb, fmap),
+            (xb_shape, fmap_shape),
+            scratch=[pltpu.VMEM((2 * EDGE_ALL, DEPTH1), bf16)],
+            aliases={3: 0, 4: 1},
+            flops=2 * EDGE_ALL * DEPTH1 * BLOCK_LANES,
             moved=16 << 20,
             limit=8 << 20,
         )
-        _, _, normed, key_near, value_near = call(
+        smap_shape = VMEM((2, COLS2, ROWS2, 128), f32)
+        w2 = stem_second.reshape(2304, 256)
+        (smap,) = call(
+            middle_kernel,
+            "middle",
+            (fmap, w2),
+            (smap_shape,),
+            scratch=[pltpu.VMEM(((COLS2 - 4) * ROWS2, 2304), bf16)],
+            flops=2 * COLS2 * ROWS2 * 2304 * 256,
+            moved=4 << 20,
+            limit=8 << 20,
+        )
+        _, _, _, normed, key_near, value_near = call(
             functools.partial(stem_kernel, col_last=n_cols - 1, row_last=n_rows - 1),
             "stem",
             (
-                col_a, col_b, xb, fmap, toep, stem_second.reshape(2304, 256), stem_third.reshape(2304, 1024),
+                col_a, col_b, xb, fmap, smap, toep, w2, stem_third.reshape(2304, 1024),
                 key_weight, value_weight,
             ),
-            (xb_shape, fmap_shape, VMEM((128, 1024), bf16), VMEM((1024, 1024), bf16), VMEM((1024, 1024), bf16)),
+            (
+                xb_shape, fmap_shape, smap_shape,
+                VMEM((128, 1024), bf16), VMEM((1024, 1024), bf16), VMEM((1024, 1024), bf16),
+            ),
             scratch=[
-                pltpu.VMEM((2 * ROWS1, TAPS1 * 128), bf16),
-                pltpu.VMEM((COLS2 * ROWS2, 2304), bf16),
-                pltpu.VMEM((2, COLS2, ROWS2, 128), f32),
+                pltpu.VMEM((2 * ROWS1, DEPTH1), bf16),
+                pltpu.VMEM((4 * ROWS2, 2304), bf16),
                 pltpu.VMEM((128, 2304), bf16),
                 pltpu.VMEM((128, 1024), f32),
                 pltpu.SemaphoreType.DMA((2,)),
             ],
-            aliases={2: 0, 3: 1},
-            far=(7, 8),
-            flops=3 << 30,
-            limit=16 << 20,
+            aliases={2: 0, 3: 1, 4: 2},
+            far=(8, 9),
+            flops=2 << 30,
+            limit=8 << 20,
         )
         normed_other = lax.ppermute(normed, "rows", swap_pairs(n_rows, False))
         (kv,) = call(

time: 44 us -> 42.9 us (0.975)
  local copies, waits for them, and re-layouts: 1.29 us -> 0.37 us
    transpose x1 -> x0, local copies, waits for them, and re-layouts: 0.78 us -> none  [on_device(): taps = stem_first.transpose(2, 0, 1, 3).reshape(TAPS1, 6, 64)]
    pallas_call x15 -> x16, Pallas kernels: 14.5 us -> 14.4 us  [call(): pl.pallas_call(kernel, in_specs=[far_spec if i in far else spec for i in...]
  transfers between devices with their start and end apart: 11 -> 11, of which waited for: 6 -> 6; matrix products, arithmetic and copies ran while one was open for 3% -> 1% of each run, Pallas kernels for 15% -> 17%
where the time goes in v5:
time: 42.9 us; the launch traced here: 42.8 us
  starting transfers between devices  19.7 us (46%)
  Pallas kernels  14.4 us (34%)
  waiting for transfers between devices  8.02 us (19%)
    pallas_call x16, Pallas kernels, call(): pl.pallas_call(kernel, in_specs=[far_spec if i in far else spec for i in...  14.4 us
    ppermute x6, starting transfers between devices, exchange(): return lax.ppermute(value, ('cols', 'rows'), pairs)  12.6 us
    ppermute x6, waiting for transfers between devices, exchange(): return lax.ppermute(value, ('cols', 'rows'), pairs)  7.1 us
    ppermute x1, starting transfers between devices, on_device(): normed_other = lax.ppermute(normed, 'rows', swap_pairs(n_rows, False))  2.66 us
    ppermute x1, starting transfers between devices, on_device(): col_a = lax.ppermute(col_a, 'cols', swap_pairs(n_cols, False))  2.58 us
    ppermute x1, waiting for transfers between devices, on_device(): normed_other = lax.ppermute(normed, 'rows', swap_pairs(n_rows, False))  0.91 us
  transfers between devices with their start and end apart: 11, of which 6 were waited for; matrix products, arithmetic and copies ran while one was open for 1% of the time, Pallas kernels for 17%

profile of v5, /device:TPU:0, one launch (start us, length us, event | category | flops | bytes accessed | tf_op | source)
XLA Modules:
  0.0 42.8 jit_solution(7674350341082843673)
XLA Ops:
  0.0 1.0 %row_edges.1 = (bf16[3,24,512]{2,1,0:T(8,128)(2,1)S(1)}, bf16[3,24,512]{2,1,0:T(8,128)(2,1)S(1)}, bf16[6,6,3,64]{3,2,1,0:T(4,128)(2,1)S(1)}) custom-call(bf16[3,256,512]{2,1,0:T(8,128)(2,1)} %slide.3, bf16[6,6,3,64]{3,2,1,0:T(4,128)(2,1)} %kernel_far.1), custom_call_target="tpu_custom_call" | custom-call | tf_op jit(solution)/shard_map/row_edges/pallas_call | solution.py:428
  1.1 0.5 %collective-permute-start = (bf16[3,24,512]{2,1,0:T(8,128)(2,1)S(1)}, bf16[3,24,512]{2,1,0:T(8,128)(2,1)S(1)}, u32[]{:S(2)}, u32[]{:S(2)}) collective-permute-start(bf16[3,24,512]{2,1,0:T(8,128)(2,1)S(1)} %get-tuple-element.30), channel_id=1, source_target_pairs={{0,1},{1,0},{2,3},{3,2},{4,5},{5,4},{6,7},{7,6},{8,9},{9,8},{10,11... | collective-permute-start | bytes 221192 | tf_op jit(solution)/shard_map/ppermute | solution.py:522
  1.6 0.7 %collective-permute-start.1 = (bf16[3,24,512]{2,1,0:T(8,128)(2,1)S(1)}, bf16[3,24,512]{2,1,0:T(8,128)(2,1)S(1)}, u32[]{:S(2)}, u32[]{:S(2)}) collective-permute-start(bf16[3,24,512]{2,1,0:T(8,128)(2,1)S(1)} %get-tuple-element.31), channel_id=1, source_target_pairs={{1,2},{2,1},{5,6},{6,5},{9,10},{10,9},{13,14},{14,13},{17,18},{18,... | collective-permute-start | bytes 221192 | tf_op jit(solution)/shard_map/ppermute | solution.py:523
  2.2 0.8 %band.1.toep = bf16[1152,896]{1,0:T(8,128)(2,1)S(1)} custom-call(bf16[6,6,3,64]{3,2,1,0:T(4,128)(2,1)S(1)} %get-tuple-element.34.kernel_ref), custom_call_target="tpu_custom_call" | custom-call | bytes 1048576 | tf_op jit(solution)/shard_map/band/pallas_call | solution.py:428
  3.1 2.2 %windows.1 = (f32[2,5,3,328,128]{4,3,2,1,0:T(8,128)S(1)}, f32[5,14,104,128]{3,2,1,0:T(8,128)S(1)}) custom-call(bf16[3,256,512]{2,1,0:T(8,128)(2,1)S(1)} %copy-done.1, bf16[1152,896]{1,0:T(8,128)(2,1)S(1)} %band.1.toep), custom_call_target="tpu_custom_call" | custom-call | flops 990904320 | bytes 4194304 | tf_op jit(solution)/shard_map/windows/pallas_call | solution.py:428
  5.5 2.6 %collective-permute-start.2 = (bf16[144,128]{1,0:T(8,128)(2,1)S(1)}, bf16[144,128]{1,0:T(8,128)(2,1)S(1)}, u32[]{:S(2)}, u32[]{:S(2)}) collective-permute-start(bf16[144,128]{1,0:T(8,128)(2,1)S(1)} %get-tuple-element.32), channel_id=1, source_target_pairs={{0,4},{4,0},{8,12},{12,8},{16,20},{20,16},{24,28},{28,24},{1,5},{5... | collective-permute-start | bytes 110600 | tf_op jit(solution)/shard_map/ppermute | solution.py:528
  8.1 0.7 %collective-permute-start.3 = (bf16[144,128]{1,0:T(8,128)(2,1)S(1)}, bf16[144,128]{1,0:T(8,128)(2,1)S(1)}, u32[]{:S(2)}, u32[]{:S(2)}) collective-permute-start(bf16[144,128]{1,0:T(8,128)(2,1)S(1)} %get-tuple-element.33), channel_id=1, source_target_pairs={{4,8},{8,4},{12,16},{16,12},{20,24},{24,20},{5,9},{9,5},{13,17},{1... | collective-permute-start | bytes 110600 | tf_op jit(solution)/shard_map/ppermute | solution.py:529
  8.8 1.2 %inner.1 = (f32[2,5,3,328,128]{4,3,2,1,0:T(8,128)S(1)}, f32[5,14,104,128]{3,2,1,0:T(8,128)S(1)}) custom-call(bf16[3,24,512]{2,1,0:T(8,128)(2,1)S(1)} %collective-permute-done.ra_ref, bf16[3,24,512]{2,1,0:T(8,128)(2,1)S(1)} %collective-permute-done.1.rb_ref, bf16[1152,896]{1,0:T(8,128)(2,1)S(1)} %band.1.toep, ...), custom_call_target="tpu_custom_call", output_to_operand_aliasing={{0}: (3, {}), {1}: (4, {})} | custom-call | flops 528482304 | bytes 16777216 | tf_op jit(solution)/shard_map/inner/pallas_call | solution.py:428
  10.0 0.2 copy-done
  10.2 1.4 %middle.1.smap_in = f32[2,34,24,128]{3,2,1,0:T(8,128)S(1)} custom-call(f32[5,14,104,128]{3,2,1,0:T(8,128)S(1)} %get-tuple-element.38.fmap.fmap_in, bf16[2304,256]{1,0:T(8,128)(2,1)S(1)} %bitcast.16), custom_call_target="tpu_custom_call" | custom-call | flops 962592768 | bytes 4194304 | tf_op jit(solution)/shard_map/middle/pallas_call | solution.py:428
  11.6 2.6 %stem.1 = (f32[2,5,3,328,128]{4,3,2,1,0:T(8,128)S(1)}, f32[5,14,104,128]{3,2,1,0:T(8,128)S(1)}, f32[2,34,24,128]{3,2,1,0:T(8,128)S(1)}, bf16[128,1024]{1,0:T(8,1...) custom-call(bf16[144,128]{1,0:T(8,128)(2,1)S(1)} %collective-permute, ...), custom_call_target="tpu_custom_call", output_to_operand_aliasing={{0}: (2, {}), {1}: (3, {}), {2}: (4, {})} | custom-call | flops 2147483648 | tf_op jit(solution)/shard_map/stem/pallas_call | solution.py:428
  14.2 2.7 %collective-permute-start.4 = (bf16[128,1024]{1,0:T(8,128)(2,1)S(1)}, bf16[128,1024]{1,0:T(8,128)(2,1)S(1)}, u32[]{:S(2)}, u32[]{:S(2)}) collective-permute-start(bf16[128,1024]{1,0:T(8,128)(2,1)S(1)} %get-tuple-element.39.mine), channel_id=1, source_target_pairs={{0,1},{1,0},{2,3},{3,2},{4,5},{5,4},{6,7},{7,6},{8,9},{9,8},{10,11... | collective-permute-start | bytes 786440 | tf_op jit(solution)/shard_map/ppermute | solution.py:598
  17.1 0.9 %collective-permute-done.4.theirs = bf16[128,1024]{1,0:T(8,128)(2,1)S(1)} collective-permute-done((bf16[128,1024]{1,0:T(8,128)(2,1)S(1)}, bf16[128,1024]{1,0:T(8,128)(2,1)S(1)}, u32[]{:S(2)}, u32[]{:S(2)}) %collective-permute-start.4) | collective-permute-done | bytes 262176 | tf_op jit(solution)/shard_map/ppermute | solution.py:598
  18.0 1.3 %project.1.kv = bf16[256,2048]{1,0:T(8,128)(2,1)S(1)} custom-call(bf16[128,1024]{1,0:T(8,128)(2,1)S(1)} %get-tuple-element.39.mine, bf16[128,1024]{1,0:T(8,128)(2,1)S(1)} %collective-permute-done.4.theirs, bf16[1024,1024]{1,0:T(8,128)(2,1)S(1)} %get-tuple-element.40.wk, bf16[1024,1024]{1,0:T(8,128)(2,1)S(1)} %get-tuple-element.41.wv), custom_call_target="tpu_custom_call" | custom-call | flops 1073741824 | tf_op jit(solution)/shard_map/project/pallas_call | solution.py:428
  19.3 0.9 %attend.2 = (bf16[64,1152]{1,0:T(8,128)(2,1)S(1)}, bf16[64,1152]{1,0:T(8,128)(2,1)S(1)}) custom-call(bf16[512,1024]{1,0:T(8,128)(2,1)S(1)} %pad_maximum_fusion.q, bf16[256,2048]{1,0:T(8,128)(2,1)S(1)} %project.1.kv), custom_call_target="tpu_custom_call" | custom-call | flops 1073741824 | tf_op jit(solution)/shard_map/attend/pallas_call | solution.py:428
  20.2 1.3 %collective-permute-start.7 = (bf16[64,1152]{1,0:T(8,128)(2,1)S(1)}, bf16[64,1152]{1,0:T(8,128)(2,1)S(1)}, u32[]{:S(2)}, u32[]{:S(2)}) collective-permute-start(bf16[64,1152]{1,0:T(8,128)(2,1)S(1)} %get-tuple-element.50), channel_id=1, source_target_pairs={{0,2},{1,5},{2,0},{3,7},{4,6},{5,1},{6,4},{7,3},{8,10},{9,13},{10,... | collective-permute-start | bytes 442376 | tf_op jit(solution)/shard_map/ppermute | solution.py:482
  21.5 0.8 %collective-permute-start.5 = (bf16[64,1152]{1,0:T(8,128)(2,1)S(1)}, bf16[64,1152]{1,0:T(8,128)(2,1)S(1)}, u32[]{:S(2)}, u32[]{:S(2)}) collective-permute-start(bf16[64,1152]{1,0:T(8,128)(2,1)S(1)} %get-tuple-element.46), channel_id=1, source_target_pairs={{0,2},{1,5},{2,0},{3,7},{4,6},{5,1},{6,4},{7,3},{8,10},{9,13},{10,... | collective-permute-start | bytes 442376 | tf_op jit(solution)/shard_map/ppermute | solution.py:482
  22.3 0.9 %attend.3 = (f32[64,1152]{1,0:T(8,128)S(1)}, f32[64,1152]{1,0:T(8,128)S(1)}) custom-call(bf16[512,1024]{1,0:T(8,128)(2,1)S(1)} %pad_maximum_fusion.q, bf16[256,2048]{1,0:T(8,128)(2,1)S(1)} %project.1.kv), custom_call_target="tpu_custom_call" | custom-call | flops 1073741824 | tf_op jit(solution)/shard_map/attend/pallas_call | solution.py:428
  23.2 2.2 %collective-permute-done.7.recv_ref = bf16[64,1152]{1,0:T(8,128)(2,1)S(1)} collective-permute-done((bf16[64,1152]{1,0:T(8,128)(2,1)S(1)}, bf16[64,1152]{1,0:T(8,128)(2,1)S(1)}, u32[]{:S(2)}, u32[]{:S(2)}) %collective-permute-start.7) | collective-permute-done | bytes 147488 | tf_op jit(solution)/shard_map/ppermute | solution.py:482
  25.5 0.2 merge.8
  25.7 4.1 %collective-permute-start.8 = (bf16[32,1152]{1,0:T(8,128)(2,1)S(1)}, bf16[32,1152]{1,0:T(8,128)(2,1)S(1)}, u32[]{:S(2)}, u32[]{:S(2)}) collective-permute-start(bf16[32,1152]{1,0:T(8,128)(2,1)S(1)} %get-tuple-element.52), channel_id=1, source_target_pairs={{0,4},{1,3},{2,6},{3,1},{4,0},{5,7},{6,2},{7,5},{8,12},{9,11},{10,... | collective-permute-start | bytes 221192 | tf_op jit(solution)/shard_map/ppermute | solution.py:482
  29.8 0.2 merge.6
  30.0 1.3 %collective-permute-start.6 = (bf16[32,1152]{1,0:T(8,128)(2,1)S(1)}, bf16[32,1152]{1,0:T(8,128)(2,1)S(1)}, u32[]{:S(2)}, u32[]{:S(2)}) collective-permute-start(bf16[32,1152]{1,0:T(8,128)(2,1)S(1)} %get-tuple-element.48), channel_id=1, source_target_pairs={{0,4},{1,3},{2,6},{3,1},{4,0},{5,7},{6,2},{7,5},{8,12},{9,11},{10,... | collective-permute-start | bytes 221192 | tf_op jit(solution)/shard_map/ppermute | solution.py:482
  31.4 0.8 %collective-permute-done.8.recv_ref = bf16[32,1152]{1,0:T(8,128)(2,1)S(1)} collective-permute-done((bf16[32,1152]{1,0:T(8,128)(2,1)S(1)}, bf16[32,1152]{1,0:T(8,128)(2,1)S(1)}, u32[]{:S(2)}, u32[]{:S(2)}) %collective-permute-start.8) | collective-permute-done | bytes 73760 | tf_op jit(solution)/shard_map/ppermute | solution.py:482
  32.1 0.2 merge.9
  32.3 2.0 %collective-permute-start.9 = (bf16[32,1152]{1,0:T(8,128)(2,1)S(1)}, bf16[32,1152]{1,0:T(8,128)(2,1)S(1)}, u32[]{:S(2)}, u32[]{:S(2)}) collective-permute-start(bf16[32,1152]{1,0:T(8,128)(2,1)S(1)} %merge.9), channel_id=1, source_target_pairs={{0,8},{1,9},{2,10},{3,11},{4,12},{5,13},{6,14},{7,15},{8,0},{9,1},... | collective-permute-start | bytes 221192 | tf_op jit(solution)/shard_map/ppermute | solution.py:482
  34.5 0.2 merge.7.keep_ref
  34.7 2.1 %collective-permute-done.9.recv_ref = bf16[32,1152]{1,0:T(8,128)(2,1)S(1)} collective-permute-done((bf16[32,1152]{1,0:T(8,128)(2,1)S(1)}, bf16[32,1152]{1,0:T(8,128)(2,1)S(1)}, u32[]{:S(2)}, u32[]{:S(2)}) %collective-permute-start.9) | collective-permute-done | bytes 73760 | tf_op jit(solution)/shard_map/ppermute | solution.py:482
  36.7 0.2 merge.10
  37.0 3.1 %collective-permute-start.10 = (bf16[16,1152]{1,0:T(8,128)(2,1)S(1)}, bf16[16,1152]{1,0:T(8,128)(2,1)S(1)}, u32[]{:S(2)}, u32[]{:S(2)}) collective-permute-start(bf16[16,1152]{1,0:T(8,128)(2,1)S(1)} %get-tuple-element.54), channel_id=1, source_target_pairs={{0,16},{1,17},{2,18},{3,19},{4,20},{5,21},{6,22},{7,23},{8,24},{9,... | collective-permute-start | bytes 110600 | tf_op jit(solution)/shard_map/ppermute | solution.py:482
  40.0 1.9 %collective-permute-done.10.recv_ref = bf16[16,1152]{1,0:T(8,128)(2,1)S(1)} collective-permute-done((bf16[16,1152]{1,0:T(8,128)(2,1)S(1)}, bf16[16,1152]{1,0:T(8,128)(2,1)S(1)}, u32[]{:S(2)}, u32[]{:S(2)}) %collective-permute-start.10) | collective-permute-done | bytes 36896 | tf_op jit(solution)/shard_map/ppermute | solution.py:482
  42.0 0.8 %merge.11 = bf16[16,1024]{1,0:T(8,128)(2,1)} custom-call(f32[16,1152]{1,0:T(8,128)S(1)} %get-tuple-element.53.keep_ref, bf16[16,1152]{1,0:T(8,128)(2,1)S(1)} %collective-permute-done.10.recv_ref), custom_call_target="tpu_custom_call" | custom-call | tf_op jit(solution)/shard_map/merge/pallas_call | solution.py:428
  (21 shorter events, 0.5 us)
Async XLA Ops:
  0.0 3.1 %copy-start.1 = (bf16[3,256,512]{2,1,0:T(8,128)(2,1)S(1)}, bf16[3,256,512]{2,1,0:T(8,128)(2,1)}, u32[]{:S(2)}) copy-start(bf16[3,256,512]{2,1,0:T(8,128)(2,1)} %slide.3) | copy-start | bytes 2359300
  1.1 4.2 %collective-permute-start = (bf16[3,24,512]{2,1,0:T(8,128)(2,1)S(1)}, bf16[3,24,512]{2,1,0:T(8,128)(2,1)S(1)}, u32[]{:S(2)}, u32[]{:S(2)}) collective-permute-start(bf16[3,24,512]{2,1,0:T(8,128)(2,1)S(1)} %get-tuple-element.30), channel_id=1, source_target_pairs={{0,1},{1,0},{2,3},{3,2},{4,5},{5,4},{6,7},{7,6},{8,9},{9,8},{10,11... | collective-permute-start | bytes 221192 | tf_op jit(solution)/shard_map/ppermute | solution.py:522
  1.6 3.7 %collective-permute-start.1 = (bf16[3,24,512]{2,1,0:T(8,128)(2,1)S(1)}, bf16[3,24,512]{2,1,0:T(8,128)(2,1)S(1)}, u32[]{:S(2)}, u32[]{:S(2)}) collective-permute-start(bf16[3,24,512]{2,1,0:T(8,128)(2,1)S(1)} %get-tuple-element.31), channel_id=1, source_target_pairs={{1,2},{2,1},{5,6},{6,5},{9,10},{10,9},{13,14},{14,13},{17,18},{18,... | collective-permute-start | bytes 221192 | tf_op jit(solution)/shard_map/ppermute | solution.py:523
  5.5 6.1 %collective-permute-start.2 = (bf16[144,128]{1,0:T(8,128)(2,1)S(1)}, bf16[144,128]{1,0:T(8,128)(2,1)S(1)}, u32[]{:S(2)}, u32[]{:S(2)}) collective-permute-start(bf16[144,128]{1,0:T(8,128)(2,1)S(1)} %get-tuple-element.32), channel_id=1, source_target_pairs={{0,4},{4,0},{8,12},{12,8},{16,20},{20,16},{24,28},{28,24},{1,5},{5... | collective-permute-start | bytes 110600 | tf_op jit(solution)/shard_map/ppermute | solution.py:528
  8.1 3.5 %collective-permute-start.3 = (bf16[144,128]{1,0:T(8,128)(2,1)S(1)}, bf16[144,128]{1,0:T(8,128)(2,1)S(1)}, u32[]{:S(2)}, u32[]{:S(2)}) collective-permute-start(bf16[144,128]{1,0:T(8,128)(2,1)S(1)} %get-tuple-element.33), channel_id=1, source_target_pairs={{4,8},{8,4},{12,16},{16,12},{20,24},{24,20},{5,9},{9,5},{13,17},{1... | collective-permute-start | bytes 110600 | tf_op jit(solution)/shard_map/ppermute | solution.py:529
  8.7 2.9 %slice-start = ((s8[4718592]{0:T(1024)(128)(4,1)}), s8[4194304]{0:T(1024)(128)(4,1)S(1)}, s32[]{:S(2)}) async-start(s8[4718592]{0:T(1024)(128)(4,1)} %bitcast.13), calls=%async_computation | async-start | bytes 8388608
  8.7 1.4 %copy-start = (bf16[6,6,64,256]{3,2,1,0:T(8,128)(2,1)S(1)}, bf16[6,6,64,256]{3,2,1,0:T(8,128)(2,1)}, u32[]{:S(2)}) copy-start(bf16[6,6,64,256]{3,2,1,0:T(8,128)(2,1)} %param.9) | copy-start | bytes 3538948
  8.8 2.8 %slice-start.1 = ((s8[4718592]{0:T(1024)(128)(4,1)}), s8[524288]{0:T(1024)(128)(4,1)S(1)}, s32[]{:S(2)}) async-start(s8[4718592]{0:T(1024)(128)(4,1)} %bitcast.13), calls=%async_computation.1 | async-start | bytes 1048576
  11.6 5.2 %copy-start.2 = (bf16[512,1024]{1,0:T(8,128)(2,1)S(1)}, bf16[512,1024]{1,0:T(8,128)(2,1)}, u32[]{:S(2)}) copy-start(bf16[512,1024]{1,0:T(8,128)(2,1)} %param.13) | copy-start | bytes 3145732
  14.2 3.8 %collective-permute-start.4 = (bf16[128,1024]{1,0:T(8,128)(2,1)S(1)}, bf16[128,1024]{1,0:T(8,128)(2,1)S(1)}, u32[]{:S(2)}, u32[]{:S(2)}) collective-permute-start(bf16[128,1024]{1,0:T(8,128)(2,1)S(1)} %get-tuple-element.39.mine), channel_id=1, source_target_pairs={{0,1},{1,0},{2,3},{3,2},{4,5},{5,4},{6,7},{7,6},{8,9},{9,8},{10,11... | collective-permute-start | bytes 786440 | tf_op jit(solution)/shard_map/ppermute | solution.py:598
  20.2 5.2 %collective-permute-start.7 = (bf16[64,1152]{1,0:T(8,128)(2,1)S(1)}, bf16[64,1152]{1,0:T(8,128)(2,1)S(1)}, u32[]{:S(2)}, u32[]{:S(2)}) collective-permute-start(bf16[64,1152]{1,0:T(8,128)(2,1)S(1)} %get-tuple-element.50), channel_id=1, source_target_pairs={{0,2},{1,5},{2,0},{3,7},{4,6},{5,1},{6,4},{7,3},{8,10},{9,13},{10,... | collective-permute-start | bytes 442376 | tf_op jit(solution)/shard_map/ppermute | solution.py:482
  21.5 8.2 %collective-permute-start.5 = (bf16[64,1152]{1,0:T(8,128)(2,1)S(1)}, bf16[64,1152]{1,0:T(8,128)(2,1)S(1)}, u32[]{:S(2)}, u32[]{:S(2)}) collective-permute-start(bf16[64,1152]{1,0:T(8,128)(2,1)S(1)} %get-tuple-element.46), channel_id=1, source_target_pairs={{0,2},{1,5},{2,0},{3,7},{4,6},{5,1},{6,4},{7,3},{8,10},{9,13},{10,... | collective-permute-start | bytes 442376 | tf_op jit(solution)/shard_map/ppermute | solution.py:482
  25.7 6.4 %collective-permute-start.8 = (bf16[32,1152]{1,0:T(8,128)(2,1)S(1)}, bf16[32,1152]{1,0:T(8,128)(2,1)S(1)}, u32[]{:S(2)}, u32[]{:S(2)}) collective-permute-start(bf16[32,1152]{1,0:T(8,128)(2,1)S(1)} %get-tuple-element.52), channel_id=1, source_target_pairs={{0,4},{1,3},{2,6},{3,1},{4,0},{5,7},{6,2},{7,5},{8,12},{9,11},{10,... | collective-permute-start | bytes 221192 | tf_op jit(solution)/shard_map/ppermute | solution.py:482
  30.0 4.4 %collective-permute-start.6 = (bf16[32,1152]{1,0:T(8,128)(2,1)S(1)}, bf16[32,1152]{1,0:T(8,128)(2,1)S(1)}, u32[]{:S(2)}, u32[]{:S(2)}) collective-permute-start(bf16[32,1152]{1,0:T(8,128)(2,1)S(1)} %get-tuple-element.48), channel_id=1, source_target_pairs={{0,4},{1,3},{2,6},{3,1},{4,0},{5,7},{6,2},{7,5},{8,12},{9,11},{10,... | collective-permute-start | bytes 221192 | tf_op jit(solution)/shard_map/ppermute | solution.py:482
  32.3 4.4 %collective-permute-start.9 = (bf16[32,1152]{1,0:T(8,128)(2,1)S(1)}, bf16[32,1152]{1,0:T(8,128)(2,1)S(1)}, u32[]{:S(2)}, u32[]{:S(2)}) collective-permute-start(bf16[32,1152]{1,0:T(8,128)(2,1)S(1)} %merge.9), channel_id=1, source_target_pairs={{0,8},{1,9},{2,10},{3,11},{4,12},{5,13},{6,14},{7,15},{8,0},{9,1},... | collective-permute-start | bytes 221192 | tf_op jit(solution)/shard_map/ppermute | solution.py:482
  37.0 5.0 %collective-permute-start.10 = (bf16[16,1152]{1,0:T(8,128)(2,1)S(1)}, bf16[16,1152]{1,0:T(8,128)(2,1)S(1)}, u32[]{:S(2)}, u32[]{:S(2)}) collective-permute-start(bf16[16,1152]{1,0:T(8,128)(2,1)S(1)} %get-tuple-element.54), channel_id=1, source_target_pairs={{0,16},{1,17},{2,18},{3,19},{4,20},{5,21},{6,22},{7,23},{8,24},{9,... | collective-permute-start | bytes 110600 | tf_op jit(solution)/shard_map/ppermute | solution.py:482

commit v6 on v5

--- a/solution.py
+++ b/solution.py
@@ -149,7 +149,9 @@
     return jnp.where(low, first, second)
 
 
-def window_kernel(slide, toep, xb, fmap, lhs1):
+def window_kernel(slide, toep, far, xb, fmap, near, lhs1, sem):
+    copy = pltpu.make_async_copy(far, near, sem)
+    copy.start()
     for c in range(3):
         for b, part in enumerate(cut(slide[c])):
             for order in range(2):
@@ -170,6 +172,7 @@
                 for u in range(size // 128):
                     tile = (HALF_LANES * half + start) // 128 + u
                     fmap[b, tile, EDGE : EDGE + MID, :] = acc[row0 : row0 + MID, 128 * u : 128 * u + 128]
+    copy.wait()
 
 
 def inner_kernel(ra_ref, rb_ref, toep, xb_in, fmap_in, xb, fmap, lhs1, *, row_last):
@@ -250,14 +253,13 @@
 
 
 def stem_kernel(
-    ca_ref, cb_ref, xb_in, fmap_in, smap_in, toep, w2, w3, wk_far, wv_far,
-    xb, fmap, smap, normed, wk, wv,
-    lhs1, lhs2, lhs3, third, sems,
+    ca_ref, cb_ref, xb_in, fmap_in, smap_in, toep, w2, w3, far,
+    xb, fmap, smap, normed, near,
+    lhs1, lhs2, lhs3, third, sem,
     *, col_last, row_last,
 ):
-    copies = [pltpu.make_async_copy(wk_far, wk, sems.at[0]), pltpu.make_async_copy(wv_far, wv, sems.at[1])]
-    for copy in copies:
-        copy.start()
+    copy = pltpu.make_async_copy(far, near, sem)
+    copy.start()
     col = lax.axis_index("cols")
     row = lax.axis_index("rows")
     even_col = col % 2 == 0
@@ -333,21 +335,17 @@
     centred = tokens - jnp.mean(tokens, axis=-1, keepdims=True)
     var = jnp.mean(centred * centred, axis=-1, keepdims=True)
     normed[...] = (centred * lax.rsqrt(var + 1e-05)).astype(jnp.bfloat16)
-    for copy in copies:
-        copy.wait()
-
-
-def project_kernel(mine, theirs, wk, wv, kv, tokens):
-    half = mine.shape[0]
-    tokens[0:half] = mine[...]
-    tokens[half:] = theirs[...]
+    copy.wait()
+
+
+def project_kernel(tokens, wk, wv, kv):
     for i, w in enumerate((wk, wv)):
         for n in range(4):
             rows = jnp.dot(tokens[...], w[:, 256 * n : 256 * n + 256], preferred_element_type=jnp.float32)
             kv[:, 1024 * i + 256 * n : 1024 * i + 256 * n + 256] = rows.astype(jnp.bfloat16)
 
 
-def attend_kernel(q, kv, lead, lag, *, bit_of, chunk_of, keep):
+def attend_kernel(q, mine, theirs, lead, lag, *, bit_of, chunk_of, keep):
     half = lead.shape[0]
     n = 2 * half
     quarter = 2 * (lax.axis_index("rows") % 2) + (bit_of() if keep else 1 - bit_of())
@@ -364,13 +362,15 @@
     for h in range(HEADS):
         lanes = slice(128 * h, 128 * h + 128)
         past = slice(1024 + 128 * h, 1024 + 128 * h + 128)
+        keys = jnp.concatenate([mine[:, lanes], theirs[:, lanes]], axis=0)
+        values = jnp.concatenate([mine[:, past], theirs[:, past]], axis=0)
         scores = lax.dot_general(
-            q[rows, lanes], kv[:, lanes], (((1,), (1,)), ((), ())), preferred_element_type=jnp.float32
+            q[rows, lanes], keys, (((1,), (1,)), ((), ())), preferred_element_type=jnp.float32
         ) * scale
         peak = jnp.max(scores, axis=1, keepdims=True)
         w = jnp.exp(scores - peak)
         total = jnp.sum(w, axis=1, keepdims=True)
-        o = jnp.dot(w.astype(jnp.bfloat16), kv[:, past], preferred_element_type=jnp.float32)
+        o = jnp.dot(w.astype(jnp.bfloat16), values, preferred_element_type=jnp.float32)
         put(lanes, o * (1.0 / total))
         stat = jnp.where(lane == h, peak + jnp.log(total), stat)
     put(slice(1024, 1152), stat if keep else pack_stat(stat).astype(jnp.float32))
@@ -539,12 +539,13 @@
         )
         xb_shape = VMEM((2, BLOCKS, 3, 328, 128), f32)
         fmap_shape = VMEM((BLOCKS, BLOCK_LANES // 128, 104, 128), f32)
-        xb, fmap = call(
+        xb, fmap, key_near = call(
             window_kernel,
             "windows",
-            (slide_pixels, toep),
-            (xb_shape, fmap_shape),
-            scratch=[pltpu.VMEM((2 * MID_ALL, DEPTH1), bf16)],
+            (slide_pixels, toep, key_weight),
+            (xb_shape, fmap_shape, VMEM(key_weight.shape, bf16)),
+            scratch=[pltpu.VMEM((2 * MID_ALL, DEPTH1), bf16), pltpu.SemaphoreType.DMA],
+            far=(2,),
             flops=2 * MID_ALL * DEPTH1 * BLOCK_LANES,
             moved=4 << 20,
             limit=8 << 20,
@@ -572,39 +573,42 @@
             moved=4 << 20,
             limit=8 << 20,
         )
-        _, _, _, normed, key_near, value_near = call(
+        _, _, _, normed, value_near = call(
             functools.partial(stem_kernel, col_last=n_cols - 1, row_last=n_rows - 1),
             "stem",
             (
                 col_a, col_b, xb, fmap, smap, toep, w2, stem_third.reshape(2304, 1024),
-                key_weight, value_weight,
+                value_weight,
             ),
             (
                 xb_shape, fmap_shape, smap_shape,
-                VMEM((128, 1024), bf16), VMEM((1024, 1024), bf16), VMEM((1024, 1024), bf16),
+                VMEM((128, 1024), bf16), VMEM(value_weight.shape, bf16),
             ),
             scratch=[
                 pltpu.VMEM((2 * ROWS1, DEPTH1), bf16),
                 pltpu.VMEM((4 * ROWS2, 2304), bf16),
                 pltpu.VMEM((128, 2304), bf16),
                 pltpu.VMEM((128, 1024), f32),
-                pltpu.SemaphoreType.DMA((2,)),
+                pltpu.SemaphoreType.DMA,
             ],
             aliases={2: 0, 3: 1, 4: 2},
-            far=(8, 9),
+            far=(8,),
             flops=2 << 30,
             limit=8 << 20,
         )
         normed_other = lax.ppermute(normed, "rows", swap_pairs(n_rows, False))
-        (kv,) = call(
-            project_kernel,
-            "project",
-            (normed, normed_other, key_near, value_near),
-            (VMEM((256, 2048), bf16),),
-            scratch=[pltpu.VMEM((256, 1024), bf16)],
-            flops=1 << 30,
-            limit=8 << 20,
-        )
+
+        def project(tokens):
+            return call(
+                project_kernel,
+                "project",
+                (tokens, key_near, value_near),
+                (VMEM((tokens.shape[0], 2048), bf16),),
+                flops=1 << 29,
+                limit=4 << 20,
+            )[0]
+
+        kv, kv_other = project(normed), project(normed_other)
         ordered = order_queries(queries)
         eighth = queries.shape[0] // 8
         width = 1024 + STAT
@@ -614,7 +618,7 @@
             return call(
                 functools.partial(attend_kernel, bit_of=bit_of(0), chunk_of=bit_of(2), keep=keep),
                 "attend",
-                (q, kv),
+                (q, kv, kv_other),
                 (shape, shape),
                 flops=1 << 30,
                 limit=8 << 20,

time: 42.9 us -> 42.1 us (0.981)
  waiting for transfers between devices: 8.02 us -> 7.27 us
    ppermute x1, waiting for transfers between devices: 0.91 us -> 0.16 us  [on_device(): normed_other = lax.ppermute(normed, 'rows', swap_pairs(n_rows, False))]
    pallas_call x16 -> x17, Pallas kernels: 14.4 us -> 14.3 us  [call(): pl.pallas_call(kernel, in_specs=[far_spec if i in far else spec for i in...]
  transfers between devices with their start and end apart: 11 -> 11, of which waited for: 6 -> 6; matrix products, arithmetic and copies ran while one was open for 1% -> 1% of each run, Pallas kernels for 17% -> 19%
where the time goes in v6:
time: 42.1 us; the launch traced here: 41.9 us
  starting transfers between devices  19.6 us (47%)
  Pallas kernels  14.3 us (34%)
  waiting for transfers between devices  7.27 us (17%)
    pallas_call x17, Pallas kernels, call(): pl.pallas_call(kernel, in_specs=[far_spec if i in far else spec for i in...  14.3 us
    ppermute x6, starting transfers between devices, exchange(): return lax.ppermute(value, ('cols', 'rows'), pairs)  12.6 us
    ppermute x6, waiting for transfers between devices, exchange(): return lax.ppermute(value, ('cols', 'rows'), pairs)  7.1 us
    ppermute x1, starting transfers between devices, on_device(): normed_other = lax.ppermute(normed, 'rows', swap_pairs(n_rows, False))  2.65 us
    ppermute x1, starting transfers between devices, on_device(): col_a = lax.ppermute(col_a, 'cols', swap_pairs(n_cols, False))  2.58 us
  transfers between devices with their start and end apart: 11, of which 6 were waited for; matrix products, arithmetic and copies ran while one was open for 1% of the time, Pallas kernels for 19%

profile of v6, /device:TPU:0, one launch (start us, length us, event | category | flops | bytes accessed | tf_op | source)
XLA Modules:
  0.0 41.9 jit_solution(12996615918973406151)
XLA Ops:
  0.0 1.0 %row_edges.1 = (bf16[3,24,512]{2,1,0:T(8,128)(2,1)S(1)}, bf16[3,24,512]{2,1,0:T(8,128)(2,1)S(1)}, bf16[6,6,3,64]{3,2,1,0:T(4,128)(2,1)S(1)}) custom-call(bf16[3,256,512]{2,1,0:T(8,128)(2,1)} %slide.3, bf16[6,6,3,64]{3,2,1,0:T(4,128)(2,1)} %kernel_far.1), custom_call_target="tpu_custom_call" | custom-call | tf_op jit(solution)/shard_map/row_edges/pallas_call | solution.py:428
  1.1 0.5 %collective-permute-start = (bf16[3,24,512]{2,1,0:T(8,128)(2,1)S(1)}, bf16[3,24,512]{2,1,0:T(8,128)(2,1)S(1)}, u32[]{:S(2)}, u32[]{:S(2)}) collective-permute-start(bf16[3,24,512]{2,1,0:T(8,128)(2,1)S(1)} %get-tuple-element.30), channel_id=1, source_target_pairs={{0,1},{1,0},{2,3},{3,2},{4,5},{5,4},{6,7},{7,6},{8,9},{9,8},{10,11... | collective-permute-start | bytes 221192 | tf_op jit(solution)/shard_map/ppermute | solution.py:522
  1.6 0.7 %collective-permute-start.1 = (bf16[3,24,512]{2,1,0:T(8,128)(2,1)S(1)}, bf16[3,24,512]{2,1,0:T(8,128)(2,1)S(1)}, u32[]{:S(2)}, u32[]{:S(2)}) collective-permute-start(bf16[3,24,512]{2,1,0:T(8,128)(2,1)S(1)} %get-tuple-element.31), channel_id=1, source_target_pairs={{1,2},{2,1},{5,6},{6,5},{9,10},{10,9},{13,14},{14,13},{17,18},{18,... | collective-permute-start | bytes 221192 | tf_op jit(solution)/shard_map/ppermute | solution.py:523
  2.2 0.8 %band.1.toep = bf16[1152,896]{1,0:T(8,128)(2,1)S(1)} custom-call(bf16[6,6,3,64]{3,2,1,0:T(4,128)(2,1)S(1)} %get-tuple-element.34.kernel_ref), custom_call_target="tpu_custom_call" | custom-call | bytes 1048576 | tf_op jit(solution)/shard_map/band/pallas_call | solution.py:428
  3.1 2.2 %windows.1 = (f32[2,5,3,328,128]{4,3,2,1,0:T(8,128)S(1)}, f32[5,14,104,128]{3,2,1,0:T(8,128)S(1)}, bf16[1024,1024]{1,0:T(8,128)(2,1)S(1)}) custom-call(bf16[3,256,512]{2,1,0:T(8,128)(2,1)S(1)} %copy-done, bf16[1152,896]{1,0:T(8,128)(2,1)S(1)} %band.1.toep, bf16[1024,1024]{1,0:T(8,128)(2,1)} %far.2), custom_call_target="tpu_custom_call" | custom-call | flops 990904320 | bytes 4194304 | tf_op jit(solution)/shard_map/windows/pallas_call | solution.py:428
  5.5 2.6 %collective-permute-start.2 = (bf16[144,128]{1,0:T(8,128)(2,1)S(1)}, bf16[144,128]{1,0:T(8,128)(2,1)S(1)}, u32[]{:S(2)}, u32[]{:S(2)}) collective-permute-start(bf16[144,128]{1,0:T(8,128)(2,1)S(1)} %get-tuple-element.32), channel_id=1, source_target_pairs={{0,4},{4,0},{8,12},{12,8},{16,20},{20,16},{24,28},{28,24},{1,5},{5... | collective-permute-start | bytes 110600 | tf_op jit(solution)/shard_map/ppermute | solution.py:528
  8.1 0.7 %collective-permute-start.3 = (bf16[144,128]{1,0:T(8,128)(2,1)S(1)}, bf16[144,128]{1,0:T(8,128)(2,1)S(1)}, u32[]{:S(2)}, u32[]{:S(2)}) collective-permute-start(bf16[144,128]{1,0:T(8,128)(2,1)S(1)} %get-tuple-element.33), channel_id=1, source_target_pairs={{4,8},{8,4},{12,16},{16,12},{20,24},{24,20},{5,9},{9,5},{13,17},{1... | collective-permute-start | bytes 110600 | tf_op jit(solution)/shard_map/ppermute | solution.py:529
  8.8 1.2 %inner.1 = (f32[2,5,3,328,128]{4,3,2,1,0:T(8,128)S(1)}, f32[5,14,104,128]{3,2,1,0:T(8,128)S(1)}) custom-call(bf16[3,24,512]{2,1,0:T(8,128)(2,1)S(1)} %collective-permute-done.ra_ref, bf16[3,24,512]{2,1,0:T(8,128)(2,1)S(1)} %collective-permute-done.1.rb_ref, bf16[1152,896]{1,0:T(8,128)(2,1)S(1)} %band.1.toep, ...), custom_call_target="tpu_custom_call", output_to_operand_aliasing={{0}: (3, {}), {1}: (4, {})} | custom-call | flops 528482304 | bytes 16777216 | tf_op jit(solution)/shard_map/inner/pallas_call | solution.py:428
  10.0 0.2 copy-done.1
  10.2 1.4 %middle.1.smap_in = f32[2,34,24,128]{3,2,1,0:T(8,128)S(1)} custom-call(f32[5,14,104,128]{3,2,1,0:T(8,128)S(1)} %get-tuple-element.38.fmap.fmap_in, bf16[2304,256]{1,0:T(8,128)(2,1)S(1)} %bitcast.13), custom_call_target="tpu_custom_call" | custom-call | flops 962592768 | bytes 4194304 | tf_op jit(solution)/shard_map/middle/pallas_call | solution.py:428
  11.6 2.3 %stem.1 = (f32[2,5,3,328,128]{4,3,2,1,0:T(8,128)S(1)}, f32[5,14,104,128]{3,2,1,0:T(8,128)S(1)}, f32[2,34,24,128]{3,2,1,0:T(8,128)S(1)}, bf16[128,1024]{1,0:T(8,128)(2,1)S(1)}, bf16[1024,1024]{1,0:T(8,128)(2,1)S(1)}) custom-call(bf16[144,128]{1,0:T(8,128)(2,1)S(1)} %collective-permute-done.2.ca_ref, ...), custom_call_target="tpu_custom_call", output_to_operand_aliasing={{0}: (2, {}), {1}: (3, {}), {2}: (4, {})} | custom-call | flops 2147483648 | tf_op jit(solution)/shard_map/stem/pallas_call | solution.py:428
  13.9 2.7 %collective-permute-start.4 = (bf16[128,1024]{1,0:T(8,128)(2,1)S(1)}, bf16[128,1024]{1,0:T(8,128)(2,1)S(1)}, u32[]{:S(2)}, u32[]{:S(2)}) collective-permute-start(bf16[128,1024]{1,0:T(8,128)(2,1)S(1)} %get-tuple-element.39.tokens), channel_id=1, source_target_pairs={{0,1},{1,0},{2,3},{3,2},{4,5},{5,4},{6,7},{7,6},{8,9},{9,8},{10,11... | collective-permute-start | bytes 786440 | tf_op jit(solution)/shard_map/ppermute | solution.py:599
  16.9 0.7 %project.2.mine = bf16[128,2048]{1,0:T(8,128)(2,1)S(1)} custom-call(bf16[128,1024]{1,0:T(8,128)(2,1)S(1)} %get-tuple-element.39.tokens, bf16[1024,1024]{1,0:T(8,128)(2,1)S(1)} %get-tuple-element.40.wk, bf16[1024,1024]{1,0:T(8,128)(2,1)S(1)} %get-tuple-element.41.wv), custom_call_target="tpu_custom_call" | custom-call | flops 536870912 | tf_op jit(solution)/shard_map/project/pallas_call | solution.py:428
  17.8 0.7 %project.3.theirs = bf16[128,2048]{1,0:T(8,128)(2,1)S(1)} custom-call(bf16[128,1024]{1,0:T(8,128)(2,1)S(1)} %collective-permute-done.4.tokens, bf16[1024,1024]{1,0:T(8,128)(2,1)S(1)} %get-tuple-element.40.wk, bf16[1024,1024]{1,0:T(8,128)(2,1)S(1)} %get-tuple-element.41.wv), custom_call_target="tpu_custom_call" | custom-call | flops 536870912 | tf_op jit(solution)/shard_map/project/pallas_call | solution.py:428
  18.5 1.0 %attend.2 = (bf16[64,1152]{1,0:T(8,128)(2,1)S(1)}, bf16[64,1152]{1,0:T(8,128)(2,1)S(1)}) custom-call(bf16[512,1024]{1,0:T(8,128)(2,1)S(1)} %pad_maximum_fusion.q, bf16[128,2048]{1,0:T(8,128)(2,1)S(1)} %project.2.mine, bf16[128,2048]{1,0:T(8,128)(2,1)S(1)} %project.3.theirs), custom_call_target="tpu_custom_call" | custom-call | flops 1073741824 | tf_op jit(solution)/shard_map/attend/pallas_call | solution.py:428
  19.5 1.3 %collective-permute-start.7 = (bf16[64,1152]{1,0:T(8,128)(2,1)S(1)}, bf16[64,1152]{1,0:T(8,128)(2,1)S(1)}, u32[]{:S(2)}, u32[]{:S(2)}) collective-permute-start(bf16[64,1152]{1,0:T(8,128)(2,1)S(1)} %get-tuple-element.50), channel_id=1, source_target_pairs={{0,2},{1,5},{2,0},{3,7},{4,6},{5,1},{6,4},{7,3},{8,10},{9,13},{10,... | collective-permute-start | bytes 442376 | tf_op jit(solution)/shard_map/ppermute | solution.py:482
  20.7 0.8 %collective-permute-start.5 = (bf16[64,1152]{1,0:T(8,128)(2,1)S(1)}, bf16[64,1152]{1,0:T(8,128)(2,1)S(1)}, u32[]{:S(2)}, u32[]{:S(2)}) collective-permute-start(bf16[64,1152]{1,0:T(8,128)(2,1)S(1)} %get-tuple-element.46), channel_id=1, source_target_pairs={{0,2},{1,5},{2,0},{3,7},{4,6},{5,1},{6,4},{7,3},{8,10},{9,13},{10,... | collective-permute-start | bytes 442376 | tf_op jit(solution)/shard_map/ppermute | solution.py:482
  21.5 0.9 %attend.3 = (f32[64,1152]{1,0:T(8,128)S(1)}, f32[64,1152]{1,0:T(8,128)S(1)}) custom-call(bf16[512,1024]{1,0:T(8,128)(2,1)S(1)} %pad_maximum_fusion.q, bf16[128,2048]{1,0:T(8,128)(2,1)S(1)} %project.2.mine, bf16[128,2048]{1,0:T(8,128)(2,1)S(1)} %project.3.theirs), custom_call_target="tpu_custom_call" | custom-call | flops 1073741824 | tf_op jit(solution)/shard_map/attend/pallas_call | solution.py:428
  22.4 2.2 %collective-permute-done.7.recv_ref = bf16[64,1152]{1,0:T(8,128)(2,1)S(1)} collective-permute-done((bf16[64,1152]{1,0:T(8,128)(2,1)S(1)}, bf16[64,1152]{1,0:T(8,128)(2,1)S(1)}, u32[]{:S(2)}, u32[]{:S(2)}) %collective-permute-start.7) | collective-permute-done | bytes 147488 | tf_op jit(solution)/shard_map/ppermute | solution.py:482
  24.7 0.2 merge.8
  24.9 4.1 %collective-permute-start.8 = (bf16[32,1152]{1,0:T(8,128)(2,1)S(1)}, bf16[32,1152]{1,0:T(8,128)(2,1)S(1)}, u32[]{:S(2)}, u32[]{:S(2)}) collective-permute-start(bf16[32,1152]{1,0:T(8,128)(2,1)S(1)} %get-tuple-element.52), channel_id=1, source_target_pairs={{0,4},{1,3},{2,6},{3,1},{4,0},{5,7},{6,2},{7,5},{8,12},{9,11},{10,... | collective-permute-start | bytes 221192 | tf_op jit(solution)/shard_map/ppermute | solution.py:482
  29.0 0.2 merge.6
  29.2 1.3 %collective-permute-start.6 = (bf16[32,1152]{1,0:T(8,128)(2,1)S(1)}, bf16[32,1152]{1,0:T(8,128)(2,1)S(1)}, u32[]{:S(2)}, u32[]{:S(2)}) collective-permute-start(bf16[32,1152]{1,0:T(8,128)(2,1)S(1)} %get-tuple-element.48), channel_id=1, source_target_pairs={{0,4},{1,3},{2,6},{3,1},{4,0},{5,7},{6,2},{7,5},{8,12},{9,11},{10,... | collective-permute-start | bytes 221192 | tf_op jit(solution)/shard_map/ppermute | solution.py:482
  30.6 0.8 %collective-permute-done.8.recv_ref = bf16[32,1152]{1,0:T(8,128)(2,1)S(1)} collective-permute-done((bf16[32,1152]{1,0:T(8,128)(2,1)S(1)}, bf16[32,1152]{1,0:T(8,128)(2,1)S(1)}, u32[]{:S(2)}, u32[]{:S(2)}) %collective-permute-start.8) | collective-permute-done | bytes 73760 | tf_op jit(solution)/shard_map/ppermute | solution.py:482
  31.3 0.2 merge.9
  31.5 2.0 %collective-permute-start.9 = (bf16[32,1152]{1,0:T(8,128)(2,1)S(1)}, bf16[32,1152]{1,0:T(8,128)(2,1)S(1)}, u32[]{:S(2)}, u32[]{:S(2)}) collective-permute-start(bf16[32,1152]{1,0:T(8,128)(2,1)S(1)} %merge.9), channel_id=1, source_target_pairs={{0,8},{1,9},{2,10},{3,11},{4,12},{5,13},{6,14},{7,15},{8,0},{9,1},... | collective-permute-start | bytes 221192 | tf_op jit(solution)/shard_map/ppermute | solution.py:482
  33.7 0.2 merge.7.keep_ref
  33.9 2.1 %collective-permute-done.9.recv_ref = bf16[32,1152]{1,0:T(8,128)(2,1)S(1)} collective-permute-done((bf16[32,1152]{1,0:T(8,128)(2,1)S(1)}, bf16[32,1152]{1,0:T(8,128)(2,1)S(1)}, u32[]{:S(2)}, u32[]{:S(2)}) %collective-permute-start.9) | collective-permute-done | bytes 73760 | tf_op jit(solution)/shard_map/ppermute | solution.py:482
  35.9 0.2 merge.10
  36.1 3.1 %collective-permute-start.10 = (bf16[16,1152]{1,0:T(8,128)(2,1)S(1)}, bf16[16,1152]{1,0:T(8,128)(2,1)S(1)}, u32[]{:S(2)}, u32[]{:S(2)}) collective-permute-start(bf16[16,1152]{1,0:T(8,128)(2,1)S(1)} %get-tuple-element.54), channel_id=1, source_target_pairs={{0,16},{1,17},{2,18},{3,19},{4,20},{5,21},{6,22},{7,23},{8,24},{9,... | collective-permute-start | bytes 110600 | tf_op jit(solution)/shard_map/ppermute | solution.py:482
  39.2 1.9 %collective-permute-done.10.recv_ref = bf16[16,1152]{1,0:T(8,128)(2,1)S(1)} collective-permute-done((bf16[16,1152]{1,0:T(8,128)(2,1)S(1)}, bf16[16,1152]{1,0:T(8,128)(2,1)S(1)}, u32[]{:S(2)}, u32[]{:S(2)}) %collective-permute-start.10) | collective-permute-done | bytes 36896 | tf_op jit(solution)/shard_map/ppermute | solution.py:482
  41.1 0.8 %merge.11 = bf16[16,1024]{1,0:T(8,128)(2,1)} custom-call(f32[16,1152]{1,0:T(8,128)S(1)} %get-tuple-element.53.keep_ref, bf16[16,1152]{1,0:T(8,128)(2,1)S(1)} %collective-permute-done.10.recv_ref), custom_call_target="tpu_custom_call" | custom-call | tf_op jit(solution)/shard_map/merge/pallas_call | solution.py:428
  (22 shorter events, 0.7 us)
Async XLA Ops:
  0.0 3.1 %copy-start = (bf16[3,256,512]{2,1,0:T(8,128)(2,1)S(1)}, bf16[3,256,512]{2,1,0:T(8,128)(2,1)}, u32[]{:S(2)}) copy-start(bf16[3,256,512]{2,1,0:T(8,128)(2,1)} %slide.3) | copy-start | bytes 2359300
  1.1 4.2 %collective-permute-start = (bf16[3,24,512]{2,1,0:T(8,128)(2,1)S(1)}, bf16[3,24,512]{2,1,0:T(8,128)(2,1)S(1)}, u32[]{:S(2)}, u32[]{:S(2)}) collective-permute-start(bf16[3,24,512]{2,1,0:T(8,128)(2,1)S(1)} %get-tuple-element.30), channel_id=1, source_target_pairs={{0,1},{1,0},{2,3},{3,2},{4,5},{5,4},{6,7},{7,6},{8,9},{9,8},{10,11... | collective-permute-start | bytes 221192 | tf_op jit(solution)/shard_map/ppermute | solution.py:522
  1.6 3.7 %collective-permute-start.1 = (bf16[3,24,512]{2,1,0:T(8,128)(2,1)S(1)}, bf16[3,24,512]{2,1,0:T(8,128)(2,1)S(1)}, u32[]{:S(2)}, u32[]{:S(2)}) collective-permute-start(bf16[3,24,512]{2,1,0:T(8,128)(2,1)S(1)} %get-tuple-element.31), channel_id=1, source_target_pairs={{1,2},{2,1},{5,6},{6,5},{9,10},{10,9},{13,14},{14,13},{17,18},{18,... | collective-permute-start | bytes 221192 | tf_op jit(solution)/shard_map/ppermute | solution.py:523
  5.5 6.1 %collective-permute-start.2 = (bf16[144,128]{1,0:T(8,128)(2,1)S(1)}, bf16[144,128]{1,0:T(8,128)(2,1)S(1)}, u32[]{:S(2)}, u32[]{:S(2)}) collective-permute-start(bf16[144,128]{1,0:T(8,128)(2,1)S(1)} %get-tuple-element.32), channel_id=1, source_target_pairs={{0,4},{4,0},{8,12},{12,8},{16,20},{20,16},{24,28},{28,24},{1,5},{5... | collective-permute-start | bytes 110600 | tf_op jit(solution)/shard_map/ppermute | solution.py:528
  8.1 3.5 %collective-permute-start.3 = (bf16[144,128]{1,0:T(8,128)(2,1)S(1)}, bf16[144,128]{1,0:T(8,128)(2,1)S(1)}, u32[]{:S(2)}, u32[]{:S(2)}) collective-permute-start(bf16[144,128]{1,0:T(8,128)(2,1)S(1)} %get-tuple-element.33), channel_id=1, source_target_pairs={{4,8},{8,4},{12,16},{16,12},{20,24},{24,20},{5,9},{9,5},{13,17},{1... | collective-permute-start | bytes 110600 | tf_op jit(solution)/shard_map/ppermute | solution.py:529
  8.7 2.9 %slice-start = ((s8[4718592]{0:T(1024)(128)(4,1)}), s8[4194304]{0:T(1024)(128)(4,1)S(1)}, s32[]{:S(2)}) async-start(s8[4718592]{0:T(1024)(128)(4,1)} %bitcast.15), calls=%async_computation | async-start | bytes 8388608
  8.8 1.4 %copy-start.1 = (bf16[6,6,64,256]{3,2,1,0:T(8,128)(2,1)S(1)}, bf16[6,6,64,256]{3,2,1,0:T(8,128)(2,1)}, u32[]{:S(2)}) copy-start(bf16[6,6,64,256]{3,2,1,0:T(8,128)(2,1)} %param.9) | copy-start | bytes 3538948
  8.8 2.8 %slice-start.1 = ((s8[4718592]{0:T(1024)(128)(4,1)}), s8[524288]{0:T(1024)(128)(4,1)S(1)}, s32[]{:S(2)}) async-start(s8[4718592]{0:T(1024)(128)(4,1)} %bitcast.15), calls=%async_computation.1 | async-start | bytes 1048576
  11.6 5.0 %copy-start.2 = (bf16[512,1024]{1,0:T(8,128)(2,1)S(1)}, bf16[512,1024]{1,0:T(8,128)(2,1)}, u32[]{:S(2)}) copy-start(bf16[512,1024]{1,0:T(8,128)(2,1)} %param.13) | copy-start | bytes 3145732
  13.9 3.8 %collective-permute-start.4 = (bf16[128,1024]{1,0:T(8,128)(2,1)S(1)}, bf16[128,1024]{1,0:T(8,128)(2,1)S(1)}, u32[]{:S(2)}, u32[]{:S(2)}) collective-permute-start(bf16[128,1024]{1,0:T(8,128)(2,1)S(1)} %get-tuple-element.39.tokens), channel_id=1, source_target_pairs={{0,1},{1,0},{2,3},{3,2},{4,5},{5,4},{6,7},{7,6},{8,9},{9,8},{10,11... | collective-permute-start | bytes 786440 | tf_op jit(solution)/shard_map/ppermute | solution.py:599
  19.5 5.2 %collective-permute-start.7 = (bf16[64,1152]{1,0:T(8,128)(2,1)S(1)}, bf16[64,1152]{1,0:T(8,128)(2,1)S(1)}, u32[]{:S(2)}, u32[]{:S(2)}) collective-permute-start(bf16[64,1152]{1,0:T(8,128)(2,1)S(1)} %get-tuple-element.50), channel_id=1, source_target_pairs={{0,2},{1,5},{2,0},{3,7},{4,6},{5,1},{6,4},{7,3},{8,10},{9,13},{10,... | collective-permute-start | bytes 442376 | tf_op jit(solution)/shard_map/ppermute | solution.py:482
  20.7 8.3 %collective-permute-start.5 = (bf16[64,1152]{1,0:T(8,128)(2,1)S(1)}, bf16[64,1152]{1,0:T(8,128)(2,1)S(1)}, u32[]{:S(2)}, u32[]{:S(2)}) collective-permute-start(bf16[64,1152]{1,0:T(8,128)(2,1)S(1)} %get-tuple-element.46), channel_id=1, source_target_pairs={{0,2},{1,5},{2,0},{3,7},{4,6},{5,1},{6,4},{7,3},{8,10},{9,13},{10,... | collective-permute-start | bytes 442376 | tf_op jit(solution)/shard_map/ppermute | solution.py:482
  24.9 6.4 %collective-permute-start.8 = (bf16[32,1152]{1,0:T(8,128)(2,1)S(1)}, bf16[32,1152]{1,0:T(8,128)(2,1)S(1)}, u32[]{:S(2)}, u32[]{:S(2)}) collective-permute-start(bf16[32,1152]{1,0:T(8,128)(2,1)S(1)} %get-tuple-element.52), channel_id=1, source_target_pairs={{0,4},{1,3},{2,6},{3,1},{4,0},{5,7},{6,2},{7,5},{8,12},{9,11},{10,... | collective-permute-start | bytes 221192 | tf_op jit(solution)/shard_map/ppermute | solution.py:482
  29.2 4.4 %collective-permute-start.6 = (bf16[32,1152]{1,0:T(8,128)(2,1)S(1)}, bf16[32,1152]{1,0:T(8,128)(2,1)S(1)}, u32[]{:S(2)}, u32[]{:S(2)}) collective-permute-start(bf16[32,1152]{1,0:T(8,128)(2,1)S(1)} %get-tuple-element.48), channel_id=1, source_target_pairs={{0,4},{1,3},{2,6},{3,1},{4,0},{5,7},{6,2},{7,5},{8,12},{9,11},{10,... | collective-permute-start | bytes 221192 | tf_op jit(solution)/shard_map/ppermute | solution.py:482
  31.5 4.4 %collective-permute-start.9 = (bf16[32,1152]{1,0:T(8,128)(2,1)S(1)}, bf16[32,1152]{1,0:T(8,128)(2,1)S(1)}, u32[]{:S(2)}, u32[]{:S(2)}) collective-permute-start(bf16[32,1152]{1,0:T(8,128)(2,1)S(1)} %merge.9), channel_id=1, source_target_pairs={{0,8},{1,9},{2,10},{3,11},{4,12},{5,13},{6,14},{7,15},{8,0},{9,1},... | collective-permute-start | bytes 221192 | tf_op jit(solution)/shard_map/ppermute | solution.py:482
  36.1 5.0 %collective-permute-start.10 = (bf16[16,1152]{1,0:T(8,128)(2,1)S(1)}, bf16[16,1152]{1,0:T(8,128)(2,1)S(1)}, u32[]{:S(2)}, u32[]{:S(2)}) collective-permute-start(bf16[16,1152]{1,0:T(8,128)(2,1)S(1)} %get-tuple-element.54), channel_id=1, source_target_pairs={{0,16},{1,17},{2,18},{3,19},{4,20},{5,21},{6,22},{7,23},{8,24},{9,... | collective-permute-start | bytes 110600 | tf_op jit(solution)/shard_map/ppermute | solution.py:482

commit v7 on v6

--- a/solution.py
+++ b/solution.py
@@ -149,9 +149,10 @@
     return jnp.where(low, first, second)
 
 
-def window_kernel(slide, toep, far, xb, fmap, near, lhs1, sem):
-    copy = pltpu.make_async_copy(far, near, sem)
-    copy.start()
+def window_kernel(slide, toep, w2_far, wk_far, xb, fmap, w2, wk, lhs1, sems):
+    copies = [pltpu.make_async_copy(w2_far, w2, sems.at[0]), pltpu.make_async_copy(wk_far, wk, sems.at[1])]
+    for copy in copies:
+        copy.start()
     for c in range(3):
         for b, part in enumerate(cut(slide[c])):
             for order in range(2):
@@ -172,7 +173,8 @@
                 for u in range(size // 128):
                     tile = (HALF_LANES * half + start) // 128 + u
                     fmap[b, tile, EDGE : EDGE + MID, :] = acc[row0 : row0 + MID, 128 * u : 128 * u + 128]
-    copy.wait()
+    for copy in copies:
+        copy.wait()
 
 
 def inner_kernel(ra_ref, rb_ref, toep, xb_in, fmap_in, xb, fmap, lhs1, *, row_last):
@@ -237,7 +239,7 @@
                 lhs2[48 * i : 48 * i + 48, 384 * kh + 128 * u : 384 * kh + 128 * u + 128] = jnp.concatenate(
                     [fmap[block, tile, rows, :] for block, tile in tiles], axis=0
                 ).astype(jnp.bfloat16)
-    step = 5
+    step = 15
     for start in range(0, len(cols), step):
         some = cols[start : start + step]
         acc = gelu(
@@ -539,13 +541,13 @@
         )
         xb_shape = VMEM((2, BLOCKS, 3, 328, 128), f32)
         fmap_shape = VMEM((BLOCKS, BLOCK_LANES // 128, 104, 128), f32)
-        xb, fmap, key_near = call(
+        xb, fmap, w2, key_near = call(
             window_kernel,
             "windows",
-            (slide_pixels, toep, key_weight),
-            (xb_shape, fmap_shape, VMEM(key_weight.shape, bf16)),
-            scratch=[pltpu.VMEM((2 * MID_ALL, DEPTH1), bf16), pltpu.SemaphoreType.DMA],
-            far=(2,),
+            (slide_pixels, toep, stem_second.reshape(2304, 256), key_weight),
+            (xb_shape, fmap_shape, VMEM((2304, 256), bf16), VMEM(key_weight.shape, bf16)),
+            scratch=[pltpu.VMEM((2 * MID_ALL, DEPTH1), bf16), pltpu.SemaphoreType.DMA((2,))],
+            far=(2, 3),
             flops=2 * MID_ALL * DEPTH1 * BLOCK_LANES,
             moved=4 << 20,
             limit=8 << 20,
@@ -562,7 +564,6 @@
             limit=8 << 20,
         )
         smap_shape = VMEM((2, COLS2, ROWS2, 128), f32)
-        w2 = stem_second.reshape(2304, 256)
         (smap,) = call(
             middle_kernel,
             "middle",

time: 42.1 us -> 42.1 us (level)
  starting transfers between devices: 19.6 us -> 20.1 us
    ppermute x6, starting transfers between devices: 12.6 us -> 13.1 us  [exchange(): return lax.ppermute(value, ('cols', 'rows'), pairs)]
  transfers between devices with their start and end apart: 11 -> 11, of which waited for: 6 -> 5; matrix products, arithmetic and copies ran while one was open for 1% -> 1% of each run, Pallas kernels for 19% -> 19%
where the time goes in v7:
time: 42.1 us; the launch traced here: 41.9 us
  starting transfers between devices  20.1 us (48%)
  Pallas kernels  14.1 us (33%)
  waiting for transfers between devices  7.24 us (17%)
    pallas_call x17, Pallas kernels, call(): pl.pallas_call(kernel, in_specs=[far_spec if i in far else spec for i in...  14.1 us
    ppermute x6, starting transfers between devices, exchange(): return lax.ppermute(value, ('cols', 'rows'), pairs)  13.1 us
    ppermute x6, waiting for transfers between devices, exchange(): return lax.ppermute(value, ('cols', 'rows'), pairs)  7.06 us
    ppermute x1, starting transfers between devices, on_device(): normed_other = lax.ppermute(normed, 'rows', swap_pairs(n_rows, False))  2.62 us
    ppermute x1, starting transfers between devices, on_device(): col_a = lax.ppermute(col_a, 'cols', swap_pairs(n_cols, False))  2.58 us
  transfers between devices with their start and end apart: 11, of which 5 were waited for; matrix products, arithmetic and copies ran while one was open for 1% of the time, Pallas kernels for 19%

profile of v7, /device:TPU:0, one launch (start us, length us, event | category | flops | bytes accessed | tf_op | source)
XLA Modules:
  0.0 41.9 jit_solution(9427207508353638263)
XLA Ops:
  0.0 1.0 %row_edges.1 = (bf16[3,24,512]{2,1,0:T(8,128)(2,1)S(1)}, bf16[3,24,512]{2,1,0:T(8,128)(2,1)S(1)}, bf16[6,6,3,64]{3,2,1,0:T(4,128)(2,1)S(1)}) custom-call(bf16[3,256,512]{2,1,0:T(8,128)(2,1)} %slide.3, bf16[6,6,3,64]{3,2,1,0:T(4,128)(2,1)} %kernel_far.1), custom_call_target="tpu_custom_call" | custom-call | tf_op jit(solution)/shard_map/row_edges/pallas_call | solution.py:430
  1.1 0.5 %collective-permute-start = (bf16[3,24,512]{2,1,0:T(8,128)(2,1)S(1)}, bf16[3,24,512]{2,1,0:T(8,128)(2,1)S(1)}, u32[]{:S(2)}, u32[]{:S(2)}) collective-permute-start(bf16[3,24,512]{2,1,0:T(8,128)(2,1)S(1)} %get-tuple-element.31), channel_id=1, source_target_pairs={{0,1},{1,0},{2,3},{3,2},{4,5},{5,4},{6,7},{7,6},{8,9},{9,8},{10,11... | collective-permute-start | bytes 221192 | tf_op jit(solution)/shard_map/ppermute | solution.py:524
  1.6 0.7 %collective-permute-start.1 = (bf16[3,24,512]{2,1,0:T(8,128)(2,1)S(1)}, bf16[3,24,512]{2,1,0:T(8,128)(2,1)S(1)}, u32[]{:S(2)}, u32[]{:S(2)}) collective-permute-start(bf16[3,24,512]{2,1,0:T(8,128)(2,1)S(1)} %get-tuple-element.32), channel_id=1, source_target_pairs={{1,2},{2,1},{5,6},{6,5},{9,10},{10,9},{13,14},{14,13},{17,18},{18,... | collective-permute-start | bytes 221192 | tf_op jit(solution)/shard_map/ppermute | solution.py:525
  2.2 0.8 %band.1.toep = bf16[1152,896]{1,0:T(8,128)(2,1)S(1)} custom-call(bf16[6,6,3,64]{3,2,1,0:T(4,128)(2,1)S(1)} %get-tuple-element.35.kernel_ref), custom_call_target="tpu_custom_call" | custom-call | bytes 1048576 | tf_op jit(solution)/shard_map/band/pallas_call | solution.py:430
  3.1 2.2 %windows.1 = (f32[2,5,3,328,128]{4,3,2,1,0:T(8,128)S(1)}, f32[5,14,104,128]{3,2,1,0:T(8,128)S(1)}, bf16[2304,256]{1,0:T(8,128)(2,1)S(1)}, bf16[1024,1024]{1,0:T(8,128)(2,1)S(1)}) custom-call(bf16[3,256,512]{2,1,0:T(8,128)(2,1)S(1)} %copy-done, bf16[1152,896]{1,0:T(8,128)(2,1)S(1)} %band.1.toep, bf16[2304,256]{1,0:T(8,128)(2,1)} %bitcast.18, ...), custom_call_target="tpu_custom_call" | custom-call | flops 990904320 | bytes 4194304 | tf_op jit(solution)/shard_map/windows/pallas_call | solution.py:430
  5.3 0.2 col_edges.1
  5.5 2.6 %collective-permute-start.2 = (bf16[144,128]{1,0:T(8,128)(2,1)S(1)}, bf16[144,128]{1,0:T(8,128)(2,1)S(1)}, u32[]{:S(2)}, u32[]{:S(2)}) collective-permute-start(bf16[144,128]{1,0:T(8,128)(2,1)S(1)} %get-tuple-element.33), channel_id=1, source_target_pairs={{0,4},{4,0},{8,12},{12,8},{16,20},{20,16},{24,28},{28,24},{1,5},{5... | collective-permute-start | bytes 110600 | tf_op jit(solution)/shard_map/ppermute | solution.py:530
  8.1 0.7 %collective-permute-start.3 = (bf16[144,128]{1,0:T(8,128)(2,1)S(1)}, bf16[144,128]{1,0:T(8,128)(2,1)S(1)}, u32[]{:S(2)}, u32[]{:S(2)}) collective-permute-start(bf16[144,128]{1,0:T(8,128)(2,1)S(1)} %get-tuple-element.34), channel_id=1, source_target_pairs={{4,8},{8,4},{12,16},{16,12},{20,24},{24,20},{5,9},{9,5},{13,17},{1... | collective-permute-start | bytes 110600 | tf_op jit(solution)/shard_map/ppermute | solution.py:531
  8.8 1.2 %inner.1 = (f32[2,5,3,328,128]{4,3,2,1,0:T(8,128)S(1)}, f32[5,14,104,128]{3,2,1,0:T(8,128)S(1)}) custom-call(bf16[3,24,512]{2,1,0:T(8,128)(2,1)S(1)} %collective-permute-done.ra_ref, bf16[3,24,512]{2,1,0:T(8,128)(2,1)S(1)} %collective-permute-done.1.rb_ref, bf16[1152,896]{1,0:T(8,128)(2,1)S(1)} %band.1.toep, ...), custom_call_target="tpu_custom_call", output_to_operand_aliasing={{0}: (3, {}), {1}: (4, {})} | custom-call | flops 528482304 | bytes 16777216 | tf_op jit(solution)/shard_map/inner/pallas_call | solution.py:430
  10.0 1.1 %middle.1.smap_in = f32[2,34,24,128]{3,2,1,0:T(8,128)S(1)} custom-call(f32[5,14,104,128]{3,2,1,0:T(8,128)S(1)} %get-tuple-element.39.fmap.fmap_in, bf16[2304,256]{1,0:T(8,128)(2,1)S(1)} %get-tuple-element.40.w2), custom_call_target="tpu_custom_call" | custom-call | flops 962592768 | bytes 4194304 | tf_op jit(solution)/shard_map/middle/pallas_call | solution.py:430
  11.2 2.3 %stem.1 = (f32[2,5,3,328,128]{4,3,2,1,0:T(8,128)S(1)}, f32[5,14,104,128]{3,2,1,0:T(8,128)S(1)}, f32[2,34,24,128]{3,2,1,0:T(8,128)S(1)}, bf16[128,1024]{1,0:T(8,128)(2,1)S(1)}, bf16[1024,1024]{1,0:T(8,128)(2,1)S(1)}) custom-call(bf16[144,128]{1,0:T(8,128)(2,1)S(1)} %collective-permute-done.2.ca_ref, ...), custom_call_target="tpu_custom_call", output_to_operand_aliasing={{0}: (2, {}), {1}: (3, {}), {2}: (4, {})} | custom-call | flops 2147483648 | tf_op jit(solution)/shard_map/stem/pallas_call | solution.py:430
  13.5 2.6 %collective-permute-start.4 = (bf16[128,1024]{1,0:T(8,128)(2,1)S(1)}, bf16[128,1024]{1,0:T(8,128)(2,1)S(1)}, u32[]{:S(2)}, u32[]{:S(2)}) collective-permute-start(bf16[128,1024]{1,0:T(8,128)(2,1)S(1)} %get-tuple-element.41.tokens), channel_id=1, source_target_pairs={{0,1},{1,0},{2,3},{3,2},{4,5},{5,4},{6,7},{7,6},{8,9},{9,8},{10,11... | collective-permute-start | bytes 786440 | tf_op jit(solution)/shard_map/ppermute | solution.py:600
  16.4 0.7 %project.2.mine = bf16[128,2048]{1,0:T(8,128)(2,1)S(1)} custom-call(bf16[128,1024]{1,0:T(8,128)(2,1)S(1)} %get-tuple-element.41.tokens, bf16[1024,1024]{1,0:T(8,128)(2,1)S(1)} %get-tuple-element.42.wk, bf16[1024,1024]{1,0:T(8,128)(2,1)S(1)} %get-tuple-element.43.wv), custom_call_target="tpu_custom_call" | custom-call | flops 536870912 | tf_op jit(solution)/shard_map/project/pallas_call | solution.py:430
  17.3 0.7 %project.3.theirs = bf16[128,2048]{1,0:T(8,128)(2,1)S(1)} custom-call(bf16[128,1024]{1,0:T(8,128)(2,1)S(1)} %collective-permute-done.4.tokens, bf16[1024,1024]{1,0:T(8,128)(2,1)S(1)} %get-tuple-element.42.wk, bf16[1024,1024]{1,0:T(8,128)(2,1)S(1)} %get-tuple-element.43.wv), custom_call_target="tpu_custom_call" | custom-call | flops 536870912 | tf_op jit(solution)/shard_map/project/pallas_call | solution.py:430
  18.0 1.0 %attend.2 = (bf16[64,1152]{1,0:T(8,128)(2,1)S(1)}, bf16[64,1152]{1,0:T(8,128)(2,1)S(1)}) custom-call(bf16[512,1024]{1,0:T(8,128)(2,1)S(1)} %pad_maximum_fusion.q, bf16[128,2048]{1,0:T(8,128)(2,1)S(1)} %project.2.mine, bf16[128,2048]{1,0:T(8,128)(2,1)S(1)} %project.3.theirs), custom_call_target="tpu_custom_call" | custom-call | flops 1073741824 | tf_op jit(solution)/shard_map/attend/pallas_call | solution.py:430
  19.0 1.3 %collective-permute-start.7 = (bf16[64,1152]{1,0:T(8,128)(2,1)S(1)}, bf16[64,1152]{1,0:T(8,128)(2,1)S(1)}, u32[]{:S(2)}, u32[]{:S(2)}) collective-permute-start(bf16[64,1152]{1,0:T(8,128)(2,1)S(1)} %get-tuple-element.52), channel_id=1, source_target_pairs={{0,2},{1,5},{2,0},{3,7},{4,6},{5,1},{6,4},{7,3},{8,10},{9,13},{10,... | collective-permute-start | bytes 442376 | tf_op jit(solution)/shard_map/ppermute | solution.py:484
  20.2 0.8 %collective-permute-start.5 = (bf16[64,1152]{1,0:T(8,128)(2,1)S(1)}, bf16[64,1152]{1,0:T(8,128)(2,1)S(1)}, u32[]{:S(2)}, u32[]{:S(2)}) collective-permute-start(bf16[64,1152]{1,0:T(8,128)(2,1)S(1)} %get-tuple-element.48), channel_id=1, source_target_pairs={{0,2},{1,5},{2,0},{3,7},{4,6},{5,1},{6,4},{7,3},{8,10},{9,13},{10,... | collective-permute-start | bytes 442376 | tf_op jit(solution)/shard_map/ppermute | solution.py:484
  21.0 0.9 %attend.3 = (f32[64,1152]{1,0:T(8,128)S(1)}, f32[64,1152]{1,0:T(8,128)S(1)}) custom-call(bf16[512,1024]{1,0:T(8,128)(2,1)S(1)} %pad_maximum_fusion.q, bf16[128,2048]{1,0:T(8,128)(2,1)S(1)} %project.2.mine, bf16[128,2048]{1,0:T(8,128)(2,1)S(1)} %project.3.theirs), custom_call_target="tpu_custom_call" | custom-call | flops 1073741824 | tf_op jit(solution)/shard_map/attend/pallas_call | solution.py:430
  21.9 2.2 %collective-permute-done.7.recv_ref = bf16[64,1152]{1,0:T(8,128)(2,1)S(1)} collective-permute-done((bf16[64,1152]{1,0:T(8,128)(2,1)S(1)}, bf16[64,1152]{1,0:T(8,128)(2,1)S(1)}, u32[]{:S(2)}, u32[]{:S(2)}) %collective-permute-start.7) | collective-permute-done | bytes 147488 | tf_op jit(solution)/shard_map/ppermute | solution.py:484
  24.2 0.2 merge.8
  24.4 4.1 %collective-permute-start.8 = (bf16[32,1152]{1,0:T(8,128)(2,1)S(1)}, bf16[32,1152]{1,0:T(8,128)(2,1)S(1)}, u32[]{:S(2)}, u32[]{:S(2)}) collective-permute-start(bf16[32,1152]{1,0:T(8,128)(2,1)S(1)} %get-tuple-element.54), channel_id=1, source_target_pairs={{0,4},{1,3},{2,6},{3,1},{4,0},{5,7},{6,2},{7,5},{8,12},{9,11},{10,... | collective-permute-start | bytes 221192 | tf_op jit(solution)/shard_map/ppermute | solution.py:484
  28.5 0.2 merge.6
  28.7 1.3 %collective-permute-start.6 = (bf16[32,1152]{1,0:T(8,128)(2,1)S(1)}, bf16[32,1152]{1,0:T(8,128)(2,1)S(1)}, u32[]{:S(2)}, u32[]{:S(2)}) collective-permute-start(bf16[32,1152]{1,0:T(8,128)(2,1)S(1)} %get-tuple-element.50), channel_id=1, source_target_pairs={{0,4},{1,3},{2,6},{3,1},{4,0},{5,7},{6,2},{7,5},{8,12},{9,11},{10,... | collective-permute-start | bytes 221192 | tf_op jit(solution)/shard_map/ppermute | solution.py:484
  30.1 0.8 %collective-permute-done.8.recv_ref = bf16[32,1152]{1,0:T(8,128)(2,1)S(1)} collective-permute-done((bf16[32,1152]{1,0:T(8,128)(2,1)S(1)}, bf16[32,1152]{1,0:T(8,128)(2,1)S(1)}, u32[]{:S(2)}, u32[]{:S(2)}) %collective-permute-start.8) | collective-permute-done | bytes 73760 | tf_op jit(solution)/shard_map/ppermute | solution.py:484
  30.8 0.2 merge.9
  31.0 2.5 %collective-permute-start.9 = (bf16[32,1152]{1,0:T(8,128)(2,1)S(1)}, bf16[32,1152]{1,0:T(8,128)(2,1)S(1)}, u32[]{:S(2)}, u32[]{:S(2)}) collective-permute-start(bf16[32,1152]{1,0:T(8,128)(2,1)S(1)} %merge.9), channel_id=1, source_target_pairs={{0,8},{1,9},{2,10},{3,11},{4,12},{5,13},{6,14},{7,15},{8,0},{9,1},... | collective-permute-start | bytes 221192 | tf_op jit(solution)/shard_map/ppermute | solution.py:484
  33.6 0.2 merge.7.keep_ref
  33.8 2.1 %collective-permute-done.9.recv_ref = bf16[32,1152]{1,0:T(8,128)(2,1)S(1)} collective-permute-done((bf16[32,1152]{1,0:T(8,128)(2,1)S(1)}, bf16[32,1152]{1,0:T(8,128)(2,1)S(1)}, u32[]{:S(2)}, u32[]{:S(2)}) %collective-permute-start.9) | collective-permute-done | bytes 73760 | tf_op jit(solution)/shard_map/ppermute | solution.py:484
  35.9 0.2 merge.10
  36.1 3.1 %collective-permute-start.10 = (bf16[16,1152]{1,0:T(8,128)(2,1)S(1)}, bf16[16,1152]{1,0:T(8,128)(2,1)S(1)}, u32[]{:S(2)}, u32[]{:S(2)}) collective-permute-start(bf16[16,1152]{1,0:T(8,128)(2,1)S(1)} %get-tuple-element.56), channel_id=1, source_target_pairs={{0,16},{1,17},{2,18},{3,19},{4,20},{5,21},{6,22},{7,23},{8,24},{9,... | collective-permute-start | bytes 110600 | tf_op jit(solution)/shard_map/ppermute | solution.py:484
  39.2 1.9 %collective-permute-done.10.recv_ref = bf16[16,1152]{1,0:T(8,128)(2,1)S(1)} collective-permute-done((bf16[16,1152]{1,0:T(8,128)(2,1)S(1)}, bf16[16,1152]{1,0:T(8,128)(2,1)S(1)}, u32[]{:S(2)}, u32[]{:S(2)}) %collective-permute-start.10) | collective-permute-done | bytes 36896 | tf_op jit(solution)/shard_map/ppermute | solution.py:484
  41.1 0.8 %merge.11 = bf16[16,1024]{1,0:T(8,128)(2,1)} custom-call(f32[16,1152]{1,0:T(8,128)S(1)} %get-tuple-element.55.keep_ref, bf16[16,1152]{1,0:T(8,128)(2,1)S(1)} %collective-permute-done.10.recv_ref), custom_call_target="tpu_custom_call" | custom-call | tf_op jit(solution)/shard_map/merge/pallas_call | solution.py:430
  (20 shorter events, 0.4 us)
Async XLA Ops:
  0.0 3.1 %copy-start = (bf16[3,256,512]{2,1,0:T(8,128)(2,1)S(1)}, bf16[3,256,512]{2,1,0:T(8,128)(2,1)}, u32[]{:S(2)}) copy-start(bf16[3,256,512]{2,1,0:T(8,128)(2,1)} %slide.3) | copy-start | bytes 2359300
  1.1 4.3 %collective-permute-start = (bf16[3,24,512]{2,1,0:T(8,128)(2,1)S(1)}, bf16[3,24,512]{2,1,0:T(8,128)(2,1)S(1)}, u32[]{:S(2)}, u32[]{:S(2)}) collective-permute-start(bf16[3,24,512]{2,1,0:T(8,128)(2,1)S(1)} %get-tuple-element.31), channel_id=1, source_target_pairs={{0,1},{1,0},{2,3},{3,2},{4,5},{5,4},{6,7},{7,6},{8,9},{9,8},{10,11... | collective-permute-start | bytes 221192 | tf_op jit(solution)/shard_map/ppermute | solution.py:524
  1.6 3.8 %collective-permute-start.1 = (bf16[3,24,512]{2,1,0:T(8,128)(2,1)S(1)}, bf16[3,24,512]{2,1,0:T(8,128)(2,1)S(1)}, u32[]{:S(2)}, u32[]{:S(2)}) collective-permute-start(bf16[3,24,512]{2,1,0:T(8,128)(2,1)S(1)} %get-tuple-element.32), channel_id=1, source_target_pairs={{1,2},{2,1},{5,6},{6,5},{9,10},{10,9},{13,14},{14,13},{17,18},{18,... | collective-permute-start | bytes 221192 | tf_op jit(solution)/shard_map/ppermute | solution.py:525
  5.5 5.6 %collective-permute-start.2 = (bf16[144,128]{1,0:T(8,128)(2,1)S(1)}, bf16[144,128]{1,0:T(8,128)(2,1)S(1)}, u32[]{:S(2)}, u32[]{:S(2)}) collective-permute-start(bf16[144,128]{1,0:T(8,128)(2,1)S(1)} %get-tuple-element.33), channel_id=1, source_target_pairs={{0,4},{4,0},{8,12},{12,8},{16,20},{20,16},{24,28},{28,24},{1,5},{5... | collective-permute-start | bytes 110600 | tf_op jit(solution)/shard_map/ppermute | solution.py:530
  8.1 3.0 %collective-permute-start.3 = (bf16[144,128]{1,0:T(8,128)(2,1)S(1)}, bf16[144,128]{1,0:T(8,128)(2,1)S(1)}, u32[]{:S(2)}, u32[]{:S(2)}) collective-permute-start(bf16[144,128]{1,0:T(8,128)(2,1)S(1)} %get-tuple-element.34), channel_id=1, source_target_pairs={{4,8},{8,4},{12,16},{16,12},{20,24},{24,20},{5,9},{9,5},{13,17},{1... | collective-permute-start | bytes 110600 | tf_op jit(solution)/shard_map/ppermute | solution.py:531
  8.8 2.4 %slice-start = ((s8[4718592]{0:T(1024)(128)(4,1)}), s8[4194304]{0:T(1024)(128)(4,1)S(1)}, s32[]{:S(2)}) async-start(s8[4718592]{0:T(1024)(128)(4,1)} %bitcast.13), calls=%async_computation | async-start | bytes 8388608
  8.8 2.4 %slice-start.1 = ((s8[4718592]{0:T(1024)(128)(4,1)}), s8[524288]{0:T(1024)(128)(4,1)S(1)}, s32[]{:S(2)}) async-start(s8[4718592]{0:T(1024)(128)(4,1)} %bitcast.13), calls=%async_computation.1 | async-start | bytes 1048576
  11.2 4.9 %copy-start.1 = (bf16[512,1024]{1,0:T(8,128)(2,1)S(1)}, bf16[512,1024]{1,0:T(8,128)(2,1)}, u32[]{:S(2)}) copy-start(bf16[512,1024]{1,0:T(8,128)(2,1)} %param.13) | copy-start | bytes 3145732
  13.5 3.8 %collective-permute-start.4 = (bf16[128,1024]{1,0:T(8,128)(2,1)S(1)}, bf16[128,1024]{1,0:T(8,128)(2,1)S(1)}, u32[]{:S(2)}, u32[]{:S(2)}) collective-permute-start(bf16[128,1024]{1,0:T(8,128)(2,1)S(1)} %get-tuple-element.41.tokens), channel_id=1, source_target_pairs={{0,1},{1,0},{2,3},{3,2},{4,5},{5,4},{6,7},{7,6},{8,9},{9,8},{10,11... | collective-permute-start | bytes 786440 | tf_op jit(solution)/shard_map/ppermute | solution.py:600
  19.0 5.2 %collective-permute-start.7 = (bf16[64,1152]{1,0:T(8,128)(2,1)S(1)}, bf16[64,1152]{1,0:T(8,128)(2,1)S(1)}, u32[]{:S(2)}, u32[]{:S(2)}) collective-permute-start(bf16[64,1152]{1,0:T(8,128)(2,1)S(1)} %get-tuple-element.52), channel_id=1, source_target_pairs={{0,2},{1,5},{2,0},{3,7},{4,6},{5,1},{6,4},{7,3},{8,10},{9,13},{10,... | collective-permute-start | bytes 442376 | tf_op jit(solution)/shard_map/ppermute | solution.py:484
  20.2 8.3 %collective-permute-start.5 = (bf16[64,1152]{1,0:T(8,128)(2,1)S(1)}, bf16[64,1152]{1,0:T(8,128)(2,1)S(1)}, u32[]{:S(2)}, u32[]{:S(2)}) collective-permute-start(bf16[64,1152]{1,0:T(8,128)(2,1)S(1)} %get-tuple-element.48), channel_id=1, source_target_pairs={{0,2},{1,5},{2,0},{3,7},{4,6},{5,1},{6,4},{7,3},{8,10},{9,13},{10,... | collective-permute-start | bytes 442376 | tf_op jit(solution)/shard_map/ppermute | solution.py:484
  24.4 6.4 %collective-permute-start.8 = (bf16[32,1152]{1,0:T(8,128)(2,1)S(1)}, bf16[32,1152]{1,0:T(8,128)(2,1)S(1)}, u32[]{:S(2)}, u32[]{:S(2)}) collective-permute-start(bf16[32,1152]{1,0:T(8,128)(2,1)S(1)} %get-tuple-element.54), channel_id=1, source_target_pairs={{0,4},{1,3},{2,6},{3,1},{4,0},{5,7},{6,2},{7,5},{8,12},{9,11},{10,... | collective-permute-start | bytes 221192 | tf_op jit(solution)/shard_map/ppermute | solution.py:484
  28.7 4.8 %collective-permute-start.6 = (bf16[32,1152]{1,0:T(8,128)(2,1)S(1)}, bf16[32,1152]{1,0:T(8,128)(2,1)S(1)}, u32[]{:S(2)}, u32[]{:S(2)}) collective-permute-start(bf16[32,1152]{1,0:T(8,128)(2,1)S(1)} %get-tuple-element.50), channel_id=1, source_target_pairs={{0,4},{1,3},{2,6},{3,1},{4,0},{5,7},{6,2},{7,5},{8,12},{9,11},{10,... | collective-permute-start | bytes 221192 | tf_op jit(solution)/shard_map/ppermute | solution.py:484
  31.0 4.9 %collective-permute-start.9 = (bf16[32,1152]{1,0:T(8,128)(2,1)S(1)}, bf16[32,1152]{1,0:T(8,128)(2,1)S(1)}, u32[]{:S(2)}, u32[]{:S(2)}) collective-permute-start(bf16[32,1152]{1,0:T(8,128)(2,1)S(1)} %merge.9), channel_id=1, source_target_pairs={{0,8},{1,9},{2,10},{3,11},{4,12},{5,13},{6,14},{7,15},{8,0},{9,1},... | collective-permute-start | bytes 221192 | tf_op jit(solution)/shard_map/ppermute | solution.py:484
  36.1 5.0 %collective-permute-start.10 = (bf16[16,1152]{1,0:T(8,128)(2,1)S(1)}, bf16[16,1152]{1,0:T(8,128)(2,1)S(1)}, u32[]{:S(2)}, u32[]{:S(2)}) collective-permute-start(bf16[16,1152]{1,0:T(8,128)(2,1)S(1)} %get-tuple-element.56), channel_id=1, source_target_pairs={{0,16},{1,17},{2,18},{3,19},{4,20},{5,21},{6,22},{7,23},{8,24},{9,... | collective-permute-start | bytes 110600 | tf_op jit(solution)/shard_map/ppermute | solution.py:484
